TPU v7x, 256 devices: a whole 4x4x8 slice. The times are simulated.
256 devices in a mesh: seq: 16 (over x_hi, y, core), fsdp: 16 (over x_lo, z).
Axes of the slice: x: 4 (x_hi: 2, x_lo: 2; x = x_hi * 2 + x_lo), y: 4, z: 8, core: 2. Of those that a mesh axis runs over, the one named last changes fastest.
Arguments:
- query: bfloat16 [16, 2560, 4096], P('fsdp', 'seq'), may hold values from -6 to 6
- key: bfloat16 [16, 2560, 4096], P('fsdp', 'seq'), may hold values from -6 to 6
- value: bfloat16 [16, 2560, 4096], P('fsdp', 'seq'), may hold values from -6 to 6
- stream: bfloat16 [16, 2560, 4096], P('fsdp', 'seq'), may hold values from -6 to 6
- targets: int32 [16, 2560], P('fsdp', 'seq'), may hold values from 0 to 3
- short_filter: float32 [7, 3, 2048], replicated, may hold values from -2 to 2
- med_filter: bfloat16 [128, 128], replicated, may hold values from -0.5 to 0.5
- out_weight: bfloat16 [2048, 2048], P('fsdp'), may hold values from -0.125 to 0.125
- head: float32 [4, 2048], replicated, may hold values from -0.09375 to 0.09375
Outputs:
- query_grad: bfloat16 [16, 2560, 4096], P('fsdp', 'seq')
- key_grad: bfloat16 [16, 2560, 4096], P('fsdp', 'seq')
- value_grad: bfloat16 [16, 2560, 4096], P('fsdp', 'seq')
- out_grad: float32 [2048, 2048], P('fsdp')
All inputs are finite; a program needn't handle non-finite values.
Results may differ from a plain program's by a relative error of at most 0.022.
Values may be sent and summed in bfloat16 or wider, within the bound.
No kernel may reach another device: no remote copies, remote signals or barrier semaphores. Data moves between devices by JAX's collectives and lax.ppermute only.
A program may use at most 192 MiB of HBM per device.

v0:
```python
import functools

import jax
import jax.numpy as jnp
import ml_dtypes
import numpy as np
from jax import lax
from jax.experimental import pallas as pl
from jax.experimental.pallas import tpu as pltpu
from jax.sharding import PartitionSpec as P

loss_scale = 64.0
far = 136
near = 8
span = 296
window = 216
step = 80
keep = 88
lead = window - keep
freqs = 112
bins = 2 * freqs
columns = 1024
per_group = 16
parts = 16
lanes = 128
sub = 256
vmem_limit = 24 * 1024 * 1024


def split_np(table):
    upper = table.astype(ml_dtypes.bfloat16)
    lower = (table - upper.astype(np.float64)).astype(ml_dtypes.bfloat16)
    return upper, lower


def dft_tables():
    omega = 2.0 * np.pi * (np.arange(freqs) + 0.5) / bins
    rows = np.arange(window)
    angles = omega[:, None] * rows
    forward = np.concatenate([np.cos(angles), -np.sin(angles)])
    return forward, forward.T / freqs


def split_bf16(value):
    upper = value.astype(jnp.bfloat16)
    return upper, (value - upper.astype(jnp.float32)).astype(jnp.bfloat16)


def dot(left, right):
    return jnp.dot(left, right, preferred_element_type=jnp.float32)


def dot_t(left, right):
    return lax.dot_general(
        left, right, (((1,), (1,)), ((), ())), preferred_element_type=jnp.float32
    )


def dot_ta(left, right):
    return lax.dot_general(
        left, right, (((0,), (0,)), ((), ())), preferred_element_type=jnp.float32
    )


def taps(pieces, weight, member, start, count, sign):
    rows = jnp.concatenate([piece.astype(jnp.float32) for piece in pieces], axis=0)
    total = rows.shape[0]
    tap = [weight[offset, member : member + 1, :] for offset in range(7)]

    def moved(value, by):
        return pltpu.roll(value, (sign * by) % total, 0)

    one = moved(rows, 1)
    two = moved(rows, 2)
    tail = tap[4] * rows + tap[5] * one + tap[6] * two
    tail = tap[2] * rows + tap[3] * one + moved(tail, 2)
    tail = tap[0] * rows + tap[1] * one + moved(tail, 2)
    return tail[start : start + count]


def gains(med, analysis, block):
    groups = med.shape[1]
    channel = lax.broadcasted_iota(jnp.int32, (groups, columns), 1) + block * columns
    group = lax.broadcasted_iota(jnp.int32, (groups, columns), 0)
    expand = jnp.where(channel // per_group == group, 1.0, 0.0).astype(jnp.bfloat16)
    wide = dot(med, expand).astype(jnp.bfloat16)
    count = med.shape[0]
    return dot(analysis[0, :, :count], wide) + dot(analysis[1, :, :count], wide)


def pack_kernel(
    length, q, k, v, out_weight, head,
    to_right, to_left, far_right, far_left, shard_out, head_out,
    sems,
):
    half = to_right.shape[1]
    copies = []

    def move(source, first, rows, side, target, at):
        copies.append(
            pltpu.make_async_copy(
                source.at[pl.ds(first, rows), pl.ds(side * half, half)],
                target.at[pl.ds(at, rows), :],
                sems.at[len(copies)],
            )
        )
        copies[-1].start()

    for target, mine, last in ((to_right, 0, True), (to_left, 1, False)):
        far_at = length - far if last else 0
        near_at = length - near if last else 0
        move(k, far_at, far, mine, target, 0)
        move(v, far_at, far, mine, target, far)
        move(q, near_at, near, mine, target, 2 * far)
        move(k, near_at, near, 1 - mine, target, 2 * far + near)
        move(v, near_at, near, 1 - mine, target, 2 * far + 2 * near)
    move(q, length - far, far, 1, far_right, 0)
    move(q, 0, far, 0, far_left, 0)

    def thirds(value):
        first, rest = split_bf16(value)
        second = (value - first.astype(jnp.float32)).astype(jnp.bfloat16)
        third = (value - first.astype(jnp.float32) - second.astype(jnp.float32)).astype(
            jnp.bfloat16
        )
        return jnp.concatenate(
            [
                first.astype(jnp.float32),
                second.astype(jnp.float32),
                third.astype(jnp.float32),
                jnp.zeros((parts - 12, value.shape[1]), jnp.float32),
            ],
            axis=0,
        ).astype(jnp.bfloat16)

    coded = thirds(head[...])
    head_out[...] = coded
    found = dot_t(coded, out_weight[...])
    shard = thirds(found[0:4] + found[4:8] + found[8:12])
    for device in range(shard_out.shape[0]):
        shard_out[device] = shard
    for copy in copies:
        copy.wait()


def class_block(class_rows):
    return jnp.concatenate([class_rows[piece] for piece in range(class_rows.shape[0])], axis=1)


def long_conv(rows_ref, spectrum, analysis, synthesis, causal):
    gain_re = spectrum[0:freqs, :]
    gain_im = spectrum[freqs:bins, :]
    if not causal:
        gain_im = -gain_im
    pieces = []
    for index in range(2):
        rows = rows_ref[index * step : index * step + window, :]
        found = dot(analysis[0], rows) + dot(analysis[1], rows)
        re, im = found[:freqs], found[freqs:]
        mixed = jnp.concatenate([re * gain_re - im * gain_im, re * gain_im + im * gain_re], axis=0)
        high, low = split_bf16(mixed)
        piece = dot(synthesis[0], high) + dot(synthesis[0], low) + dot(synthesis[1], high)
        pieces.append(piece[:step] if index == 0 else piece)
    return jnp.concatenate(pieces, axis=0)


def forward_kernel(
    length, q, k, v, s, left, right, weight, head_rows, class_rows, med, target, analysis,
    synth_c, synth_a, fold,
    gate_out, gated_out, mix_out, key_out, value_out, grad_out,
    products, spectrum, sums,
):
    block = pl.program_id(0)
    side = pl.program_id(1)

    @pl.when((block == 0) & (side == 0))
    def _():
        sums[...] = jnp.zeros_like(sums)

    @pl.when(side == 0)
    def _():
        spectrum[...] = gains(med[...], analysis, block)

    def one(forward):
        main, other = (left, right) if forward else (right, left)
        sign = 1 if forward else -1
        start = near if forward else 0
        first = span - length - near if forward else 0

        def order(*pieces):
            return pieces if forward else pieces[::-1]

        for at in range(0, columns, sub):
            cols = slice(at, at + sub)
            taken = weight[:, :, cols]
            k_far, v_far = main[0:far, cols], main[far : 2 * far, cols]
            q_near = main[2 * far : 2 * far + near, cols]
            k_near = other[2 * far + near : 2 * far + 2 * near, cols]
            v_near = other[2 * far + 2 * near : 2 * far + 3 * near, cols]
            key_feat = taps(order(k_far, k[:, cols], k_near), taken, 1, start, span, sign)
            key_out[:, cols] = key_feat[first : first + length + near].astype(jnp.bfloat16)
            value_feat = taps(order(v_far, v[:, cols], v_near), taken, 2, start, span, sign)
            value_out[:, cols] = value_feat[first : first + length + near].astype(jnp.bfloat16)
            products[:, cols] = (key_feat * value_feat).astype(jnp.bfloat16)
            gate = taps(order(q_near, q[:, cols]), taken, 0, start, length, sign)
            gate_out[:, cols] = gate.astype(jnp.bfloat16)
        mix = long_conv(products, spectrum, analysis, synth_c if forward else synth_a, forward)
        mix_out[...] = mix.astype(jnp.bfloat16)
        local = mix[:length] if forward else mix[near:]
        gated = (gate_out[...].astype(jnp.float32) * local).astype(jnp.bfloat16)
        gated_out[...] = gated
        sums[0 if forward else 1] += dot_t(gated, class_block(class_rows)) + dot_t(
            s[...], head_rows[...]
        )

    pl.when(side == 0)(functools.partial(one, True))
    pl.when(side == 1)(functools.partial(one, False))

    @pl.when((block == pl.num_programs(0) - 1) & (side == 1))
    def _():
        exact = lax.Precision.HIGHEST
        logits = jnp.dot(
            sums[0], fold[0], precision=exact, preferred_element_type=jnp.float32
        ) + jnp.dot(sums[1], fold[1], precision=exact, preferred_element_type=jnp.float32)
        logits = jnp.transpose(logits)[:8]
        row = lax.broadcasted_iota(jnp.int32, logits.shape, 0)
        valid = row < 4
        top = jnp.max(jnp.where(valid, logits, -jnp.inf), axis=0, keepdims=True)
        exponent = jnp.where(valid, jnp.exp(logits - top), 0.0)
        softmax_out = exponent / jnp.sum(exponent, axis=0, keepdims=True)
        one_hot = jnp.where(row == target[...], 1.0, 0.0)
        grad_out[...] = loss_scale * (softmax_out - one_hot)


def middle_kernel(
    length, q, far_left, far_right, gated, weight, grad,
    partial_out, halo_out,
    turned,
):
    block = pl.program_id(0)
    side = pl.program_id(1)

    @pl.when((block == 0) & (side == 0))
    def _():
        turned[0] = grad[...]
        for lane in range(4):
            turned[1, lane : lane + 1, :] = grad[3 - lane : 4 - lane, :]
        turned[1, 4:8, :] = jnp.zeros((4, length), jnp.float32)

    def one(forward):
        high, low = split_bf16(turned[0 if forward else 1])
        term = dot(high, gated[...]) + dot(low, gated[...])
        for piece in range(columns // 128):
            cut = term[:, piece * 128 : piece * 128 + 128]
            if forward:
                partial_out[piece] = cut
            else:
                partial_out[piece] += cut
        for at in range(0, columns, sub):
            cols = slice(at, at + sub)
            taken = weight[:, :, cols]
            if forward:
                halo = taps(
                    (q[length - near :, cols], far_right[:, cols]), taken, 0, near, far, 1
                )
            else:
                halo = taps((far_left[:, cols], q[:near, cols]), taken, 0, 0, far, -1)
            halo_out[:, cols] = halo.astype(jnp.bfloat16)

    pl.when(side == 0)(functools.partial(one, True))
    pl.when(side == 1)(functools.partial(one, False))


def backward_kernel(
    length, gate, halo, mix, key_feat, value_feat, weight, class_rows, med, grad, grad_left,
    grad_right, analysis, synth_c, synth_a, place,
    query_out, key_out, value_out,
    coded, mix_grad, spectrum,
):
    block = pl.program_id(0)
    side = pl.program_id(1)
    extent = length + near

    @pl.when((block == 0) & (side == 0))
    def _():
        def code(piece, side_at):
            high, low = split_bf16(piece[...])
            return (
                dot_ta(high, place[side_at, 0]) + dot_ta(low, place[side_at, 1])
            ).astype(jnp.bfloat16)

        coded[0, :length] = code(grad, 0)
        coded[0, length:] = code(grad_right, 0)[:far]
        coded[1, :far] = code(grad_left, 1)[length - far :]
        coded[1, far:] = code(grad, 1)

    @pl.when(side == 0)
    def _():
        spectrum[...] = gains(med[...], analysis, block)

    def one(forward):
        classes = class_block(class_rows)
        grads = dot(coded[0 if forward else 1], jnp.concatenate([classes, classes], axis=0))
        start = 0 if forward else near
        sign = -1 if forward else 1
        gates = (gate[...], halo[...]) if forward else (halo[...], gate[...])
        gates = jnp.concatenate([piece.astype(jnp.float32) for piece in gates], axis=0)
        mix_grad[...] = (grads * gates).astype(jnp.bfloat16)
        near_grads = grads[:extent] if forward else grads[span - extent :]
        for at in range(0, columns, sub):
            cols = slice(at, at + sub)
            query_out[:, cols] = taps(
                (near_grads[:, cols] * mix[:, cols].astype(jnp.float32),),
                weight[:, :, cols], 0, start, length, sign,
            ).astype(jnp.bfloat16)
        back = long_conv(
            mix_grad, spectrum, analysis, synth_a if forward else synth_c, not forward
        )
        for at in range(0, columns, sub):
            cols = slice(at, at + sub)
            for member, feat, out in ((1, value_feat, key_out), (2, key_feat, value_out)):
                out[:, cols] = taps(
                    (back[:, cols] * feat[:, cols].astype(jnp.float32),),
                    weight[:, :, cols], member, start, length, sign,
                ).astype(jnp.bfloat16)

    pl.when(side == 0)(functools.partial(one, True))
    pl.when(side == 1)(functools.partial(one, False))


def final_kernel(terms, head, out):
    total = jnp.sum(terms[...], axis=0)
    out[...] = lax.dot_general(
        total[:4],
        head[...] * (1.0 / loss_scale),
        (((0,), (0,)), ((), ())),
        precision=lax.Precision.HIGHEST,
        preferred_element_type=jnp.float32,
    )


def per_device(query, key, value, stream, targets, short_filter, med_filter, out_weight, head):
    length = query.shape[1]
    channels = query.shape[2]
    half = channels // 2
    blocks = half // columns
    count = lax.axis_size("seq")
    owners = lax.axis_size("fsdp")
    own = half // owners
    rightward = [(i, i + 1) for i in range(count - 1)]
    leftward = [(i + 1, i) for i in range(count - 1)]
    query, key, value, stream = query[0], key[0], value[0], stream[0]
    bf16, f32 = jnp.bfloat16, jnp.float32
    extent = length + near
    packed = 2 * far + 3 * near
    shape = jax.ShapeDtypeStruct
    raw = pl.BlockSpec(memory_space=pl.ANY)
    whole = pl.BlockSpec(memory_space=pltpu.VMEM)
    limit = pltpu.CompilerParams(vmem_limit_bytes=vmem_limit)

    to_right, to_left, far_right, far_left, shard, head_rows = pl.pallas_call(
        functools.partial(pack_kernel, length),
        in_specs=[raw] * 3 + [whole] * 2,
        out_specs=[raw] * 4 + [whole] * 2,
        out_shape=[shape((packed, half), bf16)] * 2
        + [shape((far, half), bf16)] * 2
        + [shape((owners, parts, own), bf16), shape((parts, half), bf16)],
        scratch_shapes=[pltpu.SemaphoreType.DMA((12,))],
        compiler_params=limit,
        name="pack",
    )(query, key, value, out_weight, head)

    from_left = lax.ppermute(to_right, "seq", rightward)
    from_right = lax.ppermute(to_left, "seq", leftward)
    class_rows = lax.all_to_all(shard, "fsdp", 0, 0, tiled=True)
    if own != lanes:
        class_rows = class_rows.reshape(owners, parts, -1, lanes).transpose(0, 2, 1, 3)
        class_rows = class_rows.reshape(-1, parts, lanes)
    halo_left = lax.ppermute(far_right, "seq", rightward)
    halo_right = lax.ppermute(far_left, "seq", leftward)

    forward, inverse = dft_tables()
    analysis = jnp.asarray(np.stack(split_np(forward)))
    synth_c = jnp.asarray(np.stack(split_np(inverse[lead:])))
    synth_a = jnp.asarray(np.stack(split_np(inverse[:keep])))

    fold = np.zeros((2, parts, 128), np.float32)
    place = np.zeros((2, 2, 8, 2 * parts), np.float32)
    for lane in range(4):
        for part in range(3):
            fold[0, 4 * part + lane, lane] = 1.0
            fold[1, 4 * part + 3 - lane, lane] = 1.0
            for level in range(2):
                place[0, level, lane, level * parts + 4 * part + lane] = 1.0
                place[1, level, 3 - lane, level * parts + 4 * part + lane] = 1.0
    place = jnp.asarray(place.astype(ml_dtypes.bfloat16))

    def full(array):
        rank = len(array.shape)
        return pl.BlockSpec(array.shape, lambda *_: (0,) * rank)

    def by_channel(rows):
        return pl.BlockSpec((rows, columns), lambda b, s: (0, s * blocks + b))

    def by_half(rows):
        return pl.BlockSpec((rows, columns), lambda b, s: (0, b))

    weight_spec = pl.BlockSpec(
        short_filter.shape[:2] + (columns,), lambda b, s: (0, 0, b)
    )

    def by_owner(rows):
        return pl.BlockSpec((columns // lanes, rows, lanes), lambda b, s: (b, 0, 0))

    params = pltpu.CompilerParams(
        dimension_semantics=("arbitrary", "arbitrary"), vmem_limit_bytes=vmem_limit
    )
    grad_shape = shape((8, length), f32)
    gate, gated, mix, key_feat, value_feat, grad = pl.pallas_call(
        functools.partial(forward_kernel, length),
        grid=(blocks, 2),
        in_specs=[by_channel(length)] * 4
        + [by_half(packed)] * 2
        + [
            weight_spec, by_half(parts), by_owner(parts), full(med_filter), full(targets),
            full(analysis), full(synth_c), full(synth_a), full(fold),
        ],
        out_specs=[by_channel(length)] * 2 + [by_channel(extent)] * 3 + [full(grad_shape)],
        out_shape=[shape((length, channels), bf16)] * 2
        + [shape((extent, channels), bf16)] * 3
        + [grad_shape],
        scratch_shapes=[
            pltpu.VMEM((span, columns), bf16),
            pltpu.VMEM((bins, columns), f32),
            pltpu.VMEM((2, length, parts), f32),
        ],
        compiler_params=params,
        name="features_and_logits",
    )(
        query, key, value, stream, from_left, from_right, short_filter, head_rows, class_rows,
        med_filter, targets, analysis, synth_c, synth_a, jnp.asarray(fold),
    )

    grad_left = lax.ppermute(grad, "seq", rightward)
    grad_right = lax.ppermute(grad, "seq", leftward)

    partial, halo = pl.pallas_call(
        functools.partial(middle_kernel, length),
        grid=(blocks, 2),
        in_specs=[
            by_channel(length), by_half(far), by_half(far), by_channel(length), weight_spec,
            full(grad),
        ],
        out_specs=[by_owner(8), by_channel(far)],
        out_shape=[shape((half // lanes, 8, lanes), f32), shape((far, channels), bf16)],
        scratch_shapes=[pltpu.VMEM((2, 8, length), f32)],
        compiler_params=params,
        name="weight_partial_and_gate_halo",
    )(query, halo_left, halo_right, gated, short_filter, grad)

    query_grad, key_grad, value_grad = pl.pallas_call(
        functools.partial(backward_kernel, length),
        grid=(blocks, 2),
        in_specs=[by_channel(length), by_channel(far)]
        + [by_channel(extent)] * 3
        + [
            weight_spec, by_owner(parts), full(med_filter), full(grad), full(grad), full(grad),
            full(analysis), full(synth_c), full(synth_a), full(place),
        ],
        out_specs=[by_channel(length)] * 3,
        out_shape=[shape((length, channels), bf16)] * 3,
        scratch_shapes=[
            pltpu.VMEM((2, span, 2 * parts), bf16),
            pltpu.VMEM((span, columns), bf16),
            pltpu.VMEM((bins, columns), f32),
        ],
        compiler_params=params,
        name="gradients",
    )(
        gate, halo, mix, key_feat, value_feat, short_filter, class_rows, med_filter, grad,
        grad_left, grad_right, analysis, synth_c, synth_a, place,
    )

    if own != lanes:
        partial = partial.reshape(owners, -1, 8, lanes).transpose(0, 2, 1, 3)
        partial = partial.reshape(owners, 8, own)
    over_genomes = jnp.sum(lax.all_to_all(partial, "fsdp", 0, 0, tiled=True), axis=0)
    spread = jnp.broadcast_to(over_genomes, (count,) + over_genomes.shape)
    terms = lax.all_to_all(spread, "seq", 0, 0, tiled=True)
    out_grad = pl.pallas_call(
        final_kernel,
        in_specs=[whole] * 2,
        out_specs=whole,
        out_shape=shape((own, half), f32),
        compiler_params=limit,
        name="final",
    )(terms, head)
    return query_grad[None], key_grad[None], value_grad[None], out_grad


def solution(mesh):
    rows = P("fsdp", "seq", None)
    placed = (rows, rows, rows, rows, P("fsdp", "seq"), P(), P(), P("fsdp", None), P())
    return jax.shard_map(
        per_device,
        mesh=mesh,
        in_specs=placed,
        out_specs=(rows, rows, rows, P("fsdp", None)),
        check_vma=False,
    )
```

profile of v0, /device:TPU:4, one launch (start us, length us, event | category | flops | bytes accessed | tf_op | source)
XLA Modules:
  0.0 129.5 jit_solution(9233806168542071768)
XLA Ops:
  0.6 1.3 %copy-done = bf16[1,160,4096]{2,1,0:T(8,128)(2,1)S(1)} copy-done((bf16[1,160,4096]{2,1,0:T(8,128)(2,1)S(1)}, bf16[1,160,4096]{2,1,0:T(8,128)(2,1)}, u32[]{:S(2)}) %copy-start) | copy-done | bytes 1310744
  2.0 1.3 %copy-done.2 = bf16[1,160,4096]{2,1,0:T(8,128)(2,1)S(1)} copy-done((bf16[1,160,4096]{2,1,0:T(8,128)(2,1)S(1)}, bf16[1,160,4096]{2,1,0:T(8,128)(2,1)}, u32[]{:S(2)}) %copy-start.2) | copy-done | bytes 1310744
  3.3 1.3 %copy-done.4 = bf16[1,160,4096]{2,1,0:T(8,128)(2,1)S(1)} copy-done((bf16[1,160,4096]{2,1,0:T(8,128)(2,1)S(1)}, bf16[1,160,4096]{2,1,0:T(8,128)(2,1)}, u32[]{:S(2)}) %copy-start.4) | copy-done | bytes 1310744
  4.6 1.0 copy-done.18
  5.6 0.8 copy-done.22
  6.4 2.6 %pack.1 = (bf16[296,2048]{1,0:T(8,128)(2,1)}, bf16[296,2048]{1,0:T(8,128)(2,1)}, bf16[136,2048]{1,0:T(8,128)(2,1)}, bf16[136,2048]{1,0:T(8,128)(2,1)}, bf16[16,1...) custom-call(bf16[160,4096]{1,0:T(8,128)(2,1)S(1)} %bitcast.7, bf16[160,4096]{1,0:T(8,128)(2,1)S(1)} %bitcast.10, ...), custom_call_target="tpu_custom_call" | custom-call | tf_op jit(solution)/shard_map/pack/pallas_call | solution.py:361
  9.0 1.9 %collective-permute-start = (bf16[296,2048]{1,0:T(8,128)(2,1)}, bf16[296,2048]{1,0:T(8,128)(2,1)}, u32[]{:S(2)}, u32[]{:S(2)}) collective-permute-start(bf16[296,2048]{1,0:T(8,128)(2,1)} %get-tuple-element.21), channel_id=1, source_target_pairs={{0,16},{16,32},{32,48},{48,64},{64,80},{80,96},{96,112},{112,128},... | collective-permute-start | bytes 3637256 | tf_op jit(solution)/shard_map/ppermute | solution.py:373
  11.0 7.3 %collective-permute-start.1 = (bf16[296,2048]{1,0:T(8,128)(2,1)}, bf16[296,2048]{1,0:T(8,128)(2,1)}, u32[]{:S(2)}, u32[]{:S(2)}) collective-permute-start(bf16[296,2048]{1,0:T(8,128)(2,1)} %get-tuple-element.22), channel_id=1, source_target_pairs={{16,0},{32,16},{48,32},{64,48},{80,64},{96,80},{112,96},{128,112},... | collective-permute-start | bytes 3637256 | tf_op jit(solution)/shard_map/ppermute | solution.py:374
  18.2 1.9 %collective-permute-start.2 = (bf16[136,2048]{1,0:T(8,128)(2,1)}, bf16[136,2048]{1,0:T(8,128)(2,1)}, u32[]{:S(2)}, u32[]{:S(2)}) collective-permute-start(bf16[136,2048]{1,0:T(8,128)(2,1)} %get-tuple-element.26), channel_id=1, source_target_pairs={{0,16},{16,32},{32,48},{48,64},{64,80},{80,96},{96,112},{112,128},... | collective-permute-start | bytes 1671176 | tf_op jit(solution)/shard_map/ppermute | solution.py:379
  20.2 7.3 %collective-permute-start.3 = (bf16[136,2048]{1,0:T(8,128)(2,1)}, bf16[136,2048]{1,0:T(8,128)(2,1)}, u32[]{:S(2)}, u32[]{:S(2)}) collective-permute-start(bf16[136,2048]{1,0:T(8,128)(2,1)} %get-tuple-element.27), channel_id=1, source_target_pairs={{16,0},{32,16},{48,32},{64,48},{80,64},{96,80},{112,96},{128,112},... | collective-permute-start | bytes 1671176 | tf_op jit(solution)/shard_map/ppermute | solution.py:380
  27.4 9.2 %all-to-all-start = ((bf16[16,16,128]{2,1,0:T(8,128)(2,1)}), bf16[16,16,128]{2,1,0:T(8,128)(2,1)S(1)}, u32[]{:S(2)}, u32[]{:S(2)}) async-start(bf16[16,16,128]{2,1,0:T(8,128)(2,1)} %get-tuple-element.24), calls=%async_computation | async-start | bytes 131072 | tf_op jit(solution)/shard_map/all_to_all | solution.py:375
  36.7 1.0 copy.18.weight
  37.7 7.5 %all-to-all-done.class_rows = bf16[16,16,128]{2,1,0:T(8,128)(2,1)S(1)} async-done(((bf16[16,16,128]{2,1,0:T(8,128)(2,1)}), bf16[16,16,128]{2,1,0:T(8,128)(2,1)S(1)}, u32[]{:S(2)}, u32[]{:S(2)}) %all-to-all-start) | async-done | bytes 65568 | tf_op jit(solution)/shard_map/all_to_all | solution.py:375
  45.3 1.3 %copy-done.5 = bf16[1,160,4096]{2,1,0:T(8,128)(2,1)S(1)} copy-done((bf16[1,160,4096]{2,1,0:T(8,128)(2,1)S(1)}, bf16[1,160,4096]{2,1,0:T(8,128)(2,1)}, u32[]{:S(2)}) %copy-start.5) | copy-done | bytes 1310744
  46.6 1.3 %copy-done.12 = bf16[1,160,4096]{2,1,0:T(8,128)(2,1)S(1)} copy-done((bf16[1,160,4096]{2,1,0:T(8,128)(2,1)S(1)}, bf16[1,160,4096]{2,1,0:T(8,128)(2,1)}, u32[]{:S(2)}) %copy-start.12) | copy-done | bytes 1310744
  47.9 18.7 %features_and_logits.1 = (bf16[160,4096]{1,0:T(8,128)(2,1)S(1)}, bf16[160,4096]{1,0:T(8,128)(2,1)S(1)}, bf16[168,4096]{1,0:T(8,128)(2,1)S(1)}, bf16[168,4096]{1,...) custom-call(bf16[160,4096]{1,0:T(8,128)(2,1)S(1)} %bitcast.8, bf16[160,4096]{1,0:T(8,128)(2,1)S(1)} %bitcast.11, ...), custom_call_target="tpu_custom_call" | custom-call | tf_op jit(solution)/shard_map/features_and_logits/pallas_call | solution.py:419
  66.6 1.1 copy-done.10
  67.8 1.1 copy-done.13
  68.9 5.1 %weight_partial_and_gate_halo.1 = (f32[16,8,128]{2,1,0:T(8,128)S(1)}, bf16[136,4096]{1,0:T(8,128)(2,1)S(1)}) custom-call(bf16[160,4096]{1,0:T(8,128)(2,1)S(1)} %bitcast.9, bf16[136,2048]{1,0:T(8,128)(2,1)} %collective-permute-done.2.far_left, bf16[136,2048]{1,0:T(8,128)(2,1)} %collective-permute-done.3.far_right, ...), custom_call_target="tpu_custom_call" | custom-call | tf_op jit(solution)/shard_map/weight_partial_and_gate_halo/pallas_call | solution.py:447
  74.0 1.0 copy-done.15
  75.0 12.8 %all_to_all.15 = f32[16,8,128]{2,1,0:T(8,128)S(1)} all-to-all(f32[16,8,128]{2,1,0:T(8,128)S(1)} %get-tuple-element.37), channel_id=1, replica_groups=mesh['seq'=16,'fsdp'=16] {'fsdp'}, dimensions={0} | all-to-all | bytes 131072 | tf_op jit(solution)/shard_map/all_to_all | solution.py:487
  87.8 0.6 broadcast_in_dim.15
  88.4 4.8 %all-to-all-start.2 = ((f32[16,8,128]{2,1,0:T(8,128)}), f32[16,8,128]{2,1,0:T(8,128)S(1)}, u32[]{:S(2)}, u32[]{:S(2)}) async-start(f32[16,8,128]{2,1,0:T(8,128)} %broadcast_in_dim.15), calls=%async_computation.2 | async-start | bytes 131072 | tf_op jit(solution)/shard_map/all_to_all | solution.py:489
  93.2 4.3 %collective-permute-start.5 = (f32[8,160]{1,0:T(8,128)S(1)}, f32[8,160]{1,0:T(8,128)S(1)}, u32[]{:S(2)}, u32[]{:S(2)}) collective-permute-start(f32[8,160]{1,0:T(8,128)S(1)} %get-tuple-element.29.grad), channel_id=1, source_target_pairs={{16,0},{32,16},{48,32},{64,48},{80,64},{96,80},{112,96},{128,112},... | collective-permute-start | bytes 15368 | tf_op jit(solution)/shard_map/ppermute | solution.py:445
  97.6 2.1 %collective-permute-start.4 = (f32[8,160]{1,0:T(8,128)S(1)}, f32[8,160]{1,0:T(8,128)S(1)}, u32[]{:S(2)}, u32[]{:S(2)}) collective-permute-start(f32[8,160]{1,0:T(8,128)S(1)} %get-tuple-element.29.grad), channel_id=1, source_target_pairs={{0,16},{16,32},{32,48},{48,64},{64,80},{80,96},{96,112},{112,128},... | collective-permute-start | bytes 15368 | tf_op jit(solution)/shard_map/ppermute | solution.py:444
  99.7 6.5 %collective-permute-done.4.grad_left = f32[8,160]{1,0:T(8,128)S(1)} collective-permute-done((f32[8,160]{1,0:T(8,128)S(1)}, f32[8,160]{1,0:T(8,128)S(1)}, u32[]{:S(2)}, u32[]{:S(2)}) %collective-permute-start.4) | collective-permute-done | bytes 5152 | tf_op jit(solution)/shard_map/ppermute | solution.py:444
  106.2 1.3 %copy-done.7 = bf16[168,4096]{1,0:T(8,128)(2,1)S(1)} copy-done((bf16[168,4096]{1,0:T(8,128)(2,1)S(1)}, bf16[168,4096]{1,0:T(8,128)(2,1)}, u32[]{:S(2)}) %copy-start.7) | copy-done | bytes 1376280
  107.5 1.3 %copy-done.9 = bf16[168,4096]{1,0:T(8,128)(2,1)S(1)} copy-done((bf16[168,4096]{1,0:T(8,128)(2,1)S(1)}, bf16[168,4096]{1,0:T(8,128)(2,1)}, u32[]{:S(2)}) %copy-start.9) | copy-done | bytes 1376280
  108.8 1.3 %copy-done.11 = bf16[168,4096]{1,0:T(8,128)(2,1)S(1)} copy-done((bf16[168,4096]{1,0:T(8,128)(2,1)S(1)}, bf16[168,4096]{1,0:T(8,128)(2,1)}, u32[]{:S(2)}) %copy-start.11) | copy-done | bytes 1376280
  110.2 1.2 copy-done.16
  111.4 16.1 %gradients.1 = (bf16[160,4096]{1,0:T(8,128)(2,1)}, bf16[160,4096]{1,0:T(8,128)(2,1)}, bf16[160,4096]{1,0:T(8,128)(2,1)}) custom-call(bf16[160,4096]{1,0:T(8,128)(2,1)S(1)} %copy-done.14, bf16[136,4096]{1,0:T(8,128)(2,1)S(1)} %copy-done.16, bf16[168,4096]{1,0:T(8,128)(2,1)S(1)} %copy-done.7, bf16[168,4096]{1,0:T(8,128)(2,1)S(1)} %copy-done.9, ...), custom_call_target="tpu_custom_call" | custom-call | tf_op jit(solution)/shard_map/gradients/pallas_call | solution.py:461
  127.5 2.0 %final.1 = f32[128,2048]{1,0:T(8,128)} custom-call(f32[16,8,128]{2,1,0:T(8,128)S(1)} %all-to-all-done.2.terms, f32[4,2048]{1,0:T(4,128)S(1)} %copy-done.23), custom_call_target="tpu_custom_call" | custom-call | tf_op jit(solution)/shard_map/final/pallas_call | solution.py:490
  (47 shorter events, 0.1 us)
Async XLA Ops:
  0.6 1.3 %copy-start = (bf16[1,160,4096]{2,1,0:T(8,128)(2,1)S(1)}, bf16[1,160,4096]{2,1,0:T(8,128)(2,1)}, u32[]{:S(2)}) copy-start(bf16[1,160,4096]{2,1,0:T(8,128)(2,1)} %param.14) | copy-start | bytes 3932164
  1.9 1.3 %copy-start.2 = (bf16[1,160,4096]{2,1,0:T(8,128)(2,1)S(1)}, bf16[1,160,4096]{2,1,0:T(8,128)(2,1)}, u32[]{:S(2)}) copy-start(bf16[1,160,4096]{2,1,0:T(8,128)(2,1)} %param.15) | copy-start | bytes 3932164
  3.3 1.3 %copy-start.4 = (bf16[1,160,4096]{2,1,0:T(8,128)(2,1)S(1)}, bf16[1,160,4096]{2,1,0:T(8,128)(2,1)}, u32[]{:S(2)}) copy-start(bf16[1,160,4096]{2,1,0:T(8,128)(2,1)} %param.16) | copy-start | bytes 3932164
  6.4 38.8 %copy-start.1 = (bf16[1,160,4096]{2,1,0:T(8,128)(2,1)S(1)}, bf16[1,160,4096]{2,1,0:T(8,128)(2,1)}, u32[]{:S(2)}) copy-start(bf16[1,160,4096]{2,1,0:T(8,128)(2,1)} %param.14) | copy-start | bytes 3932164
  6.4 38.8 %copy-start.3 = (bf16[1,160,4096]{2,1,0:T(8,128)(2,1)S(1)}, bf16[1,160,4096]{2,1,0:T(8,128)(2,1)}, u32[]{:S(2)}) copy-start(bf16[1,160,4096]{2,1,0:T(8,128)(2,1)} %param.15) | copy-start | bytes 3932164
  6.4 38.8 %copy-start.17 = (bf16[2,224,216]{2,1,0:T(8,128)(2,1)S(1)}, bf16[2,224,216]{2,1,0:T(8,128)(2,1)}, u32[]{:S(2)}) copy-start(bf16[2,224,216]{2,1,0:T(8,128)(2,1)} %constant.12.clone.analysis) | copy-start | bytes 580612
  6.4 38.8 %copy-start.19 = (bf16[2,88,224]{2,1,0:T(8,128)(2,1)S(1)}, bf16[2,88,224]{2,1,0:T(8,128)(2,1)}, u32[]{:S(2)}) copy-start(bf16[2,88,224]{2,1,0:T(8,128)(2,1)} %constant.14.clone.synth_a) | copy-start | bytes 236548
  6.4 38.8 %copy-start.20 = (bf16[2,88,224]{2,1,0:T(8,128)(2,1)S(1)}, bf16[2,88,224]{2,1,0:T(8,128)(2,1)}, u32[]{:S(2)}) copy-start(bf16[2,88,224]{2,1,0:T(8,128)(2,1)} %constant.13.clone.synth_c) | copy-start | bytes 236548
  6.4 38.8 %copy-start.21 = (bf16[128,128]{1,0:T(8,128)(2,1)S(1)}, bf16[128,128]{1,0:T(8,128)(2,1)}, u32[]{:S(2)}) copy-start(bf16[128,128]{1,0:T(8,128)(2,1)} %med.3) | copy-start | bytes 98308
  6.4 38.8 %copy-start.24 = (f32[2,16,128]{2,1,0:T(8,128)S(1)}, f32[2,16,128]{2,1,0:T(8,128)}, u32[]{:S(2)}) copy-start(f32[2,16,128]{2,1,0:T(8,128)} %constant.16.clone.fold) | copy-start | bytes 49156
  6.4 38.8 %copy-start.26 = (s32[1,160]{1,0:T(1,128)S(1)}, s32[1,160]{1,0:T(1,128)}, u32[]{:S(2)}) copy-start(s32[1,160]{1,0:T(1,128)} %target.1) | copy-start | bytes 1924
  9.0 36.1 %collective-permute-start = (bf16[296,2048]{1,0:T(8,128)(2,1)}, bf16[296,2048]{1,0:T(8,128)(2,1)}, u32[]{:S(2)}, u32[]{:S(2)}) collective-permute-start(bf16[296,2048]{1,0:T(8,128)(2,1)} %get-tuple-element.21), channel_id=1, source_target_pairs={{0,16},{16,32},{32,48},{48,64},{64,80},{80,96},{96,112},{112,128},... | collective-permute-start | bytes 3637256 | tf_op jit(solution)/shard_map/ppermute | solution.py:373
  11.0 34.2 %collective-permute-start.1 = (bf16[296,2048]{1,0:T(8,128)(2,1)}, bf16[296,2048]{1,0:T(8,128)(2,1)}, u32[]{:S(2)}, u32[]{:S(2)}) collective-permute-start(bf16[296,2048]{1,0:T(8,128)(2,1)} %get-tuple-element.22), channel_id=1, source_target_pairs={{16,0},{32,16},{48,32},{64,48},{80,64},{96,80},{112,96},{128,112},... | collective-permute-start | bytes 3637256 | tf_op jit(solution)/shard_map/ppermute | solution.py:374
  18.2 50.6 %collective-permute-start.2 = (bf16[136,2048]{1,0:T(8,128)(2,1)}, bf16[136,2048]{1,0:T(8,128)(2,1)}, u32[]{:S(2)}, u32[]{:S(2)}) collective-permute-start(bf16[136,2048]{1,0:T(8,128)(2,1)} %get-tuple-element.26), channel_id=1, source_target_pairs={{0,16},{16,32},{32,48},{48,64},{64,80},{80,96},{96,112},{112,128},... | collective-permute-start | bytes 1671176 | tf_op jit(solution)/shard_map/ppermute | solution.py:379
  20.2 48.7 %collective-permute-start.3 = (bf16[136,2048]{1,0:T(8,128)(2,1)}, bf16[136,2048]{1,0:T(8,128)(2,1)}, u32[]{:S(2)}, u32[]{:S(2)}) collective-permute-start(bf16[136,2048]{1,0:T(8,128)(2,1)} %get-tuple-element.27), channel_id=1, source_target_pairs={{16,0},{32,16},{48,32},{64,48},{80,64},{96,80},{112,96},{128,112},... | collective-permute-start | bytes 1671176 | tf_op jit(solution)/shard_map/ppermute | solution.py:380
  27.4 17.7 %all-to-all-start = ((bf16[16,16,128]{2,1,0:T(8,128)(2,1)}), bf16[16,16,128]{2,1,0:T(8,128)(2,1)S(1)}, u32[]{:S(2)}, u32[]{:S(2)}) async-start(bf16[16,16,128]{2,1,0:T(8,128)(2,1)} %get-tuple-element.24), calls=%async_computation | async-start | bytes 131072 | tf_op jit(solution)/shard_map/all_to_all | solution.py:375
  45.3 1.3 %copy-start.5 = (bf16[1,160,4096]{2,1,0:T(8,128)(2,1)S(1)}, bf16[1,160,4096]{2,1,0:T(8,128)(2,1)}, u32[]{:S(2)}) copy-start(bf16[1,160,4096]{2,1,0:T(8,128)(2,1)} %param.16) | copy-start | bytes 3932164
  46.6 1.3 %copy-start.12 = (bf16[1,160,4096]{2,1,0:T(8,128)(2,1)S(1)}, bf16[1,160,4096]{2,1,0:T(8,128)(2,1)}, u32[]{:S(2)}) copy-start(bf16[1,160,4096]{2,1,0:T(8,128)(2,1)} %param.17) | copy-start | bytes 3932164
  66.6 1.1 copy-start.10
  67.8 1.1 copy-start.13
  68.8 5.1 %copy-start.6 = (bf16[168,4096]{1,0:T(8,128)(2,1)}, bf16[168,4096]{1,0:T(8,128)(2,1)S(1)}, u32[]{:S(2)}) copy-start(bf16[168,4096]{1,0:T(8,128)(2,1)S(1)} %get-tuple-element.31.mix) | copy-start | bytes 4128772
  68.8 5.1 %copy-start.8 = (bf16[168,4096]{1,0:T(8,128)(2,1)}, bf16[168,4096]{1,0:T(8,128)(2,1)S(1)}, u32[]{:S(2)}) copy-start(bf16[168,4096]{1,0:T(8,128)(2,1)S(1)} %get-tuple-element.32.key_feat) | copy-start | bytes 4128772
  68.8 37.3 %copy-start.14 = (bf16[160,4096]{1,0:T(8,128)(2,1)S(1)}, bf16[160,4096]{1,0:T(8,128)(2,1)}, u32[]{:S(2)}) copy-start(bf16[160,4096]{1,0:T(8,128)(2,1)} %copy-done.13) | copy-start | bytes 3932164
  68.8 37.3 %copy-start.25 = (bf16[2,2,8,32]{3,2,1,0:T(8,128)(2,1)S(1)}, bf16[2,2,8,32]{3,2,1,0:T(8,128)(2,1)}, u32[]{:S(2)}) copy-start(bf16[2,2,8,32]{3,2,1,0:T(8,128)(2,1)} %constant.15.clone.place) | copy-start | bytes 6148
  88.4 39.1 %all-to-all-start.2 = ((f32[16,8,128]{2,1,0:T(8,128)}), f32[16,8,128]{2,1,0:T(8,128)S(1)}, u32[]{:S(2)}, u32[]{:S(2)}) async-start(f32[16,8,128]{2,1,0:T(8,128)} %broadcast_in_dim.15), calls=%async_computation.2 | async-start | bytes 131072 | tf_op jit(solution)/shard_map/all_to_all | solution.py:489
  93.2 6.4 %collective-permute-start.5 = (f32[8,160]{1,0:T(8,128)S(1)}, f32[8,160]{1,0:T(8,128)S(1)}, u32[]{:S(2)}, u32[]{:S(2)}) collective-permute-start(f32[8,160]{1,0:T(8,128)S(1)} %get-tuple-element.29.grad), channel_id=1, source_target_pairs={{16,0},{32,16},{48,32},{64,48},{80,64},{96,80},{112,96},{128,112},... | collective-permute-start | bytes 15368 | tf_op jit(solution)/shard_map/ppermute | solution.py:445
  97.6 8.6 %collective-permute-start.4 = (f32[8,160]{1,0:T(8,128)S(1)}, f32[8,160]{1,0:T(8,128)S(1)}, u32[]{:S(2)}, u32[]{:S(2)}) collective-permute-start(f32[8,160]{1,0:T(8,128)S(1)} %get-tuple-element.29.grad), channel_id=1, source_target_pairs={{0,16},{16,32},{32,48},{48,64},{64,80},{80,96},{96,112},{112,128},... | collective-permute-start | bytes 15368 | tf_op jit(solution)/shard_map/ppermute | solution.py:444
  106.2 1.3 %copy-start.7 = (bf16[168,4096]{1,0:T(8,128)(2,1)S(1)}, bf16[168,4096]{1,0:T(8,128)(2,1)}, u32[]{:S(2)}) copy-start(bf16[168,4096]{1,0:T(8,128)(2,1)} %copy-done.6) | copy-start | bytes 4128772
  107.5 1.3 %copy-start.9 = (bf16[168,4096]{1,0:T(8,128)(2,1)S(1)}, bf16[168,4096]{1,0:T(8,128)(2,1)}, u32[]{:S(2)}) copy-start(bf16[168,4096]{1,0:T(8,128)(2,1)} %copy-done.8) | copy-start | bytes 4128772
  108.8 1.3 %copy-start.11 = (bf16[168,4096]{1,0:T(8,128)(2,1)S(1)}, bf16[168,4096]{1,0:T(8,128)(2,1)}, u32[]{:S(2)}) copy-start(bf16[168,4096]{1,0:T(8,128)(2,1)} %copy-done.10) | copy-start | bytes 4128772
  110.2 1.2 copy-start.16
  111.4 16.1 %copy-start.23 = (f32[4,2048]{1,0:T(4,128)S(1)}, f32[4,2048]{1,0:T(4,128)}, u32[]{:S(2)}) copy-start(f32[4,2048]{1,0:T(4,128)} %head.3) | copy-start | bytes 98308
  (3 other events, 2.8 us)
where the time goes:
time: 130 us
  Pallas kernels  44.5 us (34%)
  starting transfers between devices  38.8 us (30%)
  local copies, waits for them, and re-layouts  18.5 us (14%)
  waiting for transfers between devices  14 us (11%)
  blocking collectives  12.8 us (10%)
    pallas_call x1, Pallas kernels, per_device(): pl.pallas_call(functools.partial(forward_kernel, length), grid=(blocks, 2...  18.7 us
    unnamed x55, local copies, waits for them, and re-layouts  17.9 us
    pallas_call x1, Pallas kernels, per_device(): pl.pallas_call(functools.partial(backward_kernel, length), grid=(blocks,...  16.1 us
    all_to_all x1, blocking collectives, per_device(): lax.all_to_all(partial, 'fsdp', 0, 0, tiled=True)  12.8 us
    all_to_all x1, starting transfers between devices, per_device(): class_rows = lax.all_to_all(shard, 'fsdp', 0, 0, tiled=True)  9.22 us
    all_to_all x1, waiting for transfers between devices, per_device(): class_rows = lax.all_to_all(shard, 'fsdp', 0, 0, tiled=True)  7.47 us
    ppermute x1, starting transfers between devices, per_device(): from_right = lax.ppermute(to_left, 'seq', leftward)  7.26 us
    ppermute x1, starting transfers between devices, per_device(): halo_right = lax.ppermute(far_left, 'seq', leftward)  7.26 us
  transfers between devices with their start and end apart: 8, of which 2 were waited for; matrix products, arithmetic and copies ran while one was open for 1% of the time, Pallas kernels for 27%

commit v1 on v0

--- a/solution.py
+++ b/solution.py
@@ -24,7 +24,7 @@
 parts = 16
 lanes = 128
 sub = 256
-vmem_limit = 24 * 1024 * 1024
+vmem_limit = 34 * 1024 * 1024
 
 
 def split_np(table):
@@ -85,15 +85,24 @@
     expand = jnp.where(channel // per_group == group, 1.0, 0.0).astype(jnp.bfloat16)
     wide = dot(med, expand).astype(jnp.bfloat16)
     count = med.shape[0]
-    return dot(analysis[0, :, :count], wide) + dot(analysis[1, :, :count], wide)
+    both = dot(analysis[:, :count], wide)
+    return both[:bins] + both[bins:]
+
+
+def in_hbm(array):
+    return pltpu.with_memory_space_constraint(array, pltpu.HBM)
 
 
 def pack_kernel(
     length, q, k, v, out_weight, head,
-    to_right, to_left, far_right, far_left, shard_out, head_out,
-    sems,
+    to_right, to_left, shard_out, head_out,
+    sems, weight_sem, head_sem, weight_rows, head_values,
 ):
     half = to_right.shape[1]
+    weight_copy = pltpu.make_async_copy(out_weight, weight_rows, weight_sem)
+    weight_copy.start()
+    head_copy = pltpu.make_async_copy(head, head_values, head_sem)
+    head_copy.start()
     copies = []
 
     def move(source, first, rows, side, target, at):
@@ -114,8 +123,6 @@
         move(q, near_at, near, mine, target, 2 * far)
         move(k, near_at, near, 1 - mine, target, 2 * far + near)
         move(v, near_at, near, 1 - mine, target, 2 * far + 2 * near)
-    move(q, length - far, far, 1, far_right, 0)
-    move(q, 0, far, 0, far_left, 0)
 
     def thirds(value):
         first, rest = split_bf16(value)
@@ -133,9 +140,11 @@
             axis=0,
         ).astype(jnp.bfloat16)
 
-    coded = thirds(head[...])
+    head_copy.wait()
+    coded = thirds(head_values[...])
     head_out[...] = coded
-    found = dot_t(coded, out_weight[...])
+    weight_copy.wait()
+    found = dot_t(coded, weight_rows[...])
     shard = thirds(found[0:4] + found[4:8] + found[8:12])
     for device in range(shard_out.shape[0]):
         shard_out[device] = shard
@@ -154,18 +163,23 @@
         gain_im = -gain_im
     pieces = []
     for index in range(2):
-        rows = rows_ref[index * step : index * step + window, :]
-        found = dot(analysis[0], rows) + dot(analysis[1], rows)
-        re, im = found[:freqs], found[freqs:]
+        both = dot(analysis[...], rows_ref[index * step : index * step + window, :])
+        re = both[:freqs] + both[bins : bins + freqs]
+        im = both[freqs:bins] + both[bins + freqs :]
         mixed = jnp.concatenate([re * gain_re - im * gain_im, re * gain_im + im * gain_re], axis=0)
         high, low = split_bf16(mixed)
-        piece = dot(synthesis[0], high) + dot(synthesis[0], low) + dot(synthesis[1], high)
+        both = dot(synthesis[...], high)
+        piece = both[:keep] + both[keep:] + dot(synthesis[:keep], low)
         pieces.append(piece[:step] if index == 0 else piece)
     return jnp.concatenate(pieces, axis=0)
 
 
+def kept(flag, piece):
+    return jnp.where(flag, piece, jnp.zeros_like(piece))
+
+
 def forward_kernel(
-    length, q, k, v, s, left, right, weight, head_rows, class_rows, med, target, analysis,
+    length, inner, q, k, v, s, left, right, weight, head_rows, class_rows, med, target, analysis,
     synth_c, synth_a, fold,
     gate_out, gated_out, mix_out, key_out, value_out, grad_out,
     products, spectrum, sums,
@@ -183,6 +197,9 @@
 
     def one(forward):
         main, other = (left, right) if forward else (right, left)
+        main_flag, other_flag = (inner[0] > 0, inner[1] > 0) if forward else (
+            inner[1] > 0, inner[0] > 0,
+        )
         sign = 1 if forward else -1
         start = near if forward else 0
         first = span - length - near if forward else 0
@@ -193,10 +210,14 @@
         for at in range(0, columns, sub):
             cols = slice(at, at + sub)
             taken = weight[:, :, cols]
-            k_far, v_far = main[0:far, cols], main[far : 2 * far, cols]
-            q_near = main[2 * far : 2 * far + near, cols]
-            k_near = other[2 * far + near : 2 * far + 2 * near, cols]
-            v_near = other[2 * far + 2 * near : 2 * far + 3 * near, cols]
+            k_far = kept(main_flag, main[0:far, cols].astype(jnp.float32))
+            v_far = kept(main_flag, main[far : 2 * far, cols].astype(jnp.float32))
+            q_near = main[2 * far : 2 * far + near, cols].astype(jnp.float32)
+            q_near = kept(main_flag, q_near)
+            k_near = other[2 * far + near : 2 * far + 2 * near, cols].astype(jnp.float32)
+            k_near = kept(other_flag, k_near)
+            v_near = other[2 * far + 2 * near : 2 * far + 3 * near, cols].astype(jnp.float32)
+            v_near = kept(other_flag, v_near)
             key_feat = taps(order(k_far, k[:, cols], k_near), taken, 1, start, span, sign)
             key_out[:, cols] = key_feat[first : first + length + near].astype(jnp.bfloat16)
             value_feat = taps(order(v_far, v[:, cols], v_near), taken, 2, start, span, sign)
@@ -205,8 +226,8 @@
             gate = taps(order(q_near, q[:, cols]), taken, 0, start, length, sign)
             gate_out[:, cols] = gate.astype(jnp.bfloat16)
         mix = long_conv(products, spectrum, analysis, synth_c if forward else synth_a, forward)
-        mix_out[...] = mix.astype(jnp.bfloat16)
         local = mix[:length] if forward else mix[near:]
+        mix_out[...] = local.astype(jnp.bfloat16)
         gated = (gate_out[...].astype(jnp.float32) * local).astype(jnp.bfloat16)
         gated_out[...] = gated
         sums[0 if forward else 1] += dot_t(gated, class_block(class_rows)) + dot_t(
@@ -233,15 +254,20 @@
 
 
 def middle_kernel(
-    length, q, far_left, far_right, gated, weight, grad,
-    partial_out, halo_out,
-    turned,
+    length, gate, gated, mix, class_rows, grad, place,
+    partial_out, mix_grad_out, gate_grad_out, to_left, to_right,
+    turned, coded,
 ):
     block = pl.program_id(0)
     side = pl.program_id(1)
 
     @pl.when((block == 0) & (side == 0))
     def _():
+        high, low = split_bf16(grad[...])
+        for side_at in range(2):
+            coded[side_at] = (
+                dot_ta(high, place[side_at, 0]) + dot_ta(low, place[side_at, 1])
+            ).astype(jnp.bfloat16)
         turned[0] = grad[...]
         for lane in range(4):
             turned[1, lane : lane + 1, :] = grad[3 - lane : 4 - lane, :]
@@ -250,71 +276,63 @@
     def one(forward):
         high, low = split_bf16(turned[0 if forward else 1])
         term = dot(high, gated[...]) + dot(low, gated[...])
-        for piece in range(columns // 128):
-            cut = term[:, piece * 128 : piece * 128 + 128]
+        for piece in range(columns // lanes):
+            cut = term[:, piece * lanes : piece * lanes + lanes]
             if forward:
                 partial_out[piece] = cut
             else:
                 partial_out[piece] += cut
-        for at in range(0, columns, sub):
-            cols = slice(at, at + sub)
-            taken = weight[:, :, cols]
-            if forward:
-                halo = taps(
-                    (q[length - near :, cols], far_right[:, cols]), taken, 0, near, far, 1
-                )
-            else:
-                halo = taps((far_left[:, cols], q[:near, cols]), taken, 0, 0, far, -1)
-            halo_out[:, cols] = halo.astype(jnp.bfloat16)
+        classes = class_block(class_rows)
+        grads = dot(coded[0 if forward else 1], jnp.concatenate([classes, classes], axis=0))
+        mix_grad = (grads * gate[...].astype(jnp.float32)).astype(jnp.bfloat16)
+        gate_grad = (grads * mix[...].astype(jnp.float32)).astype(jnp.bfloat16)
+        mix_grad_out[...] = mix_grad
+        gate_grad_out[...] = gate_grad
+        if forward:
+            to_left[0:far, :] = mix_grad[:far]
+            to_left[far:, :] = gate_grad[:near]
+        else:
+            to_right[0:far, :] = mix_grad[length - far :]
+            to_right[far:, :] = gate_grad[length - near :]
 
     pl.when(side == 0)(functools.partial(one, True))
     pl.when(side == 1)(functools.partial(one, False))
 
 
 def backward_kernel(
-    length, gate, halo, mix, key_feat, value_feat, weight, class_rows, med, grad, grad_left,
-    grad_right, analysis, synth_c, synth_a, place,
+    length, inner, mix_grad, gate_grad, left, right, key_feat, value_feat, weight, med, analysis,
+    synth_c, synth_a,
     query_out, key_out, value_out,
-    coded, mix_grad, spectrum,
+    extended, spectrum,
 ):
     block = pl.program_id(0)
     side = pl.program_id(1)
-    extent = length + near
-
-    @pl.when((block == 0) & (side == 0))
-    def _():
-        def code(piece, side_at):
-            high, low = split_bf16(piece[...])
-            return (
-                dot_ta(high, place[side_at, 0]) + dot_ta(low, place[side_at, 1])
-            ).astype(jnp.bfloat16)
-
-        coded[0, :length] = code(grad, 0)
-        coded[0, length:] = code(grad_right, 0)[:far]
-        coded[1, :far] = code(grad_left, 1)[length - far :]
-        coded[1, far:] = code(grad, 1)
 
     @pl.when(side == 0)
     def _():
         spectrum[...] = gains(med[...], analysis, block)
 
     def one(forward):
-        classes = class_block(class_rows)
-        grads = dot(coded[0 if forward else 1], jnp.concatenate([classes, classes], axis=0))
+        halo = right if forward else left
+        flag = (inner[1] if forward else inner[0]) > 0
         start = 0 if forward else near
         sign = -1 if forward else 1
-        gates = (gate[...], halo[...]) if forward else (halo[...], gate[...])
-        gates = jnp.concatenate([piece.astype(jnp.float32) for piece in gates], axis=0)
-        mix_grad[...] = (grads * gates).astype(jnp.bfloat16)
-        near_grads = grads[:extent] if forward else grads[span - extent :]
+        far_rows = kept(flag, halo[0:far, :].astype(jnp.float32)).astype(jnp.bfloat16)
+        if forward:
+            extended[0:length, :] = mix_grad[...]
+            extended[length:, :] = far_rows
+        else:
+            extended[0:far, :] = far_rows
+            extended[far:, :] = mix_grad[...]
         for at in range(0, columns, sub):
             cols = slice(at, at + sub)
+            rim = kept(flag, halo[far:, cols].astype(jnp.float32))
+            pieces = (gate_grad[:, cols], rim) if forward else (rim, gate_grad[:, cols])
             query_out[:, cols] = taps(
-                (near_grads[:, cols] * mix[:, cols].astype(jnp.float32),),
-                weight[:, :, cols], 0, start, length, sign,
+                pieces, weight[:, :, cols], 0, start, length, sign
             ).astype(jnp.bfloat16)
         back = long_conv(
-            mix_grad, spectrum, analysis, synth_a if forward else synth_c, not forward
+            extended, spectrum, analysis, synth_a if forward else synth_c, not forward
         )
         for at in range(0, columns, sub):
             cols = slice(at, at + sub)
@@ -347,25 +365,32 @@
     count = lax.axis_size("seq")
     owners = lax.axis_size("fsdp")
     own = half // owners
-    rightward = [(i, i + 1) for i in range(count - 1)]
-    leftward = [(i + 1, i) for i in range(count - 1)]
+    rightward = [(i, (i + 1) % count) for i in range(count)]
+    leftward = [((i + 1) % count, i) for i in range(count)]
     query, key, value, stream = query[0], key[0], value[0], stream[0]
     bf16, f32 = jnp.bfloat16, jnp.float32
     extent = length + near
     packed = 2 * far + 3 * near
     shape = jax.ShapeDtypeStruct
-    raw = pl.BlockSpec(memory_space=pl.ANY)
+    raw = pl.BlockSpec(memory_space=pltpu.HBM)
     whole = pl.BlockSpec(memory_space=pltpu.VMEM)
+    scalars = pl.BlockSpec(memory_space=pltpu.SMEM)
+    query, key, value, stream = in_hbm(query), in_hbm(key), in_hbm(value), in_hbm(stream)
     limit = pltpu.CompilerParams(vmem_limit_bytes=vmem_limit)
 
-    to_right, to_left, far_right, far_left, shard, head_rows = pl.pallas_call(
+    to_right, to_left, shard, head_rows = pl.pallas_call(
         functools.partial(pack_kernel, length),
-        in_specs=[raw] * 3 + [whole] * 2,
-        out_specs=[raw] * 4 + [whole] * 2,
+        in_specs=[raw] * 5,
+        out_specs=[whole] * 4,
         out_shape=[shape((packed, half), bf16)] * 2
-        + [shape((far, half), bf16)] * 2
         + [shape((owners, parts, own), bf16), shape((parts, half), bf16)],
-        scratch_shapes=[pltpu.SemaphoreType.DMA((12,))],
+        scratch_shapes=[
+            pltpu.SemaphoreType.DMA((10,)),
+            pltpu.SemaphoreType.DMA,
+            pltpu.SemaphoreType.DMA,
+            pltpu.VMEM(out_weight.shape, bf16),
+            pltpu.VMEM(head.shape, f32),
+        ],
         compiler_params=limit,
         name="pack",
     )(query, key, value, out_weight, head)
@@ -376,13 +401,13 @@
     if own != lanes:
         class_rows = class_rows.reshape(owners, parts, -1, lanes).transpose(0, 2, 1, 3)
         class_rows = class_rows.reshape(-1, parts, lanes)
-    halo_left = lax.ppermute(far_right, "seq", rightward)
-    halo_right = lax.ppermute(far_left, "seq", leftward)
+    position = lax.axis_index("seq")
+    inner = jnp.stack([position > 0, position < count - 1]).astype(jnp.int32)
 
     forward, inverse = dft_tables()
-    analysis = jnp.asarray(np.stack(split_np(forward)))
-    synth_c = jnp.asarray(np.stack(split_np(inverse[lead:])))
-    synth_a = jnp.asarray(np.stack(split_np(inverse[:keep])))
+    analysis = jnp.asarray(np.concatenate(split_np(forward)))
+    synth_c = jnp.asarray(np.concatenate(split_np(inverse[lead:])))
+    synth_a = jnp.asarray(np.concatenate(split_np(inverse[:keep])))
 
     fold = np.zeros((2, parts, 128), np.float32)
     place = np.zeros((2, 2, 8, 2 * parts), np.float32)
@@ -419,15 +444,16 @@
     gate, gated, mix, key_feat, value_feat, grad = pl.pallas_call(
         functools.partial(forward_kernel, length),
         grid=(blocks, 2),
-        in_specs=[by_channel(length)] * 4
+        in_specs=[scalars]
+        + [by_channel(length)] * 4
         + [by_half(packed)] * 2
         + [
             weight_spec, by_half(parts), by_owner(parts), full(med_filter), full(targets),
             full(analysis), full(synth_c), full(synth_a), full(fold),
         ],
-        out_specs=[by_channel(length)] * 2 + [by_channel(extent)] * 3 + [full(grad_shape)],
-        out_shape=[shape((length, channels), bf16)] * 2
-        + [shape((extent, channels), bf16)] * 3
+        out_specs=[by_channel(length)] * 3 + [by_channel(extent)] * 2 + [full(grad_shape)],
+        out_shape=[shape((length, channels), bf16)] * 3
+        + [shape((extent, channels), bf16)] * 2
         + [grad_shape],
         scratch_shapes=[
             pltpu.VMEM((span, columns), bf16),
@@ -437,48 +463,47 @@
         compiler_params=params,
         name="features_and_logits",
     )(
-        query, key, value, stream, from_left, from_right, short_filter, head_rows, class_rows,
+        inner, query, key, value, stream, from_left, from_right, short_filter, head_rows, class_rows,
         med_filter, targets, analysis, synth_c, synth_a, jnp.asarray(fold),
     )
 
-    grad_left = lax.ppermute(grad, "seq", rightward)
-    grad_right = lax.ppermute(grad, "seq", leftward)
-
-    partial, halo = pl.pallas_call(
+    partial, mix_grad, gate_grad, to_left, to_right = pl.pallas_call(
         functools.partial(middle_kernel, length),
         grid=(blocks, 2),
-        in_specs=[
-            by_channel(length), by_half(far), by_half(far), by_channel(length), weight_spec,
-            full(grad),
+        in_specs=[by_channel(length)] * 3 + [by_owner(parts), full(grad), full(place)],
+        out_specs=[by_owner(8)] + [by_channel(length)] * 2 + [by_half(far + near)] * 2,
+        out_shape=[shape((half // lanes, 8, lanes), f32)]
+        + [shape((length, channels), bf16)] * 2
+        + [shape((far + near, half), bf16)] * 2,
+        scratch_shapes=[
+            pltpu.VMEM((2, 8, length), f32),
+            pltpu.VMEM((2, length, 2 * parts), bf16),
         ],
-        out_specs=[by_owner(8), by_channel(far)],
-        out_shape=[shape((half // lanes, 8, lanes), f32), shape((far, channels), bf16)],
-        scratch_shapes=[pltpu.VMEM((2, 8, length), f32)],
         compiler_params=params,
-        name="weight_partial_and_gate_halo",
-    )(query, halo_left, halo_right, gated, short_filter, grad)
+        name="weight_partial_and_mix_grad",
+    )(gate, gated, mix, class_rows, grad, place)
+
+    mix_grad, gate_grad = in_hbm(mix_grad), in_hbm(gate_grad)
+    key_feat, value_feat = in_hbm(key_feat), in_hbm(value_feat)
+    grad_left = lax.ppermute(to_right, "seq", rightward)
+    grad_right = lax.ppermute(to_left, "seq", leftward)
 
     query_grad, key_grad, value_grad = pl.pallas_call(
         functools.partial(backward_kernel, length),
         grid=(blocks, 2),
-        in_specs=[by_channel(length), by_channel(far)]
-        + [by_channel(extent)] * 3
-        + [
-            weight_spec, by_owner(parts), full(med_filter), full(grad), full(grad), full(grad),
-            full(analysis), full(synth_c), full(synth_a), full(place),
-        ],
+        in_specs=[scalars]
+        + [by_channel(length)] * 2
+        + [by_half(far + near)] * 2
+        + [by_channel(extent)] * 2
+        + [weight_spec, full(med_filter), full(analysis), full(synth_c), full(synth_a)],
         out_specs=[by_channel(length)] * 3,
         out_shape=[shape((length, channels), bf16)] * 3,
-        scratch_shapes=[
-            pltpu.VMEM((2, span, 2 * parts), bf16),
-            pltpu.VMEM((span, columns), bf16),
-            pltpu.VMEM((bins, columns), f32),
-        ],
+        scratch_shapes=[pltpu.VMEM((span, columns), bf16), pltpu.VMEM((bins, columns), f32)],
         compiler_params=params,
         name="gradients",
     )(
-        gate, halo, mix, key_feat, value_feat, short_filter, class_rows, med_filter, grad,
-        grad_left, grad_right, analysis, synth_c, synth_a, place,
+        inner, mix_grad, gate_grad, grad_left, grad_right, key_feat, value_feat, short_filter,
+        med_filter, analysis, synth_c, synth_a,
     )
 
     if own != lanes:

time: 130 us -> 107 us (0.82)
  the two profiles are of different devices: /device:TPU:4 before, /device:TPU:1 now
where the time goes in v1:
time: 107 us; the launch traced here: 106 us
  Pallas kernels  43 us (40%)
  blocking collectives  32.6 us (30%)
  starting transfers between devices  17.5 us (16%)
  waiting for transfers between devices  7.26 us (7%)
  local copies, waits for them, and re-layouts  5.21 us (5%)
    pallas_call x1, Pallas kernels, per_device(): pl.pallas_call(functools.partial(forward_kernel, length), grid=(blocks, 2...  19.2 us
    all_to_all x1, blocking collectives, per_device(): terms = lax.all_to_all(spread, 'seq', 0, 0, tiled=True)  18.2 us
    pallas_call x1, Pallas kernels, per_device(): pl.pallas_call(functools.partial(backward_kernel, length), grid=(blocks,...  16.2 us
    all_to_all x1, blocking collectives, per_device(): lax.all_to_all(partial, 'fsdp', 0, 0, tiled=True)  14.4 us
    all_to_all x1, starting transfers between devices, per_device(): class_rows = lax.all_to_all(shard, 'fsdp', 0, 0, tiled=True)  8.58 us
    all_to_all x1, waiting for transfers between devices, per_device(): class_rows = lax.all_to_all(shard, 'fsdp', 0, 0, tiled=True)  7.24 us
    unnamed x31, local copies, waits for them, and re-layouts  5.2 us
    pallas_call x1, Pallas kernels, per_device(): pl.pallas_call(functools.partial(pack_kernel, length), in_specs=[raw] * 5...  3.37 us
  transfers between devices with their start and end apart: 5, of which 1 were waited for; matrix products, arithmetic and copies ran while one was open for 0% of the time, Pallas kernels for 2%

profile of v1, /device:TPU:1, one launch (start us, length us, event | category | flops | bytes accessed | tf_op | source)
XLA Modules:
  0.0 106.4 jit_solution(14457633755029376154)
XLA Ops:
  0.6 0.0 copy-start.5
  0.6 1.0 copy-done.5
  1.7 0.8 copy-done.9
  2.4 0.0 copy-start.8
  2.5 0.0 copy-start.11
  2.5 0.0 copy-start.13
  2.5 3.4 %pack.1 = (bf16[296,2048]{1,0:T(8,128)(2,1)}, bf16[296,2048]{1,0:T(8,128)(2,1)}, bf16[16,16,128]{2,1,0:T(8,128)(2,1)}, bf16[16,2048]{1,0:T(8,128)(2,1)S(1)}) custom-call(bf16[160,4096]{1,0:T(8,128)(2,1)} %bitcast.9, bf16[160,4096]{1,0:T(8,128)(2,1)} %bitcast.11, bf16[160,4096]{1,0:T(8,128)(2,1)} %bitcast.13, bf16[128,2048]{1,0:T(8,128)(2,1)S(1)} %copy-done.5, ...), custom_call_target="tpu_custom_call" | custom-call | tf_op jit(solution)/shard_map/pack/pallas_call | solution.py:381
  5.9 2.8 %collective-permute-start = (bf16[296,2048]{1,0:T(8,128)(2,1)}, bf16[296,2048]{1,0:T(8,128)(2,1)S(1)}, u32[]{:S(2)}, u32[]{:S(2)}) collective-permute-start(bf16[296,2048]{1,0:T(8,128)(2,1)} %get-tuple-element.22), channel_id=1, source_target_pairs={{0,16},{16,32},{32,48},{48,64},{64,80},{80,96},{96,112},{112,128},... | collective-permute-start | bytes 3637256 | tf_op jit(solution)/shard_map/ppermute | solution.py:398
  8.6 0.6 collective-permute-start.1
  9.3 8.6 %all-to-all-start = ((bf16[16,16,128]{2,1,0:T(8,128)(2,1)}), bf16[16,16,128]{2,1,0:T(8,128)(2,1)S(1)}, u32[]{:S(2)}, u32[]{:S(2)}) async-start(bf16[16,16,128]{2,1,0:T(8,128)(2,1)} %get-tuple-element.25), calls=%async_computation | async-start | bytes 131072 | tf_op jit(solution)/shard_map/all_to_all | solution.py:400
  17.9 0.0 copy-done.14
  17.9 0.1 copy.18.weight
  18.0 0.1 add_convert_fusion.inner
  18.1 7.2 %all-to-all-done.class_rows = bf16[16,16,128]{2,1,0:T(8,128)(2,1)S(1)} async-done(((bf16[16,16,128]{2,1,0:T(8,128)(2,1)}), bf16[16,16,128]{2,1,0:T(8,128)(2,1)S(1)}, u32[]{:S(2)}, u32[]{:S(2)}) %all-to-all-start) | async-done | bytes 65568 | tf_op jit(solution)/shard_map/all_to_all | solution.py:400
  25.3 0.0 collective-permute-done.left
  25.3 0.0 collective-permute-done.1.right
  25.3 0.0 copy-done.4
  25.3 0.0 copy-done.6
  25.4 0.0 copy-start.12
  25.4 19.2 %features_and_logits.1 = (bf16[160,4096]{1,0:T(8,128)(2,1)S(1)}, bf16[160,4096]{1,0:T(8,128)(2,1)S(1)}, bf16[160,4096]{1,0:T(8,128)(2,1)S(1)}, bf16[168,4096]{1,...) custom-call(s32[2]{0:T(128)S(1)} %add_convert_fusion.inner, bf16[160,4096]{1,0:T(8,128)(2,1)} %bitcast.10, ...), custom_call_target="tpu_custom_call" | custom-call | tf_op jit(solution)/shard_map/features_and_logits/pallas_call | solution.py:444
  44.6 1.1 %copy-done = bf16[168,4096]{1,0:T(8,128)(2,1)} copy-done((bf16[168,4096]{1,0:T(8,128)(2,1)}, bf16[168,4096]{1,0:T(8,128)(2,1)S(1)}, u32[]{:S(2)}) %copy-start) | copy-done | bytes 1376280
  45.7 2.3 %weight_partial_and_mix_grad.1 = (f32[16,8,128]{2,1,0:T(8,128)S(1)}, bf16[160,4096]{1,0:T(8,128)(2,1)S(1)}, bf16[160,4096]{1,0:T(8,128)(2,1)S(1)}, bf16[144,2048]{1,0:T(8,128)(2,1)S(1)}, bf16[144,2048]{1,0:T(8,128)(2,1)S(1)}) custom-call(bf16[160,4096]{1,0:T(8,128)(2,1)S(1)} %get-tuple-element.26.gate, bf16[160,4096]{1,0:T(8,128)(2,1)S(1)} %get-tuple-element.27.gated, ...), custom_call_target="tpu_custom_call" | custom-call | tf_op jit(solution)/shard_map/weight_partial_and_mix_grad/pallas_call | solution.py:470
  48.0 1.1 %copy-done.2 = bf16[160,4096]{1,0:T(8,128)(2,1)} copy-done((bf16[160,4096]{1,0:T(8,128)(2,1)}, bf16[160,4096]{1,0:T(8,128)(2,1)S(1)}, u32[]{:S(2)}) %copy-start.2) | copy-done | bytes 1310744
  49.1 1.1 %copy-done.3 = bf16[160,4096]{1,0:T(8,128)(2,1)} copy-done((bf16[160,4096]{1,0:T(8,128)(2,1)}, bf16[160,4096]{1,0:T(8,128)(2,1)S(1)}, u32[]{:S(2)}) %copy-start.3) | copy-done | bytes 1310744
  50.1 3.1 %collective-permute-start.2 = (bf16[144,2048]{1,0:T(8,128)(2,1)S(1)}, bf16[144,2048]{1,0:T(8,128)(2,1)S(1)}, u32[]{:S(2)}, u32[]{:S(2)}) collective-permute-start(bf16[144,2048]{1,0:T(8,128)(2,1)S(1)} %get-tuple-element.32), channel_id=1, source_target_pairs={{0,16},{16,32},{32,48},{48,64},{64,80},{80,96},{96,112},{112,128},... | collective-permute-start | bytes 1769480 | tf_op jit(solution)/shard_map/ppermute | solution.py:488
  53.2 2.4 %collective-permute-start.3 = (bf16[144,2048]{1,0:T(8,128)(2,1)S(1)}, bf16[144,2048]{1,0:T(8,128)(2,1)S(1)}, u32[]{:S(2)}, u32[]{:S(2)}) collective-permute-start(bf16[144,2048]{1,0:T(8,128)(2,1)S(1)} %get-tuple-element.33), channel_id=1, source_target_pairs={{16,0},{32,16},{48,32},{64,48},{80,64},{96,80},{112,96},{128,112},... | collective-permute-start | bytes 1769480 | tf_op jit(solution)/shard_map/ppermute | solution.py:489
  55.6 14.4 %all_to_all.15 = f32[16,8,128]{2,1,0:T(8,128)S(1)} all-to-all(f32[16,8,128]{2,1,0:T(8,128)S(1)} %get-tuple-element.39), channel_id=1, replica_groups=mesh['seq'=16,'fsdp'=16] {'fsdp'}, dimensions={0} | all-to-all | bytes 131072 | tf_op jit(solution)/shard_map/all_to_all | solution.py:512
  70.0 18.2 %all_to_all.16.terms = f32[16,8,128]{2,1,0:T(8,128)S(1)} all-to-all(f32[16,8,128]{2,1,0:T(8,128)S(1)} %broadcast_in_dim.15), channel_id=1, replica_groups=mesh['seq'=16,'fsdp'=16] {'seq'}, dimensions={0} | all-to-all | bytes 131072 | tf_op jit(solution)/shard_map/all_to_all | solution.py:514
  88.2 2.0 %final.1 = f32[128,2048]{1,0:T(8,128)} custom-call(f32[16,8,128]{2,1,0:T(8,128)S(1)} %all_to_all.16.terms, f32[4,2048]{1,0:T(4,128)S(1)} %copy-done.10), custom_call_target="tpu_custom_call" | custom-call | tf_op jit(solution)/shard_map/final/pallas_call | solution.py:515
  90.2 0.0 collective-permute-done.2.left
  90.2 0.0 collective-permute-done.3.right
  90.2 16.2 %gradients.1 = (bf16[160,4096]{1,0:T(8,128)(2,1)}, bf16[160,4096]{1,0:T(8,128)(2,1)}, bf16[160,4096]{1,0:T(8,128)(2,1)}) custom-call(s32[2]{0:T(128)S(1)} %add_convert_fusion.inner, bf16[160,4096]{1,0:T(8,128)(2,1)} %copy-done.2, bf16[160,4096]{1,0:T(8,128)(2,1)} %copy-done.3, bf16[144,2048]{1,0:T(8,128)(2,1)S(1)} %collective-permute-done.2.left, ...), custom_call_target="tpu_custom_call" | custom-call | tf_op jit(solution)/shard_map/gradients/pallas_call | solution.py:491
  (19 shorter events, 0.1 us)
Async XLA Ops:
  0.6 1.0 copy-start.5
  1.7 0.8 copy-start.9
  2.4 15.4 %copy-start.14 = (f32[7,3,2048]{2,0,1:T(8,128)S(1)}, f32[7,3,2048]{2,0,1:T(8,128)}, u32[]{:S(2)}) copy-start(f32[7,3,2048]{2,0,1:T(8,128)} %param.19) | copy-start | bytes 516100
  2.4 22.9 %copy-start.4 = (bf16[448,216]{1,0:T(8,128)(2,1)S(1)}, bf16[448,216]{1,0:T(8,128)(2,1)}, u32[]{:S(2)}) copy-start(bf16[448,216]{1,0:T(8,128)(2,1)} %constant.21.clone.analysis) | copy-start | bytes 580612
  2.4 22.9 %copy-start.6 = (bf16[176,224]{1,0:T(8,128)(2,1)S(1)}, bf16[176,224]{1,0:T(8,128)(2,1)}, u32[]{:S(2)}) copy-start(bf16[176,224]{1,0:T(8,128)(2,1)} %constant.23.clone.synth_a) | copy-start | bytes 236548
  2.4 22.9 %copy-start.7 = (bf16[176,224]{1,0:T(8,128)(2,1)S(1)}, bf16[176,224]{1,0:T(8,128)(2,1)}, u32[]{:S(2)}) copy-start(bf16[176,224]{1,0:T(8,128)(2,1)} %constant.22.clone.synth_c) | copy-start | bytes 236548
  2.4 22.9 %copy-start.8 = (bf16[128,128]{1,0:T(8,128)(2,1)S(1)}, bf16[128,128]{1,0:T(8,128)(2,1)}, u32[]{:S(2)}) copy-start(bf16[128,128]{1,0:T(8,128)(2,1)} %med.3) | copy-start | bytes 98308
  2.5 22.9 %copy-start.11 = (f32[2,16,128]{2,1,0:T(8,128)S(1)}, f32[2,16,128]{2,1,0:T(8,128)}, u32[]{:S(2)}) copy-start(f32[2,16,128]{2,1,0:T(8,128)} %constant.25.clone.fold) | copy-start | bytes 49156
  2.5 22.9 %copy-start.13 = (s32[1,160]{1,0:T(1,128)S(1)}, s32[1,160]{1,0:T(1,128)}, u32[]{:S(2)}) copy-start(s32[1,160]{1,0:T(1,128)} %target.1) | copy-start | bytes 1924
  5.9 19.5 %collective-permute-start = (bf16[296,2048]{1,0:T(8,128)(2,1)}, bf16[296,2048]{1,0:T(8,128)(2,1)S(1)}, u32[]{:S(2)}, u32[]{:S(2)}) collective-permute-start(bf16[296,2048]{1,0:T(8,128)(2,1)} %get-tuple-element.22), channel_id=1, source_target_pairs={{0,16},{16,32},{32,48},{48,64},{64,80},{80,96},{96,112},{112,128},... | collective-permute-start | bytes 3637256 | tf_op jit(solution)/shard_map/ppermute | solution.py:398
  8.6 16.7 %collective-permute-start.1 = (bf16[296,2048]{1,0:T(8,128)(2,1)}, bf16[296,2048]{1,0:T(8,128)(2,1)S(1)}, u32[]{:S(2)}, u32[]{:S(2)}) collective-permute-start(bf16[296,2048]{1,0:T(8,128)(2,1)} %get-tuple-element.23), channel_id=1, source_target_pairs={{16,0},{32,16},{48,32},{64,48},{80,64},{96,80},{112,96},{128,112},... | collective-permute-start | bytes 3637256 | tf_op jit(solution)/shard_map/ppermute | solution.py:399
  9.3 16.1 %all-to-all-start = ((bf16[16,16,128]{2,1,0:T(8,128)(2,1)}), bf16[16,16,128]{2,1,0:T(8,128)(2,1)S(1)}, u32[]{:S(2)}, u32[]{:S(2)}) async-start(bf16[16,16,128]{2,1,0:T(8,128)(2,1)} %get-tuple-element.25), calls=%async_computation | async-start | bytes 131072 | tf_op jit(solution)/shard_map/all_to_all | solution.py:400
  25.4 20.3 %copy-start.12 = (bf16[2,2,8,32]{3,2,1,0:T(8,128)(2,1)S(1)}, bf16[2,2,8,32]{3,2,1,0:T(8,128)(2,1)}, u32[]{:S(2)}) copy-start(bf16[2,2,8,32]{3,2,1,0:T(8,128)(2,1)} %constant.24.clone.place) | copy-start | bytes 6148
  44.6 1.1 %copy-start = (bf16[168,4096]{1,0:T(8,128)(2,1)}, bf16[168,4096]{1,0:T(8,128)(2,1)S(1)}, u32[]{:S(2)}) copy-start(bf16[168,4096]{1,0:T(8,128)(2,1)S(1)} %get-tuple-element.34.key_feat) | copy-start | bytes 4128772
  45.7 2.3 %copy-start.1 = (bf16[168,4096]{1,0:T(8,128)(2,1)}, bf16[168,4096]{1,0:T(8,128)(2,1)S(1)}, u32[]{:S(2)}) copy-start(bf16[168,4096]{1,0:T(8,128)(2,1)S(1)} %get-tuple-element.35.value_feat) | copy-start | bytes 4128772
  45.7 42.5 %copy-start.10 = (f32[4,2048]{1,0:T(4,128)S(1)}, f32[4,2048]{1,0:T(4,128)}, u32[]{:S(2)}) copy-start(f32[4,2048]{1,0:T(4,128)} %head.3) | copy-start | bytes 98308
  48.0 1.1 %copy-start.2 = (bf16[160,4096]{1,0:T(8,128)(2,1)}, bf16[160,4096]{1,0:T(8,128)(2,1)S(1)}, u32[]{:S(2)}) copy-start(bf16[160,4096]{1,0:T(8,128)(2,1)S(1)} %get-tuple-element.30.mix_grad) | copy-start | bytes 3932164
  49.1 1.1 %copy-start.3 = (bf16[160,4096]{1,0:T(8,128)(2,1)}, bf16[160,4096]{1,0:T(8,128)(2,1)S(1)}, u32[]{:S(2)}) copy-start(bf16[160,4096]{1,0:T(8,128)(2,1)S(1)} %get-tuple-element.31.gate_grad) | copy-start | bytes 3932164
  50.1 40.1 %collective-permute-start.2 = (bf16[144,2048]{1,0:T(8,128)(2,1)S(1)}, bf16[144,2048]{1,0:T(8,128)(2,1)S(1)}, u32[]{:S(2)}, u32[]{:S(2)}) collective-permute-start(bf16[144,2048]{1,0:T(8,128)(2,1)S(1)} %get-tuple-element.32), channel_id=1, source_target_pairs={{0,16},{16,32},{32,48},{48,64},{64,80},{80,96},{96,112},{112,128},... | collective-permute-start | bytes 1769480 | tf_op jit(solution)/shard_map/ppermute | solution.py:488
  53.2 37.0 %collective-permute-start.3 = (bf16[144,2048]{1,0:T(8,128)(2,1)S(1)}, bf16[144,2048]{1,0:T(8,128)(2,1)S(1)}, u32[]{:S(2)}, u32[]{:S(2)}) collective-permute-start(bf16[144,2048]{1,0:T(8,128)(2,1)S(1)} %get-tuple-element.33), channel_id=1, source_target_pairs={{16,0},{32,16},{48,32},{64,48},{80,64},{96,80},{112,96},{128,112},... | collective-permute-start | bytes 1769480 | tf_op jit(solution)/shard_map/ppermute | solution.py:489

commit v2 on v1

v2 whole, which is shorter than its diff:
```python
import functools

import jax
import jax.numpy as jnp
import ml_dtypes
import numpy as np
from jax import lax
from jax.experimental import pallas as pl
from jax.experimental.pallas import tpu as pltpu
from jax.sharding import PartitionSpec as P

loss_scale = 64.0
far = 136
near = 8
reach = 128
span = 296
window = 216
step = 80
keep = 88
lead = window - keep
freqs = 112
bins = 2 * freqs
columns = 1024
per_group = 16
parts = 16
lanes = 128
sub = 128
vmem_limit = 34 * 1024 * 1024


def split_np(table):
    upper = table.astype(ml_dtypes.bfloat16)
    lower = (table - upper.astype(np.float64)).astype(ml_dtypes.bfloat16)
    return upper, lower


def dft_tables():
    omega = 2.0 * np.pi * (np.arange(freqs) + 0.5) / bins
    rows = np.arange(window)
    angles = omega[:, None] * rows
    forward = np.concatenate([np.cos(angles), -np.sin(angles)])
    return forward, forward.T / freqs


def split_bf16(value):
    upper = value.astype(jnp.bfloat16)
    return upper, (value - upper.astype(jnp.float32)).astype(jnp.bfloat16)


def dot(left, right):
    return jnp.dot(left, right, preferred_element_type=jnp.float32)


def dot_t(left, right):
    return lax.dot_general(
        left, right, (((1,), (1,)), ((), ())), preferred_element_type=jnp.float32
    )


def dot_ta(left, right):
    return lax.dot_general(
        left, right, (((0,), (0,)), ((), ())), preferred_element_type=jnp.float32
    )


def taps(pieces, weight, member, start, count, sign):
    rows = jnp.concatenate([piece.astype(jnp.float32) for piece in pieces], axis=0)
    total = rows.shape[0]
    tap = [weight[offset, member : member + 1, :] for offset in range(7)]

    def moved(value, by):
        return pltpu.roll(value, (sign * by) % total, 0)

    one = moved(rows, 1)
    two = moved(rows, 2)
    tail = tap[4] * rows + tap[5] * one + tap[6] * two
    tail = tap[2] * rows + tap[3] * one + moved(tail, 2)
    tail = tap[0] * rows + tap[1] * one + moved(tail, 2)
    return tail[start : start + count]


def gains(med, analysis, block):
    groups = med.shape[1]
    channel = lax.broadcasted_iota(jnp.int32, (groups, columns), 1) + block * columns
    group = lax.broadcasted_iota(jnp.int32, (groups, columns), 0)
    expand = jnp.where(channel // per_group == group, 1.0, 0.0).astype(jnp.bfloat16)
    wide = dot(med, expand).astype(jnp.bfloat16)
    count = med.shape[0]
    both = dot(analysis[:, :count], wide)
    return both[:bins] + both[bins:]


def in_hbm(array):
    return pltpu.with_memory_space_constraint(array, pltpu.HBM)


def thirds(value):
    first, rest = split_bf16(value)
    second = (value - first.astype(jnp.float32)).astype(jnp.bfloat16)
    third = (value - first.astype(jnp.float32) - second.astype(jnp.float32)).astype(jnp.bfloat16)
    pieces = [piece.astype(jnp.float32) for piece in (first, second, third)]
    blank = jnp.zeros((parts - 12, value.shape[1]), jnp.float32)
    return jnp.concatenate(pieces + [blank], axis=0).astype(jnp.bfloat16)


def shard_kernel(out_weight, head, shard_out, head_out):
    coded = thirds(head[...])
    head_out[...] = coded
    found = dot_t(coded, out_weight[...])
    shard = thirds(found[0:4] + found[4:8] + found[8:12])
    for device in range(shard_out.shape[0]):
        shard_out[device] = shard


def local_kernel(
    length, q_edge, k, v, weight, key_out, value_out, products_out, to_right, to_left
):
    side = pl.program_id(1)

    def one(forward):
        sign = 1 if forward else -1
        for at in range(0, columns, sub):
            cols = slice(at, at + sub)
            taken = weight[:, :, cols]
            key_feat = taps((k[:, cols],), taken, 1, 0, length, sign)
            value_feat = taps((v[:, cols],), taken, 2, 0, length, sign)
            key_out[:, cols] = key_feat.astype(jnp.bfloat16)
            value_out[:, cols] = value_feat.astype(jnp.bfloat16)
            products_out[:, cols] = (key_feat * value_feat).astype(jnp.bfloat16)
        main, other = (to_right, to_left) if forward else (to_left, to_right)
        main_at = length - near if forward else 0
        other_at = 0 if forward else length - near
        first = length - reach if forward else 0
        main[0:reach, :] = products_out[first : first + reach, :]
        main[reach : reach + near, :] = q_edge[...]
        main[reach + near : reach + 2 * near, :] = k[main_at : main_at + near, :]
        main[reach + 2 * near : reach + 3 * near, :] = v[main_at : main_at + near, :]
        other[reach + 3 * near : reach + 4 * near, :] = k[other_at : other_at + near, :]
        other[reach + 4 * near : reach + 5 * near, :] = v[other_at : other_at + near, :]

    pl.when(side == 0)(functools.partial(one, True))
    pl.when(side == 1)(functools.partial(one, False))


def gate_kernel(length, q, s, weight, head_rows, gate_out, sums_out):
    block = pl.program_id(0)
    side = pl.program_id(1)

    def one(forward):
        for at in range(0, columns, sub):
            cols = slice(at, at + sub)
            gate = taps((q[:, cols],), weight[:, :, cols], 0, 0, length, 1 if forward else -1)
            gate_out[:, cols] = gate.astype(jnp.bfloat16)
        side_at = 0 if forward else 1
        term = dot_t(s[...], head_rows[...])

        @pl.when(block == 0)
        def _():
            sums_out[side_at] = term

        @pl.when(block > 0)
        def _():
            sums_out[side_at] += term

    pl.when(side == 0)(functools.partial(one, True))
    pl.when(side == 1)(functools.partial(one, False))


def class_block(class_rows):
    return jnp.concatenate([class_rows[piece] for piece in range(class_rows.shape[0])], axis=1)


def long_conv(rows_ref, spectrum, analysis, synthesis, causal):
    gain_re = spectrum[0:freqs, :]
    gain_im = spectrum[freqs:bins, :]
    if not causal:
        gain_im = -gain_im
    pieces = []
    for index in range(2):
        both = dot(analysis[...], rows_ref[index * step : index * step + window, :])
        re = both[:freqs] + both[bins : bins + freqs]
        im = both[freqs:bins] + both[bins + freqs :]
        mixed = jnp.concatenate([re * gain_re - im * gain_im, re * gain_im + im * gain_re], axis=0)
        high, low = split_bf16(mixed)
        both = dot(synthesis[...], high)
        piece = both[:keep] + both[keep:] + dot(synthesis[:keep], low)
        pieces.append(piece[:step] if index == 0 else piece)
    return jnp.concatenate(pieces, axis=0)


def kept(flag, piece):
    return jnp.where(flag, piece, jnp.zeros_like(piece))


def forward_kernel(
    length, inner, q_edge, k_low, k_high, v_low, v_high, local, first_gate, left, right, weight,
    class_rows, stream_sums, med, target, analysis, synth_c, synth_a, fold,
    gate_out, gated_out, mix_out, key_rim, value_rim, grad_out,
    products, spectrum, sums,
):
    block = pl.program_id(0)
    side = pl.program_id(1)

    @pl.when((block == 0) & (side == 0))
    def _():
        sums[...] = stream_sums[...]

    @pl.when(side == 0)
    def _():
        spectrum[...] = gains(med[...], analysis, block)

    def one(forward):
        main, other = (left, right) if forward else (right, left)
        left_flag, right_flag = inner[0] > 0, inner[1] > 0
        main_flag, other_flag = (left_flag, right_flag) if forward else (right_flag, left_flag)
        sign = 1 if forward else -1
        wide = jnp.float32

        def edges(low, high, member):
            at = reach + member * near
            beside_main = kept(main_flag, main[at : at + near, :].astype(wide))
            at = reach + (2 + member) * near
            beside_other = kept(other_flag, other[at : at + near, :].astype(wide))
            before, after = (
                (beside_main, beside_other) if forward else (beside_other, beside_main)
            )
            found = taps(
                (before, low[...], high[...], after), weight, member, 0, 4 * near, sign
            )
            if forward:
                return found[near : 2 * near], found[3 * near :]
            return found[2 * near : 3 * near], found[:near]

        key_fix, key_beyond = edges(k_low, k_high, 1)
        value_fix, value_beyond = edges(v_low, v_high, 2)
        key_rim[0:near, :] = key_fix.astype(jnp.bfloat16)
        key_rim[near:, :] = key_beyond.astype(jnp.bfloat16)
        value_rim[0:near, :] = value_fix.astype(jnp.bfloat16)
        value_rim[near:, :] = value_beyond.astype(jnp.bfloat16)
        halo = kept(main_flag, main[0:reach, :].astype(wide)).astype(jnp.bfloat16)
        fixed = (key_fix * value_fix).astype(jnp.bfloat16)
        beyond = (key_beyond * value_beyond).astype(jnp.bfloat16)
        q_near = kept(main_flag, main[reach : reach + near, :].astype(wide))
        if forward:
            products[0:reach, :] = halo
            products[reach : reach + near, :] = fixed
            products[reach + near : reach + length, :] = local[near:, :]
            products[reach + length :, :] = beyond
            gate = taps((q_near, q_edge[...]), weight, 0, near, near, sign)
            gate_out[0:near, :] = gate.astype(jnp.bfloat16)
            gate_out[near:, :] = first_gate[near:, :]
        else:
            products[0:near, :] = beyond
            products[near:length, :] = local[: length - near, :]
            products[length : length + near, :] = fixed
            products[length + near :, :] = halo
            gate = taps((q_edge[...], q_near), weight, 0, 0, near, sign)
            gate_out[0 : length - near, :] = first_gate[: length - near, :]
            gate_out[length - near :, :] = gate.astype(jnp.bfloat16)
        mix = long_conv(products, spectrum, analysis, synth_c if forward else synth_a, forward)
        mix = mix[:length] if forward else mix[near:]
        mix_out[...] = mix.astype(jnp.bfloat16)
        gated = (gate_out[...].astype(jnp.float32) * mix).astype(jnp.bfloat16)
        gated_out[...] = gated
        sums[0 if forward else 1] += dot_t(gated, class_block(class_rows))

    pl.when(side == 0)(functools.partial(one, True))
    pl.when(side == 1)(functools.partial(one, False))

    @pl.when((block == pl.num_programs(0) - 1) & (side == 1))
    def _():
        exact = lax.Precision.HIGHEST
        logits = jnp.dot(
            sums[0], fold[0], precision=exact, preferred_element_type=jnp.float32
        ) + jnp.dot(sums[1], fold[1], precision=exact, preferred_element_type=jnp.float32)
        logits = jnp.transpose(logits)[:8]
        row = lax.broadcasted_iota(jnp.int32, logits.shape, 0)
        valid = row < 4
        top = jnp.max(jnp.where(valid, logits, -jnp.inf), axis=0, keepdims=True)
        exponent = jnp.where(valid, jnp.exp(logits - top), 0.0)
        softmax_out = exponent / jnp.sum(exponent, axis=0, keepdims=True)
        one_hot = jnp.where(row == target[...], 1.0, 0.0)
        grad_out[...] = loss_scale * (softmax_out - one_hot)


def middle_kernel(
    length, gate, gated, mix, class_rows, grad, place,
    partial_out, mix_grad_out, gate_grad_out, to_left, to_right,
    turned, coded,
):
    block = pl.program_id(0)
    side = pl.program_id(1)

    @pl.when((block == 0) & (side == 0))
    def _():
        high, low = split_bf16(grad[...])
        for side_at in range(2):
            coded[side_at] = (
                dot_ta(high, place[side_at, 0]) + dot_ta(low, place[side_at, 1])
            ).astype(jnp.bfloat16)
        turned[0] = grad[...]
        for lane in range(4):
            turned[1, lane : lane + 1, :] = grad[3 - lane : 4 - lane, :]
        turned[1, 4:8, :] = jnp.zeros((4, length), jnp.float32)

    def one(forward):
        high, low = split_bf16(turned[0 if forward else 1])
        term = dot(high, gated[...]) + dot(low, gated[...])
        for piece in range(columns // lanes):
            cut = term[:, piece * lanes : piece * lanes + lanes]
            if forward:
                partial_out[piece] = cut
            else:
                partial_out[piece] += cut
        classes = class_block(class_rows)
        grads = dot(coded[0 if forward else 1], jnp.concatenate([classes, classes], axis=0))
        mix_grad = (grads * gate[...].astype(jnp.float32)).astype(jnp.bfloat16)
        gate_grad = (grads * mix[...].astype(jnp.float32)).astype(jnp.bfloat16)
        mix_grad_out[...] = mix_grad
        gate_grad_out[...] = gate_grad
        if forward:
            to_left[0:far, :] = mix_grad[:far]
            to_left[far:, :] = gate_grad[:near]
        else:
            to_right[0:far, :] = mix_grad[length - far :]
            to_right[far:, :] = gate_grad[length - near :]

    pl.when(side == 0)(functools.partial(one, True))
    pl.when(side == 1)(functools.partial(one, False))


def backward_kernel(
    length, forward, inner, mix_grad, gate_grad, halo, key_feat, value_feat, key_rim, value_rim,
    weight, med, analysis, synthesis, *rest,
):
    query_out, key_out, value_out, extended, spectrum = rest[-5:]
    spectrum[...] = gains(med[...], analysis, pl.program_id(0))
    flag = (inner[1] if forward else inner[0]) > 0
    start = 0 if forward else near
    sign = -1 if forward else 1
    far_rows = kept(flag, halo[0:far, :].astype(jnp.float32)).astype(jnp.bfloat16)
    if forward:
        extended[0:length, :] = mix_grad[...]
        extended[length:, :] = far_rows
    else:
        extended[0:far, :] = far_rows
        extended[far:, :] = mix_grad[...]
    for at in range(0, columns, sub):
        cols = slice(at, at + sub)
        rim = kept(flag, halo[far:, cols].astype(jnp.float32))
        pieces = (gate_grad[:, cols], rim) if forward else (rim, gate_grad[:, cols])
        query_out[:, cols] = taps(pieces, weight[:, :, cols], 0, start, length, sign).astype(
            jnp.bfloat16
        )
    back = long_conv(extended, spectrum, analysis, synthesis, not forward)
    for at in range(0, columns, sub):
        cols = slice(at, at + sub)
        for member, feat, edge, out in (
            (1, value_feat, value_rim, key_out),
            (2, key_feat, key_rim, value_out),
        ):
            fix, beyond = edge[0:near, cols], edge[near:, cols]
            if forward:
                pieces = (fix, feat[near:, cols], beyond)
            else:
                pieces = (beyond, feat[: length - near, cols], fix)
            joined = jnp.concatenate([piece.astype(jnp.float32) for piece in pieces], axis=0)
            out[:, cols] = taps(
                (back[:, cols] * joined,), weight[:, :, cols], member, start, length, sign
            ).astype(jnp.bfloat16)


def final_kernel(terms, head, out):
    total = jnp.sum(terms[...], axis=0)
    out[...] = lax.dot_general(
        total[:4],
        head[...] * (1.0 / loss_scale),
        (((0,), (0,)), ((), ())),
        precision=lax.Precision.HIGHEST,
        preferred_element_type=jnp.float32,
    )


def per_device(query, key, value, stream, targets, short_filter, med_filter, out_weight, head):
    length = query.shape[1]
    channels = query.shape[2]
    half = channels // 2
    blocks = half // columns
    count = lax.axis_size("seq")
    owners = lax.axis_size("fsdp")
    own = half // owners
    rightward = [(i, (i + 1) % count) for i in range(count)]
    leftward = [((i + 1) % count, i) for i in range(count)]
    query, key, value, stream = query[0], key[0], value[0], stream[0]
    bf16, f32 = jnp.bfloat16, jnp.float32
    packed = reach + 5 * near
    shape = jax.ShapeDtypeStruct
    whole = pl.BlockSpec(memory_space=pltpu.VMEM)
    scalars = pl.BlockSpec(memory_space=pltpu.SMEM)
    untouched = pl.BlockSpec(memory_space=pl.ANY)
    query, key, value, stream = in_hbm(query), in_hbm(key), in_hbm(value), in_hbm(stream)
    limit = pltpu.CompilerParams(vmem_limit_bytes=vmem_limit)
    params = pltpu.CompilerParams(
        dimension_semantics=("arbitrary", "arbitrary"), vmem_limit_bytes=vmem_limit
    )

    def full(array):
        rank = len(array.shape)
        return pl.BlockSpec(array.shape, lambda *_: (0,) * rank)

    def by_channel(rows):
        return pl.BlockSpec((rows, columns), lambda b, s: (0, s * blocks + b))

    def edge_rows(first, last):
        return pl.BlockSpec(
            (near, columns), lambda b, s: (first + (last - first) * s, s * blocks + b)
        )

    def by_half(rows):
        return pl.BlockSpec((rows, columns), lambda b, s: (0, b))

    def by_owner(rows):
        return pl.BlockSpec((columns // lanes, rows, lanes), lambda b, s: (b, 0, 0))

    weight_spec = pl.BlockSpec(short_filter.shape[:2] + (columns,), lambda b, s: (0, 0, b))
    end = length // near - 1
    local_rows = shape((length, channels), bf16)

    key_feat, value_feat, products, to_right, to_left = pl.pallas_call(
        functools.partial(local_kernel, length),
        grid=(blocks, 2),
        in_specs=[edge_rows(end, 0), by_channel(length), by_channel(length), weight_spec],
        out_specs=[by_channel(length)] * 3 + [by_half(packed)] * 2,
        out_shape=[local_rows] * 3 + [shape((packed, half), bf16)] * 2,
        compiler_params=params,
        name="local_features",
    )(query, key, value, short_filter)

    from_left = lax.ppermute(to_right, "seq", rightward)
    from_right = lax.ppermute(to_left, "seq", leftward)

    shard, head_rows = pl.pallas_call(
        shard_kernel,
        in_specs=[whole] * 2,
        out_specs=[whole] * 2,
        out_shape=[shape((owners, parts, own), bf16), shape((parts, half), bf16)],
        compiler_params=limit,
        name="shard",
    )(out_weight, head)
    class_rows = lax.all_to_all(shard, "fsdp", 0, 0, tiled=True)
    if own != lanes:
        class_rows = class_rows.reshape(owners, parts, -1, lanes).transpose(0, 2, 1, 3)
        class_rows = class_rows.reshape(-1, parts, lanes)

    sums_shape = shape((2, length, parts), f32)
    first_gate, stream_sums = pl.pallas_call(
        functools.partial(gate_kernel, length),
        grid=(blocks, 2),
        in_specs=[by_channel(length)] * 2 + [weight_spec, by_half(parts)],
        out_specs=[by_channel(length), full(sums_shape)],
        out_shape=[local_rows, sums_shape],
        compiler_params=params,
        name="gate_and_stream_logits",
    )(query, stream, short_filter, head_rows)

    position = lax.axis_index("seq")
    inner = jnp.stack([position > 0, position < count - 1]).astype(jnp.int32)

    forward, inverse = dft_tables()
    analysis = jnp.asarray(np.concatenate(split_np(forward)))
    synth_c = jnp.asarray(np.concatenate(split_np(inverse[lead:])))
    synth_a = jnp.asarray(np.concatenate(split_np(inverse[:keep])))

    fold = np.zeros((2, parts, 128), np.float32)
    place = np.zeros((2, 2, 8, 2 * parts), np.float32)
    for lane in range(4):
        for part in range(3):
            fold[0, 4 * part + lane, lane] = 1.0
            fold[1, 4 * part + 3 - lane, lane] = 1.0
            for level in range(2):
                place[0, level, lane, level * parts + 4 * part + lane] = 1.0
                place[1, level, 3 - lane, level * parts + 4 * part + lane] = 1.0
    place = jnp.asarray(place.astype(ml_dtypes.bfloat16))

    grad_shape = shape((8, length), f32)
    gate, gated, mix, key_rim, value_rim, grad = pl.pallas_call(
        functools.partial(forward_kernel, length),
        grid=(blocks, 2),
        in_specs=[scalars, edge_rows(0, end)]
        + [edge_rows(0, 0), edge_rows(end, end)] * 2
        + [by_channel(length)] * 2
        + [by_half(packed)] * 2
        + [
            weight_spec, by_owner(parts), full(sums_shape), full(med_filter), full(targets),
            full(analysis), full(synth_c), full(synth_a), full(fold),
        ],
        out_specs=[by_channel(length)] * 3 + [by_channel(2 * near)] * 2 + [full(grad_shape)],
        out_shape=[local_rows] * 3 + [shape((2 * near, channels), bf16)] * 2 + [grad_shape],
        scratch_shapes=[
            pltpu.VMEM((span, columns), bf16),
            pltpu.VMEM((bins, columns), f32),
            pltpu.VMEM((2, length, parts), f32),
        ],
        compiler_params=params,
        name="mix_and_logits",
    )(
        inner, query, key, key, value, value, products, first_gate, from_left, from_right,
        short_filter, class_rows, stream_sums, med_filter, targets, analysis, synth_c, synth_a,
        jnp.asarray(fold),
    )

    partial, mix_grad, gate_grad, to_left, to_right = pl.pallas_call(
        functools.partial(middle_kernel, length),
        grid=(blocks, 2),
        in_specs=[by_channel(length)] * 3 + [by_owner(parts), full(grad), full(place)],
        out_specs=[by_owner(8)] + [by_channel(length)] * 2 + [by_half(far + near)] * 2,
        out_shape=[shape((half // lanes, 8, lanes), f32)]
        + [shape((length, channels), bf16)] * 2
        + [shape((far + near, half), bf16)] * 2,
        scratch_shapes=[
            pltpu.VMEM((2, 8, length), f32),
            pltpu.VMEM((2, length, 2 * parts), bf16),
        ],
        compiler_params=params,
        name="weight_partial_and_mix_grad",
    )(gate, gated, mix, class_rows, grad, place)

    grad_left = lax.ppermute(to_right, "seq", rightward)
    grad_right = lax.ppermute(to_left, "seq", leftward)
    if own != lanes:
        partial = partial.reshape(owners, -1, 8, lanes).transpose(0, 2, 1, 3)
        partial = partial.reshape(owners, 8, own)
    by_genome = lax.all_to_all(partial, "fsdp", 0, 0, tiled=True)

    def gradients(forward, mix_grad, halo, synthesis, earlier):
        base = 0 if forward else blocks

        def by_channel(rows):
            return pl.BlockSpec((rows, columns), lambda b: (0, base + b))

        in_specs = (
            [scalars]
            + [by_channel(length)] * 2
            + [pl.BlockSpec((far + near, columns), lambda b: (0, b))]
            + [by_channel(length)] * 2
            + [by_channel(2 * near)] * 2
            + [
                pl.BlockSpec(short_filter.shape[:2] + (columns,), lambda b: (0, 0, b)),
                full(med_filter), full(analysis), full(synthesis),
            ]
            + [untouched] * len(earlier)
        )
        taken = len(in_specs) - len(earlier)
        return pl.pallas_call(
            functools.partial(backward_kernel, length, forward),
            grid=(blocks,),
            in_specs=in_specs,
            out_specs=[by_channel(length)] * 3,
            out_shape=[local_rows] * 3,
            scratch_shapes=[pltpu.VMEM((span, columns), bf16), pltpu.VMEM((bins, columns), f32)],
            input_output_aliases={taken + at: at for at in range(len(earlier))},
            compiler_params=pltpu.CompilerParams(
                dimension_semantics=("arbitrary",), vmem_limit_bytes=vmem_limit
            ),
            name="gradients_forward" if forward else "gradients_reverse",
        )(
            inner, in_hbm(mix_grad), in_hbm(gate_grad), halo, in_hbm(key_feat),
            in_hbm(value_feat), key_rim, value_rim, short_filter, med_filter, analysis,
            synthesis, *earlier,
        )

    grads = gradients(True, mix_grad, grad_right, synth_a, ())
    by_genome, grads = lax.optimization_barrier((by_genome, tuple(grads)))
    over_genomes = jnp.sum(by_genome, axis=0)
    spread = jnp.broadcast_to(over_genomes, (count,) + over_genomes.shape)
    spread, mix_grad = lax.optimization_barrier((spread, mix_grad))
    terms = lax.all_to_all(spread, "seq", 0, 0, tiled=True)
    grads = gradients(False, mix_grad, grad_left, synth_c, grads)
    terms, grads = lax.optimization_barrier((terms, tuple(grads)))
    query_grad, key_grad, value_grad = grads
    out_grad = pl.pallas_call(
        final_kernel,
        in_specs=[whole] * 2,
        out_specs=whole,
        out_shape=shape((own, half), f32),
        compiler_params=limit,
        name="final",
    )(terms, head)
    return query_grad[None], key_grad[None], value_grad[None], out_grad


def solution(mesh):
    rows = P("fsdp", "seq", None)
    placed = (rows, rows, rows, rows, P("fsdp", "seq"), P(), P(), P("fsdp", None), P())
    return jax.shard_map(
        per_device,
        mesh=mesh,
        in_specs=placed,
        out_specs=(rows, rows, rows, P("fsdp", None)),
        check_vma=False,
    )
```

time: 107 us -> 89.6 us (0.84)
  blocking collectives: 32.6 us -> 0 us
  starting transfers between devices: 17.5 us -> 31.7 us
  waiting for transfers between devices: 7.26 us -> 1.75 us
  local copies, waits for them, and re-layouts: 5.21 us -> 8.53 us
  Pallas kernels: 43 us -> 46.1 us
    all_to_all x2 -> x0, blocking collectives: 32.6 us -> none  [the longest x1 18.2 us: per_device(): terms = lax.all_to_all(spread, 'seq', 0, 0, tiled=True)]
    all_to_all x0 -> x2, starting transfers between devices: none -> 14.2 us  [the longest x1 9.12 us: per_device(): terms = lax.all_to_all(spread, 'seq', 0, 0, tiled=True)]
    pallas_call x2 -> x5, Pallas kernels: 19.5 us -> 31.9 us  [the longest x2 18.3 us: gradients(): pl.pallas_call(functools.partial(backward_kernel, length, forward), grid=...]
    pallas_call x1, Pallas kernels: 19.2 us -> 9.41 us  [per_device(): pl.pallas_call(functools.partial(forward_kernel, length), grid=(blocks, 2...]
    all_to_all x1, waiting for transfers between devices: 7.24 us -> 1.66 us  [per_device(): class_rows = lax.all_to_all(shard, 'fsdp', 0, 0, tiled=True)]
    ppermute x1, starting transfers between devices: 2.42 us -> 5.63 us  [per_device(): grad_right = lax.ppermute(to_left, 'seq', leftward)]
    ppermute x1, starting transfers between devices: 3.08 us -> 0.01 us  [per_device(): grad_left = lax.ppermute(to_right, 'seq', rightward)]
    unnamed x31 -> x35, local copies, waits for them, and re-layouts: 5.2 us -> 7.89 us
  transfers between devices with their start and end apart: 5 -> 7, of which waited for: 1 -> 2; matrix products, arithmetic and copies ran while one was open for 0% -> 1% of each run, Pallas kernels for 2% -> 27%
where the time goes in v2:
time: 89.6 us; the launch traced here: 89 us
  Pallas kernels  46.1 us (51%)
  starting transfers between devices  31.7 us (35%)
  local copies, waits for them, and re-layouts  8.53 us (10%)
  waiting for transfers between devices  1.75 us (2%)
    pallas_call x2, Pallas kernels, gradients(): pl.pallas_call(functools.partial(backward_kernel, length, forward), grid=...  18.3 us
    pallas_call x1, Pallas kernels, per_device(): pl.pallas_call(functools.partial(forward_kernel, length), grid=(blocks, 2...  9.41 us
    all_to_all x1, starting transfers between devices, per_device(): terms = lax.all_to_all(spread, 'seq', 0, 0, tiled=True)  9.12 us
    all_to_all x1, starting transfers between devices, per_device(): class_rows = lax.all_to_all(shard, 'fsdp', 0, 0, tiled=True)  8.67 us
    unnamed x35, local copies, waits for them, and re-layouts  7.89 us
    pallas_call x1, Pallas kernels, per_device(): pl.pallas_call(functools.partial(local_kernel, length), grid=(blocks, 2),...  7.8 us
    ppermute x1, starting transfers between devices, per_device(): grad_right = lax.ppermute(to_left, 'seq', leftward)  5.63 us
    all_to_all x1, starting transfers between devices, per_device(): by_genome = lax.all_to_all(partial, 'fsdp', 0, 0, tiled=True)  5.04 us
  transfers between devices with their start and end apart: 7, of which 2 were waited for; matrix products, arithmetic and copies ran while one was open for 1% of the time, Pallas kernels for 27%

profile of v2, /device:TPU:1, one launch (start us, length us, event | category | flops | bytes accessed | tf_op | source)
XLA Modules:
  0.0 89.0 jit_solution(1147380066886268598)
XLA Ops:
  0.6 1.0 %copy.21.weight = f32[7,3,2048]{2,1,0:T(4,128)S(1)} copy(f32[7,3,2048]{2,0,1:T(8,128)} %param.19) | data formatting | bytes 344064 | tf_op args[5]
  1.7 0.0 copy-start.12
  1.7 7.8 %local_features.1 = (bf16[160,4096]{1,0:T(8,128)(2,1)S(1)}, bf16[160,4096]{1,0:T(8,128)(2,1)S(1)}, bf16[160,4096]{1,0:T(8,128)(2,1)S(1)}, bf16[168,2048]{1,0:T(8,128)(2,1)}, bf16[168,2048]{1,0:T(8,128)(2,1)}) custom-call(bf16[160,4096]{1,0:T(8,128)(2,1)} %bitcast.15, bf16[160,4096]{1,0:T(8,128)(2,1)} %bitcast.9, bf16[160,4096]{1,0:T(8,128)(2,1)} %bitcast.12, ...), custom_call_target="tpu_custom_call" | custom-call | tf_op jit(solution)/shard_map/local_features/pallas_call | solution.py:429
  9.5 1.1 %copy-done = bf16[160,4096]{1,0:T(8,128)(2,1)} copy-done((bf16[160,4096]{1,0:T(8,128)(2,1)}, bf16[160,4096]{1,0:T(8,128)(2,1)S(1)}, u32[]{:S(2)}) %copy-start) | copy-done | bytes 1310744
  10.6 1.1 %copy-done.1 = bf16[160,4096]{1,0:T(8,128)(2,1)} copy-done((bf16[160,4096]{1,0:T(8,128)(2,1)}, bf16[160,4096]{1,0:T(8,128)(2,1)S(1)}, u32[]{:S(2)}) %copy-start.1) | copy-done | bytes 1310744
  11.7 2.7 %collective-permute-start = (bf16[168,2048]{1,0:T(8,128)(2,1)}, bf16[168,2048]{1,0:T(8,128)(2,1)}, u32[]{:S(2)}, u32[]{:S(2)}) collective-permute-start(bf16[168,2048]{1,0:T(8,128)(2,1)} %get-tuple-element.43), channel_id=1, source_target_pairs={{0,16},{16,32},{32,48},{48,64},{64,80},{80,96},{96,112},{112,128},... | collective-permute-start | bytes 2064392 | tf_op jit(solution)/shard_map/ppermute | solution.py:439
  14.3 0.6 collective-permute-start.1
  14.9 0.9 %shard.1 = (bf16[16,16,128]{2,1,0:T(8,128)(2,1)}, bf16[16,2048]{1,0:T(8,128)(2,1)S(1)}) custom-call(bf16[128,2048]{1,0:T(8,128)(2,1)S(1)} %copy-done.5, f32[4,2048]{1,0:T(4,128)S(1)} %copy-done.12), custom_call_target="tpu_custom_call" | custom-call | tf_op jit(solution)/shard_map/shard/pallas_call | solution.py:442
  15.8 8.7 %all-to-all-start = ((bf16[16,16,128]{2,1,0:T(8,128)(2,1)}), bf16[16,16,128]{2,1,0:T(8,128)(2,1)S(1)}, u32[]{:S(2)}, u32[]{:S(2)}) async-start(bf16[16,16,128]{2,1,0:T(8,128)(2,1)} %get-tuple-element.45), calls=%async_computation | async-start | bytes 131072 | tf_op jit(solution)/shard_map/all_to_all | solution.py:450
  24.5 0.0 copy-start.4
  24.5 0.0 copy-start.6
  24.5 0.0 copy-start.14
  24.5 4.9 %gate_and_stream_logits.1 = (bf16[160,4096]{1,0:T(8,128)(2,1)S(1)}, f32[2,160,16]{2,1,0:T(8,128)S(1)}) custom-call(bf16[160,4096]{1,0:T(8,128)(2,1)} %bitcast.16, bf16[160,4096]{1,0:T(8,128)(2,1)} %bitcast.21, f32[7,3,2048]{2,1,0:T(4,128)S(1)} %copy.21.weight, bf16[16,2048]{1,0:T(8,128)(2,1)S(1)} %get-tuple-element.41.head_rows), custom_call_target="tpu_custom_call" | custom-call | tf_op jit(solution)/shard_map/gate_and_stream_logits/pallas_call | solution.py:456
  29.5 0.7 copy-done.10
  30.1 0.1 add_convert_fusion.inner
  30.2 1.7 %all-to-all-done.class_rows = bf16[16,16,128]{2,1,0:T(8,128)(2,1)S(1)} async-done(((bf16[16,16,128]{2,1,0:T(8,128)(2,1)}), bf16[16,16,128]{2,1,0:T(8,128)(2,1)S(1)}, u32[]{:S(2)}, u32[]{:S(2)}) %all-to-all-start) | async-done | bytes 65568 | tf_op jit(solution)/shard_map/all_to_all | solution.py:450
  31.9 0.0 copy-start.7
  31.9 0.9 copy-done.7
  32.8 0.9 %copy-done.11 = f32[2,160,16]{2,1,0:T(8,128)S(1)} copy-done((f32[2,160,16]{2,1,0:T(8,128)S(1)}, f32[2,160,16]{2,1,0:T(8,128)}, u32[]{:S(2)}) %copy-start.11) | copy-done | bytes 20504
  33.7 9.4 %mix_and_logits.1 = (bf16[160,4096]{1,0:T(8,128)(2,1)S(1)}, bf16[160,4096]{1,0:T(8,128)(2,1)S(1)}, bf16[160,4096]{1,0:T(8,128)(2,1)S(1)}, bf16[16,4096]{1,0:T(8,...) custom-call(s32[2]{0:T(128)S(1)} %add_convert_fusion.inner, bf16[160,4096]{1,0:T(8,128)(2,1)} %bitcast.17, ...), custom_call_target="tpu_custom_call" | custom-call | tf_op jit(solution)/shard_map/mix_and_logits/pallas_call | solution.py:486
  43.1 0.0 copy-start.8
  43.1 2.8 %weight_partial_and_mix_grad.1 = (f32[16,8,128]{2,1,0:T(8,128)}, bf16[160,4096]{1,0:T(8,128)(2,1)S(1)}, bf16[160,4096]{1,0:T(8,128)(2,1)S(1)}, bf16[144,2048]{1,0:T(8,128)(2,1)S(1)}, bf16[144,2048]{1,0:T(8,128)(2,1)S(1)}) custom-call(bf16[160,4096]{1,0:T(8,128)(2,1)S(1)} %get-tuple-element.47.gate, bf16[160,4096]{1,0:T(8,128)(2,1)S(1)} %get-tuple-element.48.gated, ...), custom_call_target="tpu_custom_call" | custom-call | tf_op jit(solution)/shard_map/weight_partial_and_mix_grad/pallas_call | solution.py:512
  46.0 1.1 %copy-done.2 = bf16[160,4096]{1,0:T(8,128)(2,1)} copy-done((bf16[160,4096]{1,0:T(8,128)(2,1)}, bf16[160,4096]{1,0:T(8,128)(2,1)S(1)}, u32[]{:S(2)}) %copy-start.2) | copy-done | bytes 1310744
  47.1 1.1 %copy-done.3 = bf16[160,4096]{1,0:T(8,128)(2,1)} copy-done((bf16[160,4096]{1,0:T(8,128)(2,1)}, bf16[160,4096]{1,0:T(8,128)(2,1)S(1)}, u32[]{:S(2)}) %copy-start.3) | copy-done | bytes 1310744
  48.2 5.6 %collective-permute-start.2 = (bf16[144,2048]{1,0:T(8,128)(2,1)S(1)}, bf16[144,2048]{1,0:T(8,128)(2,1)S(1)}, u32[]{:S(2)}, u32[]{:S(2)}) collective-permute-start(bf16[144,2048]{1,0:T(8,128)(2,1)S(1)} %get-tuple-element.54), channel_id=1, source_target_pairs={{16,0},{32,16},{48,32},{64,48},{80,64},{96,80},{112,96},{128,112},... | collective-permute-start | bytes 1769480 | tf_op jit(solution)/shard_map/ppermute | solution.py:529
  53.8 5.0 %all-to-all-start.1 = ((f32[16,8,128]{2,1,0:T(8,128)}), f32[16,8,128]{2,1,0:T(8,128)S(1)}, u32[]{:S(2)}, u32[]{:S(2)}) async-start(f32[16,8,128]{2,1,0:T(8,128)} %get-tuple-element.51), calls=%async_computation.1 | async-start | bytes 131072 | tf_op jit(solution)/shard_map/all_to_all | solution.py:533
  58.8 0.1 collective-permute-done.2.halo
  58.9 9.3 %gradients_forward.1 = (bf16[160,4096]{1,0:T(8,128)(2,1)}, bf16[160,4096]{1,0:T(8,128)(2,1)}, bf16[160,4096]{1,0:T(8,128)(2,1)}) custom-call(s32[2]{0:T(128)S(1)} %add_convert_fusion.inner, bf16[160,4096]{1,0:T(8,128)(2,1)} %copy-done.2, bf16[160,4096]{1,0:T(8,128)(2,1)} %copy-done.3, bf16[144,2048]{1,0:T(8,128)(2,1)S(1)} %collective-permute-done.2.halo, ...), custom_call_target="tpu_custom_call" | custom-call | tf_op jit(solution)/shard_map/gradients_forward/pallas_call | solution.py:554
  68.3 0.6 broadcast_in_dim.12
  68.9 9.1 %all-to-all-start.2 = ((f32[16,8,128]{2,1,0:T(8,128)}), f32[16,8,128]{2,1,0:T(8,128)S(1)}, u32[]{:S(2)}, u32[]{:S(2)}) async-start(f32[16,8,128]{2,1,0:T(8,128)} %broadcast_in_dim.12), calls=%async_computation.2 | async-start | bytes 131072 | tf_op jit(solution)/shard_map/all_to_all | solution.py:577
  78.0 9.0 %gradients_reverse.1 = (bf16[160,4096]{1,0:T(8,128)(2,1)}, bf16[160,4096]{1,0:T(8,128)(2,1)}, bf16[160,4096]{1,0:T(8,128)(2,1)}) custom-call(s32[2]{0:T(128)S(1)} %add_convert_fusion.inner, bf16[160,4096]{1,0:T(8,128)(2,1)} %copy-done.2, bf16[160,4096]{1,0:T(8,128)(2,1)} %copy-done.3, ...), custom_call_target="tpu_custom_call", output_to_operand_aliasing={{0}: (12, {}), {1}: (13, {}), {2}: (14, {})} | custom-call | tf_op jit(solution)/shard_map/gradients_reverse/pallas_call | solution.py:554
  87.0 2.0 %final.1 = f32[128,2048]{1,0:T(8,128)} custom-call(f32[16,8,128]{2,1,0:T(8,128)S(1)} %all-to-all-done.2.terms, f32[4,2048]{1,0:T(4,128)S(1)} %copy-done.13), custom_call_target="tpu_custom_call" | custom-call | tf_op jit(solution)/shard_map/final/pallas_call | solution.py:581
  (28 shorter events, 0.1 us)
Async XLA Ops:
  1.7 13.2 %copy-start.5 = (bf16[128,2048]{1,0:T(8,128)(2,1)S(1)}, bf16[128,2048]{1,0:T(8,128)(2,1)}, u32[]{:S(2)}) copy-start(bf16[128,2048]{1,0:T(8,128)(2,1)} %out_weight.1) | copy-start | bytes 1572868
  1.7 13.2 %copy-start.12 = (f32[4,2048]{1,0:T(4,128)S(1)}, f32[4,2048]{1,0:T(4,128)}, u32[]{:S(2)}) copy-start(f32[4,2048]{1,0:T(4,128)} %head.3) | copy-start | bytes 98308
  9.5 1.1 %copy-start = (bf16[160,4096]{1,0:T(8,128)(2,1)}, bf16[160,4096]{1,0:T(8,128)(2,1)S(1)}, u32[]{:S(2)}) copy-start(bf16[160,4096]{1,0:T(8,128)(2,1)S(1)} %get-tuple-element.55.key_feat) | copy-start | bytes 3932164
  10.6 1.1 %copy-start.1 = (bf16[160,4096]{1,0:T(8,128)(2,1)}, bf16[160,4096]{1,0:T(8,128)(2,1)S(1)}, u32[]{:S(2)}) copy-start(bf16[160,4096]{1,0:T(8,128)(2,1)S(1)} %get-tuple-element.56.value_feat) | copy-start | bytes 3932164
  11.7 20.2 %collective-permute-start = (bf16[168,2048]{1,0:T(8,128)(2,1)}, bf16[168,2048]{1,0:T(8,128)(2,1)}, u32[]{:S(2)}, u32[]{:S(2)}) collective-permute-start(bf16[168,2048]{1,0:T(8,128)(2,1)} %get-tuple-element.43), channel_id=1, source_target_pairs={{0,16},{16,32},{32,48},{48,64},{64,80},{80,96},{96,112},{112,128},... | collective-permute-start | bytes 2064392 | tf_op jit(solution)/shard_map/ppermute | solution.py:439
  14.3 17.5 %collective-permute-start.1 = (bf16[168,2048]{1,0:T(8,128)(2,1)}, bf16[168,2048]{1,0:T(8,128)(2,1)}, u32[]{:S(2)}, u32[]{:S(2)}) collective-permute-start(bf16[168,2048]{1,0:T(8,128)(2,1)} %get-tuple-element.44), channel_id=1, source_target_pairs={{16,0},{32,16},{48,32},{64,48},{80,64},{96,80},{112,96},{128,112},... | collective-permute-start | bytes 2064392 | tf_op jit(solution)/shard_map/ppermute | solution.py:440
  15.8 16.0 %all-to-all-start = ((bf16[16,16,128]{2,1,0:T(8,128)(2,1)}), bf16[16,16,128]{2,1,0:T(8,128)(2,1)S(1)}, u32[]{:S(2)}, u32[]{:S(2)}) async-start(bf16[16,16,128]{2,1,0:T(8,128)(2,1)} %get-tuple-element.45), calls=%async_computation | async-start | bytes 131072 | tf_op jit(solution)/shard_map/all_to_all | solution.py:450
  24.5 7.4 %copy-start.4 = (bf16[448,216]{1,0:T(8,128)(2,1)S(1)}, bf16[448,216]{1,0:T(8,128)(2,1)}, u32[]{:S(2)}) copy-start(bf16[448,216]{1,0:T(8,128)(2,1)} %constant.21.clone.analysis) | copy-start | bytes 580612
  24.5 7.4 %copy-start.6 = (bf16[176,224]{1,0:T(8,128)(2,1)S(1)}, bf16[176,224]{1,0:T(8,128)(2,1)}, u32[]{:S(2)}) copy-start(bf16[176,224]{1,0:T(8,128)(2,1)} %constant.22.clone.synth_c.synthesis) | copy-start | bytes 236548
  24.5 7.4 %copy-start.9 = (bf16[128,128]{1,0:T(8,128)(2,1)S(1)}, bf16[128,128]{1,0:T(8,128)(2,1)}, u32[]{:S(2)}) copy-start(bf16[128,128]{1,0:T(8,128)(2,1)} %med.5) | copy-start | bytes 98308
  24.5 7.4 %copy-start.14 = (f32[2,16,128]{2,1,0:T(8,128)S(1)}, f32[2,16,128]{2,1,0:T(8,128)}, u32[]{:S(2)}) copy-start(f32[2,16,128]{2,1,0:T(8,128)} %constant.25.clone.fold) | copy-start | bytes 49156
  24.5 7.4 %copy-start.16 = (s32[1,160]{1,0:T(1,128)S(1)}, s32[1,160]{1,0:T(1,128)}, u32[]{:S(2)}) copy-start(s32[1,160]{1,0:T(1,128)} %target.1) | copy-start | bytes 1924
  29.4 0.7 copy-start.10
  31.9 0.9 %copy-start.7 = (bf16[176,224]{1,0:T(8,128)(2,1)S(1)}, bf16[176,224]{1,0:T(8,128)(2,1)}, u32[]{:S(2)}) copy-start(bf16[176,224]{1,0:T(8,128)(2,1)} %constant.23.clone.synth_a.synthesis) | copy-start | bytes 236548
  32.8 0.9 %copy-start.11 = (f32[2,160,16]{2,1,0:T(8,128)S(1)}, f32[2,160,16]{2,1,0:T(8,128)}, u32[]{:S(2)}) copy-start(f32[2,160,16]{2,1,0:T(8,128)} %copy-done.10) | copy-start | bytes 61444
  33.7 9.4 %copy-start.15 = (bf16[2,2,8,32]{3,2,1,0:T(8,128)(2,1)S(1)}, bf16[2,2,8,32]{3,2,1,0:T(8,128)(2,1)}, u32[]{:S(2)}) copy-start(bf16[2,2,8,32]{3,2,1,0:T(8,128)(2,1)} %constant.24.clone.place) | copy-start | bytes 6148
  43.1 15.8 %copy-start.8 = (bf16[176,224]{1,0:T(8,128)(2,1)S(1)}, bf16[176,224]{1,0:T(8,128)(2,1)}, u32[]{:S(2)}) copy-start(bf16[176,224]{1,0:T(8,128)(2,1)} %constant.23.clone.synth_a.synthesis) | copy-start | bytes 236548
  46.0 1.1 %copy-start.2 = (bf16[160,4096]{1,0:T(8,128)(2,1)}, bf16[160,4096]{1,0:T(8,128)(2,1)S(1)}, u32[]{:S(2)}) copy-start(bf16[160,4096]{1,0:T(8,128)(2,1)S(1)} %get-tuple-element.64.mix_grad) | copy-start | bytes 3932164
  47.1 1.1 %copy-start.3 = (bf16[160,4096]{1,0:T(8,128)(2,1)}, bf16[160,4096]{1,0:T(8,128)(2,1)S(1)}, u32[]{:S(2)}) copy-start(bf16[160,4096]{1,0:T(8,128)(2,1)S(1)} %get-tuple-element.53.gate_grad) | copy-start | bytes 3932164
  48.2 10.8 %collective-permute-start.2 = (bf16[144,2048]{1,0:T(8,128)(2,1)S(1)}, bf16[144,2048]{1,0:T(8,128)(2,1)S(1)}, u32[]{:S(2)}, u32[]{:S(2)}) collective-permute-start(bf16[144,2048]{1,0:T(8,128)(2,1)S(1)} %get-tuple-element.54), channel_id=1, source_target_pairs={{16,0},{32,16},{48,32},{64,48},{80,64},{96,80},{112,96},{128,112},... | collective-permute-start | bytes 1769480 | tf_op jit(solution)/shard_map/ppermute | solution.py:529
  53.8 24.2 %collective-permute-start.3 = (bf16[144,2048]{1,0:T(8,128)(2,1)S(1)}, bf16[144,2048]{1,0:T(8,128)(2,1)S(1)}, u32[]{:S(2)}, u32[]{:S(2)}) collective-permute-start(bf16[144,2048]{1,0:T(8,128)(2,1)S(1)} %get-tuple-element.65), channel_id=1, source_target_pairs={{0,16},{16,32},{32,48},{48,64},{64,80},{80,96},{96,112},{112,128},... | collective-permute-start | bytes 1769480 | tf_op jit(solution)/shard_map/ppermute | solution.py:528
  53.8 14.4 %all-to-all-start.1 = ((f32[16,8,128]{2,1,0:T(8,128)}), f32[16,8,128]{2,1,0:T(8,128)S(1)}, u32[]{:S(2)}, u32[]{:S(2)}) async-start(f32[16,8,128]{2,1,0:T(8,128)} %get-tuple-element.51), calls=%async_computation.1 | async-start | bytes 131072 | tf_op jit(solution)/shard_map/all_to_all | solution.py:533
  68.9 18.1 %all-to-all-start.2 = ((f32[16,8,128]{2,1,0:T(8,128)}), f32[16,8,128]{2,1,0:T(8,128)S(1)}, u32[]{:S(2)}, u32[]{:S(2)}) async-start(f32[16,8,128]{2,1,0:T(8,128)} %broadcast_in_dim.12), calls=%async_computation.2 | async-start | bytes 131072 | tf_op jit(solution)/shard_map/all_to_all | solution.py:577
  78.0 9.0 %copy-start.13 = (f32[4,2048]{1,0:T(4,128)S(1)}, f32[4,2048]{1,0:T(4,128)}, u32[]{:S(2)}) copy-start(f32[4,2048]{1,0:T(4,128)} %head.3) | copy-start | bytes 98308

commit v3 on v2

--- a/solution.py
+++ b/solution.py
@@ -66,7 +66,7 @@
 def taps(pieces, weight, member, start, count, sign):
     rows = jnp.concatenate([piece.astype(jnp.float32) for piece in pieces], axis=0)
     total = rows.shape[0]
-    tap = [weight[offset, member : member + 1, :] for offset in range(7)]
+    tap = [weight[member, offset : offset + 1, :] for offset in range(7)]
 
     def moved(value, by):
         return pltpu.roll(value, (sign * by) % total, 0)
@@ -392,13 +392,14 @@
     rightward = [(i, (i + 1) % count) for i in range(count)]
     leftward = [((i + 1) % count, i) for i in range(count)]
     query, key, value, stream = query[0], key[0], value[0], stream[0]
+    short_filter = short_filter.transpose(1, 0, 2)
     bf16, f32 = jnp.bfloat16, jnp.float32
     packed = reach + 5 * near
     shape = jax.ShapeDtypeStruct
     whole = pl.BlockSpec(memory_space=pltpu.VMEM)
     scalars = pl.BlockSpec(memory_space=pltpu.SMEM)
     untouched = pl.BlockSpec(memory_space=pl.ANY)
-    query, key, value, stream = in_hbm(query), in_hbm(key), in_hbm(value), in_hbm(stream)
+    query, key, value = in_hbm(query), in_hbm(key), in_hbm(value)
     limit = pltpu.CompilerParams(vmem_limit_bytes=vmem_limit)
     params = pltpu.CompilerParams(
         dimension_semantics=("arbitrary", "arbitrary"), vmem_limit_bytes=vmem_limit
@@ -425,19 +426,7 @@
     weight_spec = pl.BlockSpec(short_filter.shape[:2] + (columns,), lambda b, s: (0, 0, b))
     end = length // near - 1
     local_rows = shape((length, channels), bf16)
-
-    key_feat, value_feat, products, to_right, to_left = pl.pallas_call(
-        functools.partial(local_kernel, length),
-        grid=(blocks, 2),
-        in_specs=[edge_rows(end, 0), by_channel(length), by_channel(length), weight_spec],
-        out_specs=[by_channel(length)] * 3 + [by_half(packed)] * 2,
-        out_shape=[local_rows] * 3 + [shape((packed, half), bf16)] * 2,
-        compiler_params=params,
-        name="local_features",
-    )(query, key, value, short_filter)
-
-    from_left = lax.ppermute(to_right, "seq", rightward)
-    from_right = lax.ppermute(to_left, "seq", leftward)
+    hbm_rows = pltpu.HBM((length, channels), bf16)
 
     shard, head_rows = pl.pallas_call(
         shard_kernel,
@@ -447,10 +436,25 @@
         compiler_params=limit,
         name="shard",
     )(out_weight, head)
+    shard, key = lax.optimization_barrier((shard, key))
     class_rows = lax.all_to_all(shard, "fsdp", 0, 0, tiled=True)
     if own != lanes:
         class_rows = class_rows.reshape(owners, parts, -1, lanes).transpose(0, 2, 1, 3)
         class_rows = class_rows.reshape(-1, parts, lanes)
+
+    key_feat, value_feat, products, to_right, to_left = pl.pallas_call(
+        functools.partial(local_kernel, length),
+        grid=(blocks, 2),
+        in_specs=[edge_rows(end, 0), by_channel(length), by_channel(length), weight_spec],
+        out_specs=[by_channel(length)] * 3 + [by_half(packed)] * 2,
+        out_shape=[hbm_rows] * 2 + [local_rows] + [shape((packed, half), bf16)] * 2,
+        compiler_params=params,
+        name="local_features",
+    )(query, key, value, short_filter)
+
+    class_rows, to_right, to_left = lax.optimization_barrier((class_rows, to_right, to_left))
+    from_left = lax.ppermute(to_right, "seq", rightward)
+    from_right = lax.ppermute(to_left, "seq", leftward)
 
     sums_shape = shape((2, length, parts), f32)
     first_gate, stream_sums = pl.pallas_call(
@@ -461,7 +465,7 @@
         out_shape=[local_rows, sums_shape],
         compiler_params=params,
         name="gate_and_stream_logits",
-    )(query, stream, short_filter, head_rows)
+    )(query, in_hbm(stream), short_filter, head_rows)
 
     position = lax.axis_index("seq")
     inner = jnp.stack([position > 0, position < count - 1]).astype(jnp.int32)
@@ -515,7 +519,7 @@
         in_specs=[by_channel(length)] * 3 + [by_owner(parts), full(grad), full(place)],
         out_specs=[by_owner(8)] + [by_channel(length)] * 2 + [by_half(far + near)] * 2,
         out_shape=[shape((half // lanes, 8, lanes), f32)]
-        + [shape((length, channels), bf16)] * 2
+        + [hbm_rows] * 2
         + [shape((far + near, half), bf16)] * 2,
         scratch_shapes=[
             pltpu.VMEM((2, 8, length), f32),

time: 89.6 us -> 92.6 us (1.033)
  local copies, waits for them, and re-layouts: 8.53 us -> 4.26 us
  waiting for transfers between devices: 1.75 us -> 5.82 us
  starting transfers between devices: 31.7 us -> 34.8 us
    unnamed x35 -> x30, local copies, waits for them, and re-layouts: 7.89 us -> 3.62 us
    all_to_all x1, starting transfers between devices: 9.12 us -> 12.6 us  [per_device(): terms = lax.all_to_all(spread, 'seq', 0, 0, tiled=True)]
    ppermute x1, starting transfers between devices: 5.63 us -> 2.15 us  [per_device(): grad_right = lax.ppermute(to_left, 'seq', leftward)]
    ppermute x1, waiting for transfers between devices: 0.01 us -> 3.13 us  [per_device(): from_left = lax.ppermute(to_right, 'seq', rightward)]
    all_to_all x1, starting transfers between devices: 5.04 us -> 7.86 us  [per_device(): by_genome = lax.all_to_all(partial, 'fsdp', 0, 0, tiled=True)]
    ppermute x1, waiting for transfers between devices: 0.01 us -> 2.67 us  [per_device(): from_right = lax.ppermute(to_left, 'seq', leftward)]
    all_to_all x1, waiting for transfers between devices: 1.66 us -> 0.01 us  [per_device(): class_rows = lax.all_to_all(shard, 'fsdp', 0, 0, tiled=True)]
    all_to_all x1, starting transfers between devices: 8.67 us -> 10 us  [per_device(): class_rows = lax.all_to_all(shard, 'fsdp', 0, 0, tiled=True)]
  transfers between devices with their start and end apart: 7 -> 7, of which waited for: 2 -> 2; matrix products, arithmetic and copies ran while one was open for 1% -> 1% of each run, Pallas kernels for 27% -> 33%
where the time goes in v3:
time: 92.6 us; the launch traced here: 92 us
  Pallas kernels  46.2 us (50%)
  starting transfers between devices  34.8 us (38%)
  waiting for transfers between devices  5.82 us (6%)
  local copies, waits for them, and re-layouts  4.26 us (5%)
    pallas_call x2, Pallas kernels, gradients(): pl.pallas_call(functools.partial(backward_kernel, length, forward), grid=...  18.3 us
    all_to_all x1, starting transfers between devices, per_device(): terms = lax.all_to_all(spread, 'seq', 0, 0, tiled=True)  12.6 us
    all_to_all x1, starting transfers between devices, per_device(): class_rows = lax.all_to_all(shard, 'fsdp', 0, 0, tiled=True)  10 us
    pallas_call x1, Pallas kernels, per_device(): pl.pallas_call(functools.partial(forward_kernel, length), grid=(blocks, 2...  9.15 us
    all_to_all x1, starting transfers between devices, per_device(): by_genome = lax.all_to_all(partial, 'fsdp', 0, 0, tiled=True)  7.86 us
    pallas_call x1, Pallas kernels, per_device(): pl.pallas_call(functools.partial(local_kernel, length), grid=(blocks, 2),...  7.65 us
    pallas_call x1, Pallas kernels, per_device(): pl.pallas_call(functools.partial(gate_kernel, length), grid=(blocks, 2),...  4.91 us
    unnamed x30, local copies, waits for them, and re-layouts  3.62 us
  transfers between devices with their start and end apart: 7, of which 2 were waited for; matrix products, arithmetic and copies ran while one was open for 1% of the time, Pallas kernels for 33%

profile of v3, /device:TPU:1, one launch (start us, length us, event | category | flops | bytes accessed | tf_op | source)
XLA Modules:
  0.0 92.0 jit_solution(2141347138171570445)
XLA Ops:
  0.6 1.0 %copy-done.3 = bf16[128,2048]{1,0:T(8,128)(2,1)S(1)} copy-done((bf16[128,2048]{1,0:T(8,128)(2,1)S(1)}, bf16[128,2048]{1,0:T(8,128)(2,1)}, u32[]{:S(2)}) %copy-start.3) | copy-done | bytes 524312
  1.7 0.8 copy-done.9
  2.4 0.9 shard.1
  3.3 10.0 %all-to-all-start = ((bf16[16,16,128]{2,1,0:T(8,128)(2,1)}), bf16[16,16,128]{2,1,0:T(8,128)(2,1)S(1)}, u32[]{:S(2)}, u32[]{:S(2)}) async-start(bf16[16,16,128]{2,1,0:T(8,128)(2,1)} %get-tuple-element.50), calls=%async_computation | async-start | bytes 131072 | tf_op jit(solution)/shard_map/all_to_all | solution.py:440
  13.4 0.0 copy-start
  13.4 0.9 copy-done
  14.3 7.7 %local_features.1 = (bf16[160,4096]{1,0:T(8,128)(2,1)}, bf16[160,4096]{1,0:T(8,128)(2,1)}, bf16[160,4096]{1,0:T(8,128)(2,1)S(1)}, bf16[168,2048]{1,0:T(8,128)(2,1)}, bf16[168,2048]{1,0:T(8,128)(2,1)S(1)}) custom-call(bf16[160,4096]{1,0:T(8,128)(2,1)} %bitcast.21, bf16[160,4096]{1,0:T(8,128)(2,1)} %bitcast.15, bf16[160,4096]{1,0:T(8,128)(2,1)} %bitcast.18, ...), custom_call_target="tpu_custom_call" | custom-call | tf_op jit(solution)/shard_map/local_features/pallas_call | solution.py:445
  22.0 0.8 copy-done.14
  22.8 0.0 all-to-all-done.class_rows
  22.8 2.1 %collective-permute-start = (bf16[168,2048]{1,0:T(8,128)(2,1)}, bf16[168,2048]{1,0:T(8,128)(2,1)S(1)}, u32[]{:S(2)}, u32[]{:S(2)}) collective-permute-start(bf16[168,2048]{1,0:T(8,128)(2,1)} %get-tuple-element.53), channel_id=1, source_target_pairs={{0,16},{16,32},{32,48},{48,64},{64,80},{80,96},{96,112},{112,128},... | collective-permute-start | bytes 2064392 | tf_op jit(solution)/shard_map/ppermute | solution.py:456
  25.0 0.0 copy-start.5
  25.0 0.0 copy-start.7
  25.0 0.0 copy-start.11
  25.0 0.0 copy-start.13
  25.0 4.9 %gate_and_stream_logits.1 = (bf16[160,4096]{1,0:T(8,128)(2,1)S(1)}, f32[2,160,16]{2,1,0:T(8,128)S(1)}) custom-call(bf16[160,4096]{1,0:T(8,128)(2,1)} %bitcast.22, bf16[160,4096]{1,0:T(8,128)(2,1)} %bitcast.27, f32[3,7,2048]{2,1,0:T(8,128)S(1)} %bitcast.11, bf16[16,2048]{1,0:T(8,128)(2,1)S(1)} %get-tuple-element.48.head_rows), custom_call_target="tpu_custom_call" | custom-call | tf_op jit(solution)/shard_map/gate_and_stream_logits/pallas_call | solution.py:460
  29.9 0.1 add_convert_fusion.inner
  30.0 3.1 %collective-permute-done.left = bf16[168,2048]{1,0:T(8,128)(2,1)S(1)} collective-permute-done((bf16[168,2048]{1,0:T(8,128)(2,1)}, bf16[168,2048]{1,0:T(8,128)(2,1)S(1)}, u32[]{:S(2)}, u32[]{:S(2)}) %collective-permute-start) | collective-permute-done | bytes 688160 | tf_op jit(solution)/shard_map/ppermute | solution.py:456
  33.2 2.7 %collective-permute-done.1.right = bf16[168,2048]{1,0:T(8,128)(2,1)S(1)} collective-permute-done((bf16[168,2048]{1,0:T(8,128)(2,1)}, bf16[168,2048]{1,0:T(8,128)(2,1)S(1)}, u32[]{:S(2)}, u32[]{:S(2)}) %collective-permute-start.1) | collective-permute-done | bytes 688160 | tf_op jit(solution)/shard_map/ppermute | solution.py:457
  35.9 0.0 copy-start.12
  35.9 9.1 %mix_and_logits.1 = (bf16[160,4096]{1,0:T(8,128)(2,1)S(1)}, bf16[160,4096]{1,0:T(8,128)(2,1)S(1)}, bf16[160,4096]{1,0:T(8,128)(2,1)S(1)}, bf16[16,4096]{1,0:T(8,...) custom-call(s32[2]{0:T(128)S(1)} %add_convert_fusion.inner, bf16[160,4096]{1,0:T(8,128)(2,1)} %bitcast.23, ...), custom_call_target="tpu_custom_call" | custom-call | tf_op jit(solution)/shard_map/mix_and_logits/pallas_call | solution.py:490
  45.0 0.0 copy-start.6
  45.1 0.0 copy-start.8
  45.1 3.3 %weight_partial_and_mix_grad.1 = (f32[16,8,128]{2,1,0:T(8,128)}, bf16[160,4096]{1,0:T(8,128)(2,1)}, bf16[160,4096]{1,0:T(8,128)(2,1)}, bf16[144,2048]{1,0:T(8,128)(2,1)S(1)}, bf16[144,2048]{1,0:T(8,128)(2,1)S(1)}) custom-call(bf16[160,4096]{1,0:T(8,128)(2,1)S(1)} %get-tuple-element.57.gate, bf16[160,4096]{1,0:T(8,128)(2,1)S(1)} %get-tuple-element.58.gated, ...), custom_call_target="tpu_custom_call" | custom-call | tf_op jit(solution)/shard_map/weight_partial_and_mix_grad/pallas_call | solution.py:516
  48.4 2.1 %collective-permute-start.2 = (bf16[144,2048]{1,0:T(8,128)(2,1)S(1)}, bf16[144,2048]{1,0:T(8,128)(2,1)S(1)}, u32[]{:S(2)}, u32[]{:S(2)}) collective-permute-start(bf16[144,2048]{1,0:T(8,128)(2,1)S(1)} %get-tuple-element.64), channel_id=1, source_target_pairs={{16,0},{32,16},{48,32},{64,48},{80,64},{96,80},{112,96},{128,112},... | collective-permute-start | bytes 1769480 | tf_op jit(solution)/shard_map/ppermute | solution.py:533
  50.5 0.0 collective-permute-start.3
  50.5 7.9 %all-to-all-start.1 = ((f32[16,8,128]{2,1,0:T(8,128)}), f32[16,8,128]{2,1,0:T(8,128)S(1)}, u32[]{:S(2)}, u32[]{:S(2)}) async-start(f32[16,8,128]{2,1,0:T(8,128)} %get-tuple-element.61), calls=%async_computation.1 | async-start | bytes 131072 | tf_op jit(solution)/shard_map/all_to_all | solution.py:537
  58.4 0.0 collective-permute-done.2.halo
  58.4 9.3 %gradients_forward.1 = (bf16[160,4096]{1,0:T(8,128)(2,1)}, bf16[160,4096]{1,0:T(8,128)(2,1)}, bf16[160,4096]{1,0:T(8,128)(2,1)}) custom-call(s32[2]{0:T(128)S(1)} %add_convert_fusion.inner, bf16[160,4096]{1,0:T(8,128)(2,1)} %get-tuple-element.74.mix_grad, bf16[160,4096]{1,0:T(8,128)(2,1)} %get-tuple-element.63.gate_grad, ...), custom_call_target="tpu_custom_call" | custom-call | tf_op jit(solution)/shard_map/gradients_forward/pallas_call | solution.py:558
  67.8 0.6 broadcast_in_dim.12
  68.4 12.6 %all-to-all-start.2 = ((f32[16,8,128]{2,1,0:T(8,128)}), f32[16,8,128]{2,1,0:T(8,128)S(1)}, u32[]{:S(2)}, u32[]{:S(2)}) async-start(f32[16,8,128]{2,1,0:T(8,128)} %broadcast_in_dim.12), calls=%async_computation.2 | async-start | bytes 131072 | tf_op jit(solution)/shard_map/all_to_all | solution.py:581
  81.0 8.9 %gradients_reverse.1 = (bf16[160,4096]{1,0:T(8,128)(2,1)}, bf16[160,4096]{1,0:T(8,128)(2,1)}, bf16[160,4096]{1,0:T(8,128)(2,1)}) custom-call(s32[2]{0:T(128)S(1)} %add_convert_fusion.inner, bf16[160,4096]{1,0:T(8,128)(2,1)} %get-tuple-element.74.mix_grad, ...), custom_call_target="tpu_custom_call", output_to_operand_aliasing={{0}: (12, {}), {1}: (13, {}), {2}: (14, {})} | custom-call | tf_op jit(solution)/shard_map/gradients_reverse/pallas_call | solution.py:558
  90.0 2.0 %final.1 = f32[128,2048]{1,0:T(8,128)} custom-call(f32[16,8,128]{2,1,0:T(8,128)S(1)} %all-to-all-done.2.terms, f32[4,2048]{1,0:T(4,128)S(1)} %copy-done.10), custom_call_target="tpu_custom_call" | custom-call | tf_op jit(solution)/shard_map/final/pallas_call | solution.py:585
  (23 shorter events, 0.1 us)
Async XLA Ops:
  0.6 1.0 %copy-start.3 = (bf16[128,2048]{1,0:T(8,128)(2,1)S(1)}, bf16[128,2048]{1,0:T(8,128)(2,1)}, u32[]{:S(2)}) copy-start(bf16[128,2048]{1,0:T(8,128)(2,1)} %out_weight.1) | copy-start | bytes 1572868
  1.7 0.8 copy-start.9
  3.3 19.5 %all-to-all-start = ((bf16[16,16,128]{2,1,0:T(8,128)(2,1)}), bf16[16,16,128]{2,1,0:T(8,128)(2,1)S(1)}, u32[]{:S(2)}, u32[]{:S(2)}) async-start(bf16[16,16,128]{2,1,0:T(8,128)(2,1)} %get-tuple-element.50), calls=%async_computation | async-start | bytes 131072 | tf_op jit(solution)/shard_map/all_to_all | solution.py:440
  13.4 0.9 %copy-start = (f32[7,3,2048]{2,0,1:T(8,128)S(1)}, f32[7,3,2048]{2,0,1:T(8,128)}, u32[]{:S(2)}) copy-start(f32[7,3,2048]{2,0,1:T(8,128)} %param.19) | copy-start | bytes 516100
  14.3 10.7 %copy-start.1 = (f32[7,3,2048]{2,0,1:T(8,128)S(1)}, f32[7,3,2048]{2,0,1:T(8,128)}, u32[]{:S(2)}) copy-start(f32[7,3,2048]{2,0,1:T(8,128)} %param.19) | copy-start | bytes 516100
  22.0 0.8 copy-start.14
  22.8 10.3 %collective-permute-start = (bf16[168,2048]{1,0:T(8,128)(2,1)}, bf16[168,2048]{1,0:T(8,128)(2,1)S(1)}, u32[]{:S(2)}, u32[]{:S(2)}) collective-permute-start(bf16[168,2048]{1,0:T(8,128)(2,1)} %get-tuple-element.53), channel_id=1, source_target_pairs={{0,16},{16,32},{32,48},{48,64},{64,80},{80,96},{96,112},{112,128},... | collective-permute-start | bytes 2064392 | tf_op jit(solution)/shard_map/ppermute | solution.py:456
  25.0 10.9 %collective-permute-start.1 = (bf16[168,2048]{1,0:T(8,128)(2,1)}, bf16[168,2048]{1,0:T(8,128)(2,1)S(1)}, u32[]{:S(2)}, u32[]{:S(2)}) collective-permute-start(bf16[168,2048]{1,0:T(8,128)(2,1)} %copy-done.14), channel_id=1, source_target_pairs={{16,0},{32,16},{48,32},{64,48},{80,64},{96,80},{112,96},{128,112},... | collective-permute-start | bytes 2064392 | tf_op jit(solution)/shard_map/ppermute | solution.py:457
  25.0 10.9 %copy-start.2 = (bf16[448,216]{1,0:T(8,128)(2,1)S(1)}, bf16[448,216]{1,0:T(8,128)(2,1)}, u32[]{:S(2)}) copy-start(bf16[448,216]{1,0:T(8,128)(2,1)} %constant.21.clone.analysis) | copy-start | bytes 580612
  25.0 10.9 %copy-start.4 = (bf16[176,224]{1,0:T(8,128)(2,1)S(1)}, bf16[176,224]{1,0:T(8,128)(2,1)}, u32[]{:S(2)}) copy-start(bf16[176,224]{1,0:T(8,128)(2,1)} %constant.22.clone.synth_c.synthesis) | copy-start | bytes 236548
  25.0 10.9 %copy-start.5 = (bf16[176,224]{1,0:T(8,128)(2,1)S(1)}, bf16[176,224]{1,0:T(8,128)(2,1)}, u32[]{:S(2)}) copy-start(bf16[176,224]{1,0:T(8,128)(2,1)} %constant.23.clone.synth_a.synthesis) | copy-start | bytes 236548
  25.0 10.9 %copy-start.7 = (bf16[128,128]{1,0:T(8,128)(2,1)S(1)}, bf16[128,128]{1,0:T(8,128)(2,1)}, u32[]{:S(2)}) copy-start(bf16[128,128]{1,0:T(8,128)(2,1)} %med.5) | copy-start | bytes 98308
  25.0 10.8 %copy-start.11 = (f32[2,16,128]{2,1,0:T(8,128)S(1)}, f32[2,16,128]{2,1,0:T(8,128)}, u32[]{:S(2)}) copy-start(f32[2,16,128]{2,1,0:T(8,128)} %constant.25.clone.fold) | copy-start | bytes 49156
  25.0 10.8 %copy-start.13 = (s32[1,160]{1,0:T(1,128)S(1)}, s32[1,160]{1,0:T(1,128)}, u32[]{:S(2)}) copy-start(s32[1,160]{1,0:T(1,128)} %target.1) | copy-start | bytes 1924
  35.9 9.2 %copy-start.12 = (bf16[2,2,8,32]{3,2,1,0:T(8,128)(2,1)S(1)}, bf16[2,2,8,32]{3,2,1,0:T(8,128)(2,1)}, u32[]{:S(2)}) copy-start(bf16[2,2,8,32]{3,2,1,0:T(8,128)(2,1)} %constant.24.clone.place) | copy-start | bytes 6148
  45.0 13.3 %copy-start.6 = (bf16[176,224]{1,0:T(8,128)(2,1)S(1)}, bf16[176,224]{1,0:T(8,128)(2,1)}, u32[]{:S(2)}) copy-start(bf16[176,224]{1,0:T(8,128)(2,1)} %constant.23.clone.synth_a.synthesis) | copy-start | bytes 236548
  45.1 13.3 %copy-start.8 = (bf16[128,128]{1,0:T(8,128)(2,1)S(1)}, bf16[128,128]{1,0:T(8,128)(2,1)}, u32[]{:S(2)}) copy-start(bf16[128,128]{1,0:T(8,128)(2,1)} %med.5) | copy-start | bytes 98308
  48.4 10.0 %collective-permute-start.2 = (bf16[144,2048]{1,0:T(8,128)(2,1)S(1)}, bf16[144,2048]{1,0:T(8,128)(2,1)S(1)}, u32[]{:S(2)}, u32[]{:S(2)}) collective-permute-start(bf16[144,2048]{1,0:T(8,128)(2,1)S(1)} %get-tuple-element.64), channel_id=1, source_target_pairs={{16,0},{32,16},{48,32},{64,48},{80,64},{96,80},{112,96},{128,112},... | collective-permute-start | bytes 1769480 | tf_op jit(solution)/shard_map/ppermute | solution.py:533
  50.5 30.5 %collective-permute-start.3 = (bf16[144,2048]{1,0:T(8,128)(2,1)S(1)}, bf16[144,2048]{1,0:T(8,128)(2,1)S(1)}, u32[]{:S(2)}, u32[]{:S(2)}) collective-permute-start(bf16[144,2048]{1,0:T(8,128)(2,1)S(1)} %get-tuple-element.75), channel_id=1, source_target_pairs={{0,16},{16,32},{32,48},{48,64},{64,80},{80,96},{96,112},{112,128},... | collective-permute-start | bytes 1769480 | tf_op jit(solution)/shard_map/ppermute | solution.py:532
  50.5 17.2 %all-to-all-start.1 = ((f32[16,8,128]{2,1,0:T(8,128)}), f32[16,8,128]{2,1,0:T(8,128)S(1)}, u32[]{:S(2)}, u32[]{:S(2)}) async-start(f32[16,8,128]{2,1,0:T(8,128)} %get-tuple-element.61), calls=%async_computation.1 | async-start | bytes 131072 | tf_op jit(solution)/shard_map/all_to_all | solution.py:537
  68.4 21.6 %all-to-all-start.2 = ((f32[16,8,128]{2,1,0:T(8,128)}), f32[16,8,128]{2,1,0:T(8,128)S(1)}, u32[]{:S(2)}, u32[]{:S(2)}) async-start(f32[16,8,128]{2,1,0:T(8,128)} %broadcast_in_dim.12), calls=%async_computation.2 | async-start | bytes 131072 | tf_op jit(solution)/shard_map/all_to_all | solution.py:581
  81.0 9.0 %copy-start.10 = (f32[4,2048]{1,0:T(4,128)S(1)}, f32[4,2048]{1,0:T(4,128)}, u32[]{:S(2)}) copy-start(f32[4,2048]{1,0:T(4,128)} %head.3) | copy-start | bytes 98308

commit v4 on v2

--- a/solution.py
+++ b/solution.py
@@ -66,7 +66,7 @@
 def taps(pieces, weight, member, start, count, sign):
     rows = jnp.concatenate([piece.astype(jnp.float32) for piece in pieces], axis=0)
     total = rows.shape[0]
-    tap = [weight[offset, member : member + 1, :] for offset in range(7)]
+    tap = [weight[member, offset : offset + 1, :] for offset in range(7)]
 
     def moved(value, by):
         return pltpu.roll(value, (sign * by) % total, 0)
@@ -181,9 +181,8 @@
         re = both[:freqs] + both[bins : bins + freqs]
         im = both[freqs:bins] + both[bins + freqs :]
         mixed = jnp.concatenate([re * gain_re - im * gain_im, re * gain_im + im * gain_re], axis=0)
-        high, low = split_bf16(mixed)
-        both = dot(synthesis[...], high)
-        piece = both[:keep] + both[keep:] + dot(synthesis[:keep], low)
+        both = dot(synthesis[...], mixed.astype(jnp.bfloat16))
+        piece = both[:keep] + both[keep:]
         pieces.append(piece[:step] if index == 0 else piece)
     return jnp.concatenate(pieces, axis=0)
 
@@ -392,6 +391,8 @@
     rightward = [(i, (i + 1) % count) for i in range(count)]
     leftward = [((i + 1) % count, i) for i in range(count)]
     query, key, value, stream = query[0], key[0], value[0], stream[0]
+    short_filter = in_hbm(short_filter.transpose(1, 0, 2))
+    med_filter = in_hbm(med_filter)
     bf16, f32 = jnp.bfloat16, jnp.float32
     packed = reach + 5 * near
     shape = jax.ShapeDtypeStruct
@@ -425,13 +426,14 @@
     weight_spec = pl.BlockSpec(short_filter.shape[:2] + (columns,), lambda b, s: (0, 0, b))
     end = length // near - 1
     local_rows = shape((length, channels), bf16)
+    hbm_rows = pltpu.HBM((length, channels), bf16)
 
     key_feat, value_feat, products, to_right, to_left = pl.pallas_call(
         functools.partial(local_kernel, length),
         grid=(blocks, 2),
         in_specs=[edge_rows(end, 0), by_channel(length), by_channel(length), weight_spec],
         out_specs=[by_channel(length)] * 3 + [by_half(packed)] * 2,
-        out_shape=[local_rows] * 3 + [shape((packed, half), bf16)] * 2,
+        out_shape=[hbm_rows] * 2 + [local_rows] + [shape((packed, half), bf16)] * 2,
         compiler_params=params,
         name="local_features",
     )(query, key, value, short_filter)
@@ -458,7 +460,7 @@
         grid=(blocks, 2),
         in_specs=[by_channel(length)] * 2 + [weight_spec, by_half(parts)],
         out_specs=[by_channel(length), full(sums_shape)],
-        out_shape=[local_rows, sums_shape],
+        out_shape=[local_rows, pltpu.HBM(sums_shape.shape, f32)],
         compiler_params=params,
         name="gate_and_stream_logits",
     )(query, stream, short_filter, head_rows)

time: 89.6 us -> 88.9 us (level)
  waiting for transfers between devices: 1.75 us -> 0.51 us
    pallas_call x2, Pallas kernels: 18.3 us -> 16.9 us  [gradients(): pl.pallas_call(functools.partial(backward_kernel, length, forward), grid=...]
    all_to_all x1, waiting for transfers between devices: 1.66 us -> 0.49 us  [per_device(): class_rows = lax.all_to_all(shard, 'fsdp', 0, 0, tiled=True)]
    all_to_all x1, starting transfers between devices: 5.04 us -> 6.16 us  [per_device(): by_genome = lax.all_to_all(partial, 'fsdp', 0, 0, tiled=True)]
    all_to_all x1, starting transfers between devices: 9.12 us -> 8.05 us  [per_device(): terms = lax.all_to_all(spread, 'seq', 0, 0, tiled=True)]
    pallas_call x1, Pallas kernels: 9.41 us -> 8.42 us  [per_device(): pl.pallas_call(functools.partial(forward_kernel, length), grid=(blocks, 2...]
    unnamed x35 -> x46, local copies, waits for them, and re-layouts: 7.89 us -> 8.57 us
  transfers between devices with their start and end apart: 7 -> 7, of which waited for: 2 -> 1; matrix products, arithmetic and copies ran while one was open for 1% -> 1% of each run, Pallas kernels for 27% -> 26%
where the time goes in v4:
time: 88.9 us; the launch traced here: 88.2 us
  Pallas kernels  45.3 us (51%)
  starting transfers between devices  31.8 us (36%)
  local copies, waits for them, and re-layouts  9.2 us (10%)
    pallas_call x2, Pallas kernels, gradients(): pl.pallas_call(functools.partial(backward_kernel, length, forward), grid=...  16.9 us
    all_to_all x1, starting transfers between devices, per_device(): class_rows = lax.all_to_all(shard, 'fsdp', 0, 0, tiled=True)  8.64 us
    unnamed x46, local copies, waits for them, and re-layouts  8.57 us
    pallas_call x1, Pallas kernels, per_device(): pl.pallas_call(functools.partial(forward_kernel, length), grid=(blocks, 2...  8.42 us
    all_to_all x1, starting transfers between devices, per_device(): terms = lax.all_to_all(spread, 'seq', 0, 0, tiled=True)  8.05 us
    pallas_call x1, Pallas kernels, per_device(): pl.pallas_call(functools.partial(local_kernel, length), grid=(blocks, 2),...  7.86 us
    all_to_all x1, starting transfers between devices, per_device(): by_genome = lax.all_to_all(partial, 'fsdp', 0, 0, tiled=True)  6.16 us
    ppermute x1, starting transfers between devices, per_device(): grad_right = lax.ppermute(to_left, 'seq', leftward)  5.59 us
  transfers between devices with their start and end apart: 7, of which 1 were waited for; matrix products, arithmetic and copies ran while one was open for 1% of the time, Pallas kernels for 26%

profile of v4, /device:TPU:1, one launch (start us, length us, event | category | flops | bytes accessed | tf_op | source)
XLA Modules:
  0.0 88.2 jit_solution(1275393519321899283)
XLA Ops:
  0.6 0.0 copy-start.14
  0.7 7.9 %local_features.1 = (bf16[160,4096]{1,0:T(8,128)(2,1)}, bf16[160,4096]{1,0:T(8,128)(2,1)}, bf16[160,4096]{1,0:T(8,128)(2,1)S(1)}, bf16[168,2048]{1,0:T(8,128)(2,1)}, bf16[168,2048]{1,0:T(8,128)(2,1)}) custom-call(bf16[160,4096]{1,0:T(8,128)(2,1)} %bitcast.16, bf16[160,4096]{1,0:T(8,128)(2,1)} %bitcast.10, bf16[160,4096]{1,0:T(8,128)(2,1)} %bitcast.13, ...), custom_call_target="tpu_custom_call" | custom-call | tf_op jit(solution)/shard_map/local_features/pallas_call | solution.py:431
  8.5 2.7 %collective-permute-start = (bf16[168,2048]{1,0:T(8,128)(2,1)}, bf16[168,2048]{1,0:T(8,128)(2,1)S(1)}, u32[]{:S(2)}, u32[]{:S(2)}) collective-permute-start(bf16[168,2048]{1,0:T(8,128)(2,1)} %get-tuple-element.43), channel_id=1, source_target_pairs={{0,16},{16,32},{32,48},{48,64},{64,80},{80,96},{96,112},{112,128},... | collective-permute-start | bytes 2064392 | tf_op jit(solution)/shard_map/ppermute | solution.py:441
  11.2 0.6 collective-permute-start.1
  11.8 0.9 %shard.1 = (bf16[16,16,128]{2,1,0:T(8,128)(2,1)}, bf16[16,2048]{1,0:T(8,128)(2,1)S(1)}) custom-call(bf16[128,2048]{1,0:T(8,128)(2,1)S(1)} %copy-done.8, f32[4,2048]{1,0:T(4,128)S(1)} %copy-done.14), custom_call_target="tpu_custom_call" | custom-call | tf_op jit(solution)/shard_map/shard/pallas_call | solution.py:444
  12.7 8.6 %all-to-all-start = ((bf16[16,16,128]{2,1,0:T(8,128)(2,1)}), bf16[16,16,128]{2,1,0:T(8,128)(2,1)}, u32[]{:S(2)}, u32[]{:S(2)}) async-start(bf16[16,16,128]{2,1,0:T(8,128)(2,1)} %get-tuple-element.45), calls=%async_computation | async-start | bytes 131072 | tf_op jit(solution)/shard_map/all_to_all | solution.py:452
  21.4 0.0 copy-start.17
  21.4 0.8 copy-done.17
  22.3 5.5 %gate_and_stream_logits.1 = (bf16[160,4096]{1,0:T(8,128)(2,1)S(1)}, f32[2,160,16]{2,1,0:T(8,128)}) custom-call(bf16[160,4096]{1,0:T(8,128)(2,1)} %bitcast.17, bf16[160,4096]{1,0:T(8,128)(2,1)} %bitcast.27, f32[3,7,2048]{2,1,0:T(8,128)} %bitcast.20, bf16[16,2048]{1,0:T(8,128)(2,1)S(1)} %copy-done.17), custom_call_target="tpu_custom_call" | custom-call | tf_op jit(solution)/shard_map/gate_and_stream_logits/pallas_call | solution.py:458
  27.7 0.6 add_convert_fusion.inner
  28.3 0.5 all-to-all-done.class_rows
  28.8 0.0 copy-start.9
  28.8 0.9 copy-done.9
  29.7 0.9 %copy-done.11 = bf16[176,224]{1,0:T(8,128)(2,1)S(1)} copy-done((bf16[176,224]{1,0:T(8,128)(2,1)S(1)}, bf16[176,224]{1,0:T(8,128)(2,1)}, u32[]{:S(2)}) %copy-start.11) | copy-done | bytes 78872
  30.6 0.9 %copy-done.13 = f32[2,160,16]{2,1,0:T(8,128)S(1)} copy-done((f32[2,160,16]{2,1,0:T(8,128)S(1)}, f32[2,160,16]{2,1,0:T(8,128)}, u32[]{:S(2)}) %copy-start.13) | copy-done | bytes 20504
  31.5 0.6 copy-done.20
  32.1 0.7 copy-done.22
  32.8 8.4 %mix_and_logits.1 = (bf16[160,4096]{1,0:T(8,128)(2,1)S(1)}, bf16[160,4096]{1,0:T(8,128)(2,1)S(1)}, bf16[160,4096]{1,0:T(8,128)(2,1)S(1)}, bf16[16,4096]{1,0:T(8,...) custom-call(s32[2]{0:T(128)S(1)} %copy-done.20, bf16[160,4096]{1,0:T(8,128)(2,1)} %bitcast.18, ...), custom_call_target="tpu_custom_call" | custom-call | tf_op jit(solution)/shard_map/mix_and_logits/pallas_call | solution.py:488
  41.2 0.0 copy-start.3
  41.3 0.6 copy-done.3
  41.9 3.7 %weight_partial_and_mix_grad.1 = (f32[16,8,128]{2,1,0:T(8,128)}, bf16[160,4096]{1,0:T(8,128)(2,1)S(1)}, bf16[160,4096]{1,0:T(8,128)(2,1)S(1)}, bf16[144,2048]{1,0:T(8,128)(2,1)S(1)}, bf16[144,2048]{1,0:T(8,128)(2,1)S(1)}) custom-call(bf16[160,4096]{1,0:T(8,128)(2,1)S(1)} %get-tuple-element.47.gate, bf16[160,4096]{1,0:T(8,128)(2,1)S(1)} %get-tuple-element.48.gated, ...), custom_call_target="tpu_custom_call" | custom-call | tf_op jit(solution)/shard_map/weight_partial_and_mix_grad/pallas_call | solution.py:514
  45.7 1.1 %copy-done = bf16[160,4096]{1,0:T(8,128)(2,1)} copy-done((bf16[160,4096]{1,0:T(8,128)(2,1)}, bf16[160,4096]{1,0:T(8,128)(2,1)S(1)}, u32[]{:S(2)}) %copy-start) | copy-done | bytes 1310744
  46.7 1.1 %copy-done.1 = bf16[160,4096]{1,0:T(8,128)(2,1)} copy-done((bf16[160,4096]{1,0:T(8,128)(2,1)}, bf16[160,4096]{1,0:T(8,128)(2,1)S(1)}, u32[]{:S(2)}) %copy-start.1) | copy-done | bytes 1310744
  47.8 5.6 %collective-permute-start.2 = (bf16[144,2048]{1,0:T(8,128)(2,1)S(1)}, bf16[144,2048]{1,0:T(8,128)(2,1)S(1)}, u32[]{:S(2)}, u32[]{:S(2)}) collective-permute-start(bf16[144,2048]{1,0:T(8,128)(2,1)S(1)} %get-tuple-element.54), channel_id=1, source_target_pairs={{16,0},{32,16},{48,32},{64,48},{80,64},{96,80},{112,96},{128,112},... | collective-permute-start | bytes 1769480 | tf_op jit(solution)/shard_map/ppermute | solution.py:531
  53.4 0.0 collective-permute-start.3
  53.4 6.2 %all-to-all-start.1 = ((f32[16,8,128]{2,1,0:T(8,128)}), f32[16,8,128]{2,1,0:T(8,128)S(1)}, u32[]{:S(2)}, u32[]{:S(2)}) async-start(f32[16,8,128]{2,1,0:T(8,128)} %get-tuple-element.51), calls=%async_computation.1 | async-start | bytes 131072 | tf_op jit(solution)/shard_map/all_to_all | solution.py:535
  59.6 0.9 %copy-done.6 = bf16[16,4096]{1,0:T(8,128)(2,1)S(1)} copy-done((bf16[16,4096]{1,0:T(8,128)(2,1)S(1)}, bf16[16,4096]{1,0:T(8,128)(2,1)}, u32[]{:S(2)}) %copy-start.6) | copy-done | bytes 131096
  60.5 8.6 %gradients_forward.1 = (bf16[160,4096]{1,0:T(8,128)(2,1)}, bf16[160,4096]{1,0:T(8,128)(2,1)}, bf16[160,4096]{1,0:T(8,128)(2,1)}) custom-call(s32[2]{0:T(128)S(1)} %copy-done.21, bf16[160,4096]{1,0:T(8,128)(2,1)} %copy-done, bf16[160,4096]{1,0:T(8,128)(2,1)} %copy-done.1, bf16[144,2048]{1,0:T(8,128)(2,1)S(1)} %collective-permute-done.2.halo, ...), custom_call_target="tpu_custom_call" | custom-call | tf_op jit(solution)/shard_map/gradients_forward/pallas_call | solution.py:556
  69.2 0.6 broadcast_in_dim.12
  69.8 8.1 %all-to-all-start.2 = ((f32[16,8,128]{2,1,0:T(8,128)}), f32[16,8,128]{2,1,0:T(8,128)S(1)}, u32[]{:S(2)}, u32[]{:S(2)}) async-start(f32[16,8,128]{2,1,0:T(8,128)} %broadcast_in_dim.12), calls=%async_computation.2 | async-start | bytes 131072 | tf_op jit(solution)/shard_map/all_to_all | solution.py:579
  77.9 8.3 %gradients_reverse.1 = (bf16[160,4096]{1,0:T(8,128)(2,1)}, bf16[160,4096]{1,0:T(8,128)(2,1)}, bf16[160,4096]{1,0:T(8,128)(2,1)}) custom-call(s32[2]{0:T(128)S(1)} %copy-done.21, bf16[160,4096]{1,0:T(8,128)(2,1)} %copy-done, bf16[160,4096]{1,0:T(8,128)(2,1)} %copy-done.1, ...), custom_call_target="tpu_custom_call", output_to_operand_aliasing={{0}: (12, {}), {1}: (13, {}), {2}: (14, {})} | custom-call | tf_op jit(solution)/shard_map/gradients_reverse/pallas_call | solution.py:556
  86.2 2.0 %final.1 = f32[128,2048]{1,0:T(8,128)} custom-call(f32[16,8,128]{2,1,0:T(8,128)S(1)} %all-to-all-done.2.terms, f32[4,2048]{1,0:T(4,128)S(1)} %copy-done.15), custom_call_target="tpu_custom_call" | custom-call | tf_op jit(solution)/shard_map/final/pallas_call | solution.py:583
  (39 shorter events, 0.1 us)
Async XLA Ops:
  0.6 11.2 %copy-start.8 = (bf16[128,2048]{1,0:T(8,128)(2,1)S(1)}, bf16[128,2048]{1,0:T(8,128)(2,1)}, u32[]{:S(2)}) copy-start(bf16[128,2048]{1,0:T(8,128)(2,1)} %out_weight.1) | copy-start | bytes 1572868
  0.6 11.2 %copy-start.14 = (f32[4,2048]{1,0:T(4,128)S(1)}, f32[4,2048]{1,0:T(4,128)}, u32[]{:S(2)}) copy-start(f32[4,2048]{1,0:T(4,128)} %head.3) | copy-start | bytes 98308
  8.5 20.3 %collective-permute-start = (bf16[168,2048]{1,0:T(8,128)(2,1)}, bf16[168,2048]{1,0:T(8,128)(2,1)S(1)}, u32[]{:S(2)}, u32[]{:S(2)}) collective-permute-start(bf16[168,2048]{1,0:T(8,128)(2,1)} %get-tuple-element.43), channel_id=1, source_target_pairs={{0,16},{16,32},{32,48},{48,64},{64,80},{80,96},{96,112},{112,128},... | collective-permute-start | bytes 2064392 | tf_op jit(solution)/shard_map/ppermute | solution.py:441
  11.2 17.6 %collective-permute-start.1 = (bf16[168,2048]{1,0:T(8,128)(2,1)}, bf16[168,2048]{1,0:T(8,128)(2,1)}, u32[]{:S(2)}, u32[]{:S(2)}) collective-permute-start(bf16[168,2048]{1,0:T(8,128)(2,1)} %get-tuple-element.44), channel_id=1, source_target_pairs={{16,0},{32,16},{48,32},{64,48},{80,64},{96,80},{112,96},{128,112},... | collective-permute-start | bytes 2064392 | tf_op jit(solution)/shard_map/ppermute | solution.py:442
  12.7 8.7 %copy-start.16 = (bf16[16,2048]{1,0:T(8,128)(2,1)}, bf16[16,2048]{1,0:T(8,128)(2,1)S(1)}, u32[]{:S(2)}) copy-start(bf16[16,2048]{1,0:T(8,128)(2,1)S(1)} %get-tuple-element.41.head_rows) | copy-start | bytes 196612
  12.7 16.1 %all-to-all-start = ((bf16[16,16,128]{2,1,0:T(8,128)(2,1)}), bf16[16,16,128]{2,1,0:T(8,128)(2,1)}, u32[]{:S(2)}, u32[]{:S(2)}) async-start(bf16[16,16,128]{2,1,0:T(8,128)(2,1)} %get-tuple-element.45), calls=%async_computation | async-start | bytes 131072 | tf_op jit(solution)/shard_map/all_to_all | solution.py:452
  21.4 0.8 copy-start.17
  22.2 6.6 %copy-start.2 = (bf16[448,216]{1,0:T(8,128)(2,1)S(1)}, bf16[448,216]{1,0:T(8,128)(2,1)}, u32[]{:S(2)}) copy-start(bf16[448,216]{1,0:T(8,128)(2,1)} %constant.21.clone.analysis) | copy-start | bytes 580612
  22.2 6.6 %copy-start.18 = (f32[2,16,128]{2,1,0:T(8,128)S(1)}, f32[2,16,128]{2,1,0:T(8,128)}, u32[]{:S(2)}) copy-start(f32[2,16,128]{2,1,0:T(8,128)} %constant.25.clone.fold) | copy-start | bytes 49156
  28.8 0.9 %copy-start.9 = (bf16[176,224]{1,0:T(8,128)(2,1)S(1)}, bf16[176,224]{1,0:T(8,128)(2,1)}, u32[]{:S(2)}) copy-start(bf16[176,224]{1,0:T(8,128)(2,1)} %constant.22.clone.synth_c.synthesis) | copy-start | bytes 236548
  29.7 0.9 %copy-start.11 = (bf16[176,224]{1,0:T(8,128)(2,1)S(1)}, bf16[176,224]{1,0:T(8,128)(2,1)}, u32[]{:S(2)}) copy-start(bf16[176,224]{1,0:T(8,128)(2,1)} %constant.23.clone.synth_a.synthesis) | copy-start | bytes 236548
  30.6 0.9 %copy-start.13 = (f32[2,160,16]{2,1,0:T(8,128)S(1)}, f32[2,160,16]{2,1,0:T(8,128)}, u32[]{:S(2)}) copy-start(f32[2,160,16]{2,1,0:T(8,128)} %get-tuple-element.46.stream_sums) | copy-start | bytes 61444
  31.5 0.6 copy-start.20
  32.1 0.7 copy-start.22
  32.8 9.1 %copy-start.19 = (bf16[2,2,8,32]{3,2,1,0:T(8,128)(2,1)S(1)}, bf16[2,2,8,32]{3,2,1,0:T(8,128)(2,1)}, u32[]{:S(2)}) copy-start(bf16[2,2,8,32]{3,2,1,0:T(8,128)(2,1)} %constant.24.clone.place) | copy-start | bytes 6148
  41.2 0.7 copy-start.3
  41.9 3.7 %copy-start.5 = (bf16[16,4096]{1,0:T(8,128)(2,1)}, bf16[16,4096]{1,0:T(8,128)(2,1)S(1)}, u32[]{:S(2)}) copy-start(bf16[16,4096]{1,0:T(8,128)(2,1)S(1)} %get-tuple-element.58.value_rim) | copy-start | bytes 393220
  41.9 17.7 %copy-start.4 = (bf16[16,4096]{1,0:T(8,128)(2,1)S(1)}, bf16[16,4096]{1,0:T(8,128)(2,1)}, u32[]{:S(2)}) copy-start(bf16[16,4096]{1,0:T(8,128)(2,1)} %copy-done.3) | copy-start | bytes 393220
  41.9 17.7 %copy-start.12 = (bf16[176,224]{1,0:T(8,128)(2,1)S(1)}, bf16[176,224]{1,0:T(8,128)(2,1)}, u32[]{:S(2)}) copy-start(bf16[176,224]{1,0:T(8,128)(2,1)} %constant.23.clone.synth_a.synthesis) | copy-start | bytes 236548
  41.9 17.7 %copy-start.21 = (s32[2]{0:T(128)S(1)}, s32[2]{0:T(128)}, u32[]{:S(2)}) copy-start(s32[2]{0:T(128)} %add_convert_fusion.inner) | copy-start | bytes 28
  45.7 1.1 %copy-start = (bf16[160,4096]{1,0:T(8,128)(2,1)}, bf16[160,4096]{1,0:T(8,128)(2,1)S(1)}, u32[]{:S(2)}) copy-start(bf16[160,4096]{1,0:T(8,128)(2,1)S(1)} %get-tuple-element.64.mix_grad) | copy-start | bytes 3932164
  46.7 1.1 %copy-start.1 = (bf16[160,4096]{1,0:T(8,128)(2,1)}, bf16[160,4096]{1,0:T(8,128)(2,1)S(1)}, u32[]{:S(2)}) copy-start(bf16[160,4096]{1,0:T(8,128)(2,1)S(1)} %get-tuple-element.53.gate_grad) | copy-start | bytes 3932164
  47.8 11.8 %collective-permute-start.2 = (bf16[144,2048]{1,0:T(8,128)(2,1)S(1)}, bf16[144,2048]{1,0:T(8,128)(2,1)S(1)}, u32[]{:S(2)}, u32[]{:S(2)}) collective-permute-start(bf16[144,2048]{1,0:T(8,128)(2,1)S(1)} %get-tuple-element.54), channel_id=1, source_target_pairs={{16,0},{32,16},{48,32},{64,48},{80,64},{96,80},{112,96},{128,112},... | collective-permute-start | bytes 1769480 | tf_op jit(solution)/shard_map/ppermute | solution.py:531
  53.4 24.5 %collective-permute-start.3 = (bf16[144,2048]{1,0:T(8,128)(2,1)S(1)}, bf16[144,2048]{1,0:T(8,128)(2,1)S(1)}, u32[]{:S(2)}, u32[]{:S(2)}) collective-permute-start(bf16[144,2048]{1,0:T(8,128)(2,1)S(1)} %get-tuple-element.65), channel_id=1, source_target_pairs={{0,16},{16,32},{32,48},{48,64},{64,80},{80,96},{96,112},{112,128},... | collective-permute-start | bytes 1769480 | tf_op jit(solution)/shard_map/ppermute | solution.py:530
  53.4 15.7 %all-to-all-start.1 = ((f32[16,8,128]{2,1,0:T(8,128)}), f32[16,8,128]{2,1,0:T(8,128)S(1)}, u32[]{:S(2)}, u32[]{:S(2)}) async-start(f32[16,8,128]{2,1,0:T(8,128)} %get-tuple-element.51), calls=%async_computation.1 | async-start | bytes 131072 | tf_op jit(solution)/shard_map/all_to_all | solution.py:535
  59.6 0.9 %copy-start.6 = (bf16[16,4096]{1,0:T(8,128)(2,1)S(1)}, bf16[16,4096]{1,0:T(8,128)(2,1)}, u32[]{:S(2)}) copy-start(bf16[16,4096]{1,0:T(8,128)(2,1)} %copy-done.5) | copy-start | bytes 393220
  60.5 17.3 %copy-start.7 = (bf16[16,4096]{1,0:T(8,128)(2,1)S(1)}, bf16[16,4096]{1,0:T(8,128)(2,1)}, u32[]{:S(2)}) copy-start(bf16[16,4096]{1,0:T(8,128)(2,1)} %copy-done.5) | copy-start | bytes 393220
  60.5 17.4 %copy-start.10 = (bf16[176,224]{1,0:T(8,128)(2,1)S(1)}, bf16[176,224]{1,0:T(8,128)(2,1)}, u32[]{:S(2)}) copy-start(bf16[176,224]{1,0:T(8,128)(2,1)} %constant.22.clone.synth_c.synthesis) | copy-start | bytes 236548
  69.8 16.4 %all-to-all-start.2 = ((f32[16,8,128]{2,1,0:T(8,128)}), f32[16,8,128]{2,1,0:T(8,128)S(1)}, u32[]{:S(2)}, u32[]{:S(2)}) async-start(f32[16,8,128]{2,1,0:T(8,128)} %broadcast_in_dim.12), calls=%async_computation.2 | async-start | bytes 131072 | tf_op jit(solution)/shard_map/all_to_all | solution.py:579
  77.9 8.3 %copy-start.15 = (f32[4,2048]{1,0:T(4,128)S(1)}, f32[4,2048]{1,0:T(4,128)}, u32[]{:S(2)}) copy-start(f32[4,2048]{1,0:T(4,128)} %head.3) | copy-start | bytes 98308

commit v5 on v4

--- a/solution.py
+++ b/solution.py
@@ -469,9 +469,9 @@
     inner = jnp.stack([position > 0, position < count - 1]).astype(jnp.int32)
 
     forward, inverse = dft_tables()
-    analysis = jnp.asarray(np.concatenate(split_np(forward)))
-    synth_c = jnp.asarray(np.concatenate(split_np(inverse[lead:])))
-    synth_a = jnp.asarray(np.concatenate(split_np(inverse[:keep])))
+    analysis = in_hbm(jnp.asarray(np.concatenate(split_np(forward))))
+    synth_c = in_hbm(jnp.asarray(np.concatenate(split_np(inverse[lead:]))))
+    synth_a = in_hbm(jnp.asarray(np.concatenate(split_np(inverse[:keep]))))
 
     fold = np.zeros((2, parts, 128), np.float32)
     place = np.zeros((2, 2, 8, 2 * parts), np.float32)
@@ -482,7 +482,7 @@
             for level in range(2):
                 place[0, level, lane, level * parts + 4 * part + lane] = 1.0
                 place[1, level, 3 - lane, level * parts + 4 * part + lane] = 1.0
-    place = jnp.asarray(place.astype(ml_dtypes.bfloat16))
+    place = in_hbm(jnp.asarray(place.astype(ml_dtypes.bfloat16)))
 
     grad_shape = shape((8, length), f32)
     gate, gated, mix, key_rim, value_rim, grad = pl.pallas_call(
@@ -497,7 +497,7 @@
             full(analysis), full(synth_c), full(synth_a), full(fold),
         ],
         out_specs=[by_channel(length)] * 3 + [by_channel(2 * near)] * 2 + [full(grad_shape)],
-        out_shape=[local_rows] * 3 + [shape((2 * near, channels), bf16)] * 2 + [grad_shape],
+        out_shape=[local_rows] * 3 + [pltpu.HBM((2 * near, channels), bf16)] * 2 + [grad_shape],
         scratch_shapes=[
             pltpu.VMEM((span, columns), bf16),
             pltpu.VMEM((bins, columns), f32),
@@ -507,8 +507,8 @@
         name="mix_and_logits",
     )(
         inner, query, key, key, value, value, products, first_gate, from_left, from_right,
-        short_filter, class_rows, stream_sums, med_filter, targets, analysis, synth_c, synth_a,
-        jnp.asarray(fold),
+        short_filter, class_rows, in_hbm(stream_sums), med_filter, in_hbm(targets), analysis, synth_c, synth_a,
+        in_hbm(jnp.asarray(fold)),
     )
 
     partial, mix_grad, gate_grad, to_left, to_right = pl.pallas_call(
@@ -566,8 +566,8 @@
             ),
             name="gradients_forward" if forward else "gradients_reverse",
         )(
-            inner, in_hbm(mix_grad), in_hbm(gate_grad), halo, in_hbm(key_feat),
-            in_hbm(value_feat), key_rim, value_rim, short_filter, med_filter, analysis,
+            inner, mix_grad, gate_grad, halo, in_hbm(key_feat),
+            in_hbm(value_feat), in_hbm(key_rim), in_hbm(value_rim), short_filter, med_filter, analysis,
             synthesis, *earlier,
         )
 

time: 88.9 us -> 82.4 us (0.927)
  local copies, waits for them, and re-layouts: 9.2 us -> 0.65 us
  waiting for transfers between devices: 0.51 us -> 2.34 us
  Pallas kernels: 45.3 us -> 46.5 us
    unnamed x46 -> x4, local copies, waits for them, and re-layouts: 8.57 us -> 0.01 us
    all_to_all x1, waiting for transfers between devices: 0.49 us -> 1.81 us  [per_device(): class_rows = lax.all_to_all(shard, 'fsdp', 0, 0, tiled=True)]
    all_to_all x1, starting transfers between devices: 6.16 us -> 4.93 us  [per_device(): by_genome = lax.all_to_all(partial, 'fsdp', 0, 0, tiled=True)]
    all_to_all x1, starting transfers between devices: 8.05 us -> 9.17 us  [per_device(): terms = lax.all_to_all(spread, 'seq', 0, 0, tiled=True)]
    pallas_call x1, Pallas kernels: 8.42 us -> 9.33 us  [per_device(): pl.pallas_call(functools.partial(forward_kernel, length), grid=(blocks, 2...]
  transfers between devices with their start and end apart: 7 -> 7, of which waited for: 1 -> 2; matrix products, arithmetic and copies ran while one was open for 1% -> 1% of each run, Pallas kernels for 26% -> 28%
where the time goes in v5:
time: 82.4 us; the launch traced here: 81.9 us
  Pallas kernels  46.5 us (56%)
  starting transfers between devices  31.6 us (38%)
  waiting for transfers between devices  2.34 us (3%)
    pallas_call x2, Pallas kernels, gradients(): pl.pallas_call(functools.partial(backward_kernel, length, forward), grid=...  16.9 us
    pallas_call x1, Pallas kernels, per_device(): pl.pallas_call(functools.partial(forward_kernel, length), grid=(blocks, 2...  9.33 us
    all_to_all x1, starting transfers between devices, per_device(): terms = lax.all_to_all(spread, 'seq', 0, 0, tiled=True)  9.17 us
    all_to_all x1, starting transfers between devices, per_device(): class_rows = lax.all_to_all(shard, 'fsdp', 0, 0, tiled=True)  8.59 us
    pallas_call x1, Pallas kernels, per_device(): pl.pallas_call(functools.partial(local_kernel, length), grid=(blocks, 2),...  7.86 us
    ppermute x1, starting transfers between devices, per_device(): grad_right = lax.ppermute(to_left, 'seq', leftward)  5.6 us
    pallas_call x1, Pallas kernels, per_device(): pl.pallas_call(functools.partial(gate_kernel, length), grid=(blocks, 2),...  5.48 us
    all_to_all x1, starting transfers between devices, per_device(): by_genome = lax.all_to_all(partial, 'fsdp', 0, 0, tiled=True)  4.93 us
  transfers between devices with their start and end apart: 7, of which 2 were waited for; matrix products, arithmetic and copies ran while one was open for 1% of the time, Pallas kernels for 28%

profile of v5, /device:TPU:1, one launch (start us, length us, event | category | flops | bytes accessed | tf_op | source)
XLA Modules:
  0.0 81.9 jit_solution(18081140264386546892)
XLA Ops:
  0.6 0.0 copy-start
  0.6 0.0 copy-start.1
  0.7 7.9 %local_features.1 = (bf16[160,4096]{1,0:T(8,128)(2,1)}, bf16[160,4096]{1,0:T(8,128)(2,1)}, bf16[160,4096]{1,0:T(8,128)(2,1)S(1)}, bf16[168,2048]{1,0:T(8,128)(2,1)}, bf16[168,2048]{1,0:T(8,128)(2,1)}) custom-call(bf16[160,4096]{1,0:T(8,128)(2,1)} %bitcast.16, bf16[160,4096]{1,0:T(8,128)(2,1)} %bitcast.10, bf16[160,4096]{1,0:T(8,128)(2,1)} %bitcast.13, ...), custom_call_target="tpu_custom_call" | custom-call | tf_op jit(solution)/shard_map/local_features/pallas_call | solution.py:431
  8.5 2.7 %collective-permute-start = (bf16[168,2048]{1,0:T(8,128)(2,1)}, bf16[168,2048]{1,0:T(8,128)(2,1)S(1)}, u32[]{:S(2)}, u32[]{:S(2)}) collective-permute-start(bf16[168,2048]{1,0:T(8,128)(2,1)} %get-tuple-element.43), channel_id=1, source_target_pairs={{0,16},{16,32},{32,48},{48,64},{64,80},{80,96},{96,112},{112,128},... | collective-permute-start | bytes 2064392 | tf_op jit(solution)/shard_map/ppermute | solution.py:441
  11.2 0.6 collective-permute-start.1
  11.8 0.0 copy-done
  11.8 0.0 copy-done.1
  11.8 0.9 %shard.1 = (bf16[16,16,128]{2,1,0:T(8,128)(2,1)}, bf16[16,2048]{1,0:T(8,128)(2,1)S(1)}) custom-call(bf16[128,2048]{1,0:T(8,128)(2,1)S(1)} %copy-done, f32[4,2048]{1,0:T(4,128)S(1)} %copy-done.1), custom_call_target="tpu_custom_call" | custom-call | tf_op jit(solution)/shard_map/shard/pallas_call | solution.py:444
  12.7 8.6 %all-to-all-start = ((bf16[16,16,128]{2,1,0:T(8,128)(2,1)}), bf16[16,16,128]{2,1,0:T(8,128)(2,1)S(1)}, u32[]{:S(2)}, u32[]{:S(2)}) async-start(bf16[16,16,128]{2,1,0:T(8,128)(2,1)} %get-tuple-element.45), calls=%async_computation | async-start | bytes 131072 | tf_op jit(solution)/shard_map/all_to_all | solution.py:452
  21.3 5.5 %gate_and_stream_logits.1 = (bf16[160,4096]{1,0:T(8,128)(2,1)S(1)}, f32[2,160,16]{2,1,0:T(8,128)}) custom-call(bf16[160,4096]{1,0:T(8,128)(2,1)} %bitcast.17, bf16[160,4096]{1,0:T(8,128)(2,1)} %bitcast.27, f32[3,7,2048]{2,1,0:T(8,128)} %bitcast.20, bf16[16,2048]{1,0:T(8,128)(2,1)S(1)} %get-tuple-element.41.head_rows), custom_call_target="tpu_custom_call" | custom-call | tf_op jit(solution)/shard_map/gate_and_stream_logits/pallas_call | solution.py:458
  26.8 0.1 add_convert_fusion.inner
  26.9 1.8 %all-to-all-done.class_rows = bf16[16,16,128]{2,1,0:T(8,128)(2,1)S(1)} async-done(((bf16[16,16,128]{2,1,0:T(8,128)(2,1)}), bf16[16,16,128]{2,1,0:T(8,128)(2,1)S(1)}, u32[]{:S(2)}, u32[]{:S(2)}) %all-to-all-start) | async-done | bytes 65568 | tf_op jit(solution)/shard_map/all_to_all | solution.py:452
  28.7 0.0 collective-permute-done.left
  28.7 0.0 collective-permute-done.1.right
  28.7 9.3 %mix_and_logits.1 = (bf16[160,4096]{1,0:T(8,128)(2,1)S(1)}, bf16[160,4096]{1,0:T(8,128)(2,1)S(1)}, bf16[160,4096]{1,0:T(8,128)(2,1)S(1)}, bf16[16,4096]{1,0:T(8,...) custom-call(s32[2]{0:T(128)S(1)} %add_convert_fusion.inner, bf16[160,4096]{1,0:T(8,128)(2,1)} %bitcast.18, ...), custom_call_target="tpu_custom_call" | custom-call | tf_op jit(solution)/shard_map/mix_and_logits/pallas_call | solution.py:488
  38.0 4.0 %weight_partial_and_mix_grad.1 = (f32[16,8,128]{2,1,0:T(8,128)}, bf16[160,4096]{1,0:T(8,128)(2,1)S(1)}, bf16[160,4096]{1,0:T(8,128)(2,1)S(1)}, bf16[144,2048]{1,0:T(8,128)(2,1)}, bf16[144,2048]{1,0:T(8,128)(2,1)}) custom-call(bf16[160,4096]{1,0:T(8,128)(2,1)S(1)} %get-tuple-element.47.gate, bf16[160,4096]{1,0:T(8,128)(2,1)S(1)} %get-tuple-element.48.gated, ...), custom_call_target="tpu_custom_call" | custom-call | tf_op jit(solution)/shard_map/weight_partial_and_mix_grad/pallas_call | solution.py:514
  42.1 5.6 %collective-permute-start.2 = (bf16[144,2048]{1,0:T(8,128)(2,1)}, bf16[144,2048]{1,0:T(8,128)(2,1)}, u32[]{:S(2)}, u32[]{:S(2)}) collective-permute-start(bf16[144,2048]{1,0:T(8,128)(2,1)} %get-tuple-element.54), channel_id=1, source_target_pairs={{16,0},{32,16},{48,32},{64,48},{80,64},{96,80},{112,96},{128,112},... | collective-permute-start | bytes 1769480 | tf_op jit(solution)/shard_map/ppermute | solution.py:531
  47.7 0.0 collective-permute-start.3
  47.7 4.9 %all-to-all-start.1 = ((f32[16,8,128]{2,1,0:T(8,128)}), f32[16,8,128]{2,1,0:T(8,128)S(1)}, u32[]{:S(2)}, u32[]{:S(2)}) async-start(f32[16,8,128]{2,1,0:T(8,128)} %get-tuple-element.51), calls=%async_computation.1 | async-start | bytes 131072 | tf_op jit(solution)/shard_map/all_to_all | solution.py:535
  52.6 0.5 collective-permute-done.2.halo
  53.1 8.6 %gradients_forward.1 = (bf16[160,4096]{1,0:T(8,128)(2,1)}, bf16[160,4096]{1,0:T(8,128)(2,1)}, bf16[160,4096]{1,0:T(8,128)(2,1)}) custom-call(s32[2]{0:T(128)S(1)} %add_convert_fusion.inner, bf16[160,4096]{1,0:T(8,128)(2,1)S(1)} %get-tuple-element.64.mix_grad, bf16[160,4096]{1,0:T(8,128)(2,1)S(1)} %get-tuple-element.53.gate_grad, ...), custom_call_target="tpu_custom_call" | custom-call | tf_op jit(solution)/shard_map/gradients_forward/pallas_call | solution.py:556
  61.8 0.0 all-to-all-done.1
  61.8 0.6 broadcast_in_dim.12
  62.4 9.2 %all-to-all-start.2 = ((f32[16,8,128]{2,1,0:T(8,128)}), f32[16,8,128]{2,1,0:T(8,128)S(1)}, u32[]{:S(2)}, u32[]{:S(2)}) async-start(f32[16,8,128]{2,1,0:T(8,128)} %broadcast_in_dim.12), calls=%async_computation.2 | async-start | bytes 131072 | tf_op jit(solution)/shard_map/all_to_all | solution.py:579
  71.6 0.0 collective-permute-done.3.halo
  71.6 8.3 %gradients_reverse.1 = (bf16[160,4096]{1,0:T(8,128)(2,1)}, bf16[160,4096]{1,0:T(8,128)(2,1)}, bf16[160,4096]{1,0:T(8,128)(2,1)}) custom-call(s32[2]{0:T(128)S(1)} %add_convert_fusion.inner, bf16[160,4096]{1,0:T(8,128)(2,1)S(1)} %get-tuple-element.64.mix_grad, ...), custom_call_target="tpu_custom_call", output_to_operand_aliasing={{0}: (12, {}), {1}: (13, {}), {2}: (14, {})} | custom-call | tf_op jit(solution)/shard_map/gradients_reverse/pallas_call | solution.py:556
  79.9 0.0 all-to-all-done.2.terms
  79.9 2.0 %final.1 = f32[128,2048]{1,0:T(8,128)} custom-call(f32[16,8,128]{2,1,0:T(8,128)S(1)} %all-to-all-done.2.terms, f32[4,2048]{1,0:T(4,128)S(1)} %copy-done.1), custom_call_target="tpu_custom_call" | custom-call | tf_op jit(solution)/shard_map/final/pallas_call | solution.py:583
  (1 shorter events, 0.0 us)
Async XLA Ops:
  0.6 11.2 %copy-start = (bf16[128,2048]{1,0:T(8,128)(2,1)S(1)}, bf16[128,2048]{1,0:T(8,128)(2,1)}, u32[]{:S(2)}) copy-start(bf16[128,2048]{1,0:T(8,128)(2,1)} %out_weight.1) | copy-start | bytes 1572868
  0.6 11.2 %copy-start.1 = (f32[4,2048]{1,0:T(4,128)S(1)}, f32[4,2048]{1,0:T(4,128)}, u32[]{:S(2)}) copy-start(f32[4,2048]{1,0:T(4,128)} %head.3) | copy-start | bytes 98308
  8.5 20.2 %collective-permute-start = (bf16[168,2048]{1,0:T(8,128)(2,1)}, bf16[168,2048]{1,0:T(8,128)(2,1)S(1)}, u32[]{:S(2)}, u32[]{:S(2)}) collective-permute-start(bf16[168,2048]{1,0:T(8,128)(2,1)} %get-tuple-element.43), channel_id=1, source_target_pairs={{0,16},{16,32},{32,48},{48,64},{64,80},{80,96},{96,112},{112,128},... | collective-permute-start | bytes 2064392 | tf_op jit(solution)/shard_map/ppermute | solution.py:441
  11.2 17.5 %collective-permute-start.1 = (bf16[168,2048]{1,0:T(8,128)(2,1)}, bf16[168,2048]{1,0:T(8,128)(2,1)}, u32[]{:S(2)}, u32[]{:S(2)}) collective-permute-start(bf16[168,2048]{1,0:T(8,128)(2,1)} %get-tuple-element.44), channel_id=1, source_target_pairs={{16,0},{32,16},{48,32},{64,48},{80,64},{96,80},{112,96},{128,112},... | collective-permute-start | bytes 2064392 | tf_op jit(solution)/shard_map/ppermute | solution.py:442
  12.7 16.0 %all-to-all-start = ((bf16[16,16,128]{2,1,0:T(8,128)(2,1)}), bf16[16,16,128]{2,1,0:T(8,128)(2,1)S(1)}, u32[]{:S(2)}, u32[]{:S(2)}) async-start(bf16[16,16,128]{2,1,0:T(8,128)(2,1)} %get-tuple-element.45), calls=%async_computation | async-start | bytes 131072 | tf_op jit(solution)/shard_map/all_to_all | solution.py:452
  42.1 11.1 %collective-permute-start.2 = (bf16[144,2048]{1,0:T(8,128)(2,1)}, bf16[144,2048]{1,0:T(8,128)(2,1)}, u32[]{:S(2)}, u32[]{:S(2)}) collective-permute-start(bf16[144,2048]{1,0:T(8,128)(2,1)} %get-tuple-element.54), channel_id=1, source_target_pairs={{16,0},{32,16},{48,32},{64,48},{80,64},{96,80},{112,96},{128,112},... | collective-permute-start | bytes 1769480 | tf_op jit(solution)/shard_map/ppermute | solution.py:531
  47.7 23.9 %collective-permute-start.3 = (bf16[144,2048]{1,0:T(8,128)(2,1)}, bf16[144,2048]{1,0:T(8,128)(2,1)S(1)}, u32[]{:S(2)}, u32[]{:S(2)}) collective-permute-start(bf16[144,2048]{1,0:T(8,128)(2,1)} %get-tuple-element.65), channel_id=1, source_target_pairs={{0,16},{16,32},{32,48},{48,64},{64,80},{80,96},{96,112},{112,128},... | collective-permute-start | bytes 1769480 | tf_op jit(solution)/shard_map/ppermute | solution.py:530
  47.7 14.1 %all-to-all-start.1 = ((f32[16,8,128]{2,1,0:T(8,128)}), f32[16,8,128]{2,1,0:T(8,128)S(1)}, u32[]{:S(2)}, u32[]{:S(2)}) async-start(f32[16,8,128]{2,1,0:T(8,128)} %get-tuple-element.51), calls=%async_computation.1 | async-start | bytes 131072 | tf_op jit(solution)/shard_map/all_to_all | solution.py:535
  62.4 17.4 %all-to-all-start.2 = ((f32[16,8,128]{2,1,0:T(8,128)}), f32[16,8,128]{2,1,0:T(8,128)S(1)}, u32[]{:S(2)}, u32[]{:S(2)}) async-start(f32[16,8,128]{2,1,0:T(8,128)} %broadcast_in_dim.12), calls=%async_computation.2 | async-start | bytes 131072 | tf_op jit(solution)/shard_map/all_to_all | solution.py:579

commit v6 on v5

--- a/solution.py
+++ b/solution.py
@@ -369,15 +369,14 @@
             ).astype(jnp.bfloat16)
 
 
-def final_kernel(terms, head, out):
-    total = jnp.sum(terms[...], axis=0)
-    out[...] = lax.dot_general(
-        total[:4],
-        head[...] * (1.0 / loss_scale),
-        (((0,), (0,)), ((), ())),
-        precision=lax.Precision.HIGHEST,
-        preferred_element_type=jnp.float32,
-    )
+def final_kernel(terms, head_rows, out):
+    total = jnp.sum(terms[...], axis=0)[:4] * (1.0 / loss_scale)
+    coded = thirds(total).astype(jnp.float32)
+    heads = head_rows[...].astype(jnp.float32)
+    pairs = ((0, 0), (0, 1), (1, 0), (1, 1), (0, 2), (2, 0))
+    left = jnp.concatenate([coded[4 * a : 4 * a + 4] for a, _ in pairs], axis=0)
+    right = jnp.concatenate([heads[4 * b : 4 * b + 4] for _, b in pairs], axis=0)
+    out[...] = dot_ta(left.astype(jnp.bfloat16), right.astype(jnp.bfloat16))
 
 
 def per_device(query, key, value, stream, targets, short_filter, med_filter, out_weight, head):
@@ -582,12 +581,15 @@
     query_grad, key_grad, value_grad = grads
     out_grad = pl.pallas_call(
         final_kernel,
-        in_specs=[whole] * 2,
-        out_specs=whole,
+        grid=(blocks,),
+        in_specs=[full(terms), pl.BlockSpec((parts, columns), lambda b: (0, b))],
+        out_specs=pl.BlockSpec((own, columns), lambda b: (0, b)),
         out_shape=shape((own, half), f32),
-        compiler_params=limit,
+        compiler_params=pltpu.CompilerParams(
+            dimension_semantics=("arbitrary",), vmem_limit_bytes=vmem_limit
+        ),
         name="final",
-    )(terms, head)
+    )(terms, head_rows)
     return query_grad[None], key_grad[None], value_grad[None], out_grad
 
 

time: 82.4 us -> 81.8 us (level)
  transfers between devices with their start and end apart: 7 -> 7, of which waited for: 2 -> 2; matrix products, arithmetic and copies ran while one was open for 1% -> 1% of each run, Pallas kernels for 28% -> 29%
where the time goes in v6:
time: 81.8 us; the launch traced here: 81.3 us
  Pallas kernels  45.9 us (56%)
  starting transfers between devices  31.6 us (39%)
  waiting for transfers between devices  2.34 us (3%)
    pallas_call x2, Pallas kernels, gradients(): pl.pallas_call(functools.partial(backward_kernel, length, forward), grid=...  16.9 us
    pallas_call x1, Pallas kernels, per_device(): pl.pallas_call(functools.partial(forward_kernel, length), grid=(blocks, 2...  9.33 us
    all_to_all x1, starting transfers between devices, per_device(): terms = lax.all_to_all(spread, 'seq', 0, 0, tiled=True)  9.17 us
    all_to_all x1, starting transfers between devices, per_device(): class_rows = lax.all_to_all(shard, 'fsdp', 0, 0, tiled=True)  8.59 us
    pallas_call x1, Pallas kernels, per_device(): pl.pallas_call(functools.partial(local_kernel, length), grid=(blocks, 2),...  7.86 us
    ppermute x1, starting transfers between devices, per_device(): grad_right = lax.ppermute(to_left, 'seq', leftward)  5.6 us
    pallas_call x1, Pallas kernels, per_device(): pl.pallas_call(functools.partial(gate_kernel, length), grid=(blocks, 2),...  5.48 us
    all_to_all x1, starting transfers between devices, per_device(): by_genome = lax.all_to_all(partial, 'fsdp', 0, 0, tiled=True)  4.93 us
  transfers between devices with their start and end apart: 7, of which 2 were waited for; matrix products, arithmetic and copies ran while one was open for 1% of the time, Pallas kernels for 29%

profile of v6, /device:TPU:1, one launch (start us, length us, event | category | flops | bytes accessed | tf_op | source)
XLA Modules:
  0.0 81.3 jit_solution(330861283567036629)
XLA Ops:
  0.6 0.0 copy-start
  0.6 0.0 copy-start.1
  0.7 7.9 %local_features.1 = (bf16[160,4096]{1,0:T(8,128)(2,1)}, bf16[160,4096]{1,0:T(8,128)(2,1)}, bf16[160,4096]{1,0:T(8,128)(2,1)S(1)}, bf16[168,2048]{1,0:T(8,128)(2,1)}, bf16[168,2048]{1,0:T(8,128)(2,1)}) custom-call(bf16[160,4096]{1,0:T(8,128)(2,1)} %bitcast.16, bf16[160,4096]{1,0:T(8,128)(2,1)} %bitcast.10, bf16[160,4096]{1,0:T(8,128)(2,1)} %bitcast.13, ...), custom_call_target="tpu_custom_call" | custom-call | tf_op jit(solution)/shard_map/local_features/pallas_call | solution.py:430
  8.5 2.7 %collective-permute-start = (bf16[168,2048]{1,0:T(8,128)(2,1)}, bf16[168,2048]{1,0:T(8,128)(2,1)S(1)}, u32[]{:S(2)}, u32[]{:S(2)}) collective-permute-start(bf16[168,2048]{1,0:T(8,128)(2,1)} %get-tuple-element.43), channel_id=1, source_target_pairs={{0,16},{16,32},{32,48},{48,64},{64,80},{80,96},{96,112},{112,128},... | collective-permute-start | bytes 2064392 | tf_op jit(solution)/shard_map/ppermute | solution.py:440
  11.2 0.6 collective-permute-start.1
  11.8 0.0 copy-done
  11.8 0.0 copy-done.1
  11.8 0.9 %shard.1 = (bf16[16,16,128]{2,1,0:T(8,128)(2,1)}, bf16[16,2048]{1,0:T(8,128)(2,1)S(1)}) custom-call(bf16[128,2048]{1,0:T(8,128)(2,1)S(1)} %copy-done, f32[4,2048]{1,0:T(4,128)S(1)} %copy-done.1), custom_call_target="tpu_custom_call" | custom-call | tf_op jit(solution)/shard_map/shard/pallas_call | solution.py:443
  12.7 8.6 %all-to-all-start = ((bf16[16,16,128]{2,1,0:T(8,128)(2,1)}), bf16[16,16,128]{2,1,0:T(8,128)(2,1)S(1)}, u32[]{:S(2)}, u32[]{:S(2)}) async-start(bf16[16,16,128]{2,1,0:T(8,128)(2,1)} %get-tuple-element.45), calls=%async_computation | async-start | bytes 131072 | tf_op jit(solution)/shard_map/all_to_all | solution.py:451
  21.3 5.5 %gate_and_stream_logits.1 = (bf16[160,4096]{1,0:T(8,128)(2,1)S(1)}, f32[2,160,16]{2,1,0:T(8,128)}) custom-call(bf16[160,4096]{1,0:T(8,128)(2,1)} %bitcast.17, bf16[160,4096]{1,0:T(8,128)(2,1)} %bitcast.27, f32[3,7,2048]{2,1,0:T(8,128)} %bitcast.20, bf16[16,2048]{1,0:T(8,128)(2,1)S(1)} %get-tuple-element.41.head_rows), custom_call_target="tpu_custom_call" | custom-call | tf_op jit(solution)/shard_map/gate_and_stream_logits/pallas_call | solution.py:457
  26.8 0.1 add_convert_fusion.inner
  26.9 1.8 %all-to-all-done.class_rows = bf16[16,16,128]{2,1,0:T(8,128)(2,1)S(1)} async-done(((bf16[16,16,128]{2,1,0:T(8,128)(2,1)}), bf16[16,16,128]{2,1,0:T(8,128)(2,1)S(1)}, u32[]{:S(2)}, u32[]{:S(2)}) %all-to-all-start) | async-done | bytes 65568 | tf_op jit(solution)/shard_map/all_to_all | solution.py:451
  28.7 0.0 collective-permute-done.left
  28.7 0.0 collective-permute-done.1.right
  28.7 9.3 %mix_and_logits.1 = (bf16[160,4096]{1,0:T(8,128)(2,1)S(1)}, bf16[160,4096]{1,0:T(8,128)(2,1)S(1)}, bf16[160,4096]{1,0:T(8,128)(2,1)S(1)}, bf16[16,4096]{1,0:T(8,...) custom-call(s32[2]{0:T(128)S(1)} %add_convert_fusion.inner, bf16[160,4096]{1,0:T(8,128)(2,1)} %bitcast.18, ...), custom_call_target="tpu_custom_call" | custom-call | tf_op jit(solution)/shard_map/mix_and_logits/pallas_call | solution.py:487
  38.0 4.0 %weight_partial_and_mix_grad.1 = (f32[16,8,128]{2,1,0:T(8,128)}, bf16[160,4096]{1,0:T(8,128)(2,1)S(1)}, bf16[160,4096]{1,0:T(8,128)(2,1)S(1)}, bf16[144,2048]{1,0:T(8,128)(2,1)}, bf16[144,2048]{1,0:T(8,128)(2,1)}) custom-call(bf16[160,4096]{1,0:T(8,128)(2,1)S(1)} %get-tuple-element.47.gate, bf16[160,4096]{1,0:T(8,128)(2,1)S(1)} %get-tuple-element.48.gated, ...), custom_call_target="tpu_custom_call" | custom-call | tf_op jit(solution)/shard_map/weight_partial_and_mix_grad/pallas_call | solution.py:513
  42.1 5.6 %collective-permute-start.2 = (bf16[144,2048]{1,0:T(8,128)(2,1)}, bf16[144,2048]{1,0:T(8,128)(2,1)}, u32[]{:S(2)}, u32[]{:S(2)}) collective-permute-start(bf16[144,2048]{1,0:T(8,128)(2,1)} %get-tuple-element.54), channel_id=1, source_target_pairs={{16,0},{32,16},{48,32},{64,48},{80,64},{96,80},{112,96},{128,112},... | collective-permute-start | bytes 1769480 | tf_op jit(solution)/shard_map/ppermute | solution.py:530
  47.7 0.0 collective-permute-start.3
  47.7 4.9 %all-to-all-start.1 = ((f32[16,8,128]{2,1,0:T(8,128)}), f32[16,8,128]{2,1,0:T(8,128)S(1)}, u32[]{:S(2)}, u32[]{:S(2)}) async-start(f32[16,8,128]{2,1,0:T(8,128)} %get-tuple-element.51), calls=%async_computation.1 | async-start | bytes 131072 | tf_op jit(solution)/shard_map/all_to_all | solution.py:534
  52.6 0.5 collective-permute-done.2.halo
  53.1 8.6 %gradients_forward.1 = (bf16[160,4096]{1,0:T(8,128)(2,1)}, bf16[160,4096]{1,0:T(8,128)(2,1)}, bf16[160,4096]{1,0:T(8,128)(2,1)}) custom-call(s32[2]{0:T(128)S(1)} %add_convert_fusion.inner, bf16[160,4096]{1,0:T(8,128)(2,1)S(1)} %get-tuple-element.64.mix_grad, bf16[160,4096]{1,0:T(8,128)(2,1)S(1)} %get-tuple-element.53.gate_grad, ...), custom_call_target="tpu_custom_call" | custom-call | tf_op jit(solution)/shard_map/gradients_forward/pallas_call | solution.py:555
  61.8 0.0 all-to-all-done.1
  61.8 0.6 broadcast_in_dim.12
  62.4 9.2 %all-to-all-start.2 = ((f32[16,8,128]{2,1,0:T(8,128)}), f32[16,8,128]{2,1,0:T(8,128)S(1)}, u32[]{:S(2)}, u32[]{:S(2)}) async-start(f32[16,8,128]{2,1,0:T(8,128)} %broadcast_in_dim.12), calls=%async_computation.2 | async-start | bytes 131072 | tf_op jit(solution)/shard_map/all_to_all | solution.py:578
  71.6 0.0 collective-permute-done.3.halo
  71.6 8.3 %gradients_reverse.1 = (bf16[160,4096]{1,0:T(8,128)(2,1)}, bf16[160,4096]{1,0:T(8,128)(2,1)}, bf16[160,4096]{1,0:T(8,128)(2,1)}) custom-call(s32[2]{0:T(128)S(1)} %add_convert_fusion.inner, bf16[160,4096]{1,0:T(8,128)(2,1)S(1)} %get-tuple-element.64.mix_grad, ...), custom_call_target="tpu_custom_call", output_to_operand_aliasing={{0}: (12, {}), {1}: (13, {}), {2}: (14, {})} | custom-call | tf_op jit(solution)/shard_map/gradients_reverse/pallas_call | solution.py:555
  79.9 0.0 all-to-all-done.2.terms
  79.9 1.4 %final.1 = f32[128,2048]{1,0:T(8,128)} custom-call(f32[16,8,128]{2,1,0:T(8,128)S(1)} %all-to-all-done.2.terms, bf16[16,2048]{1,0:T(8,128)(2,1)S(1)} %get-tuple-element.41.head_rows), custom_call_target="tpu_custom_call" | custom-call | tf_op jit(solution)/shard_map/final/pallas_call | solution.py:582
  (1 shorter events, 0.0 us)
Async XLA Ops:
  0.6 11.2 %copy-start = (bf16[128,2048]{1,0:T(8,128)(2,1)S(1)}, bf16[128,2048]{1,0:T(8,128)(2,1)}, u32[]{:S(2)}) copy-start(bf16[128,2048]{1,0:T(8,128)(2,1)} %out_weight.1) | copy-start | bytes 1572868
  0.6 11.2 %copy-start.1 = (f32[4,2048]{1,0:T(4,128)S(1)}, f32[4,2048]{1,0:T(4,128)}, u32[]{:S(2)}) copy-start(f32[4,2048]{1,0:T(4,128)} %head.1) | copy-start | bytes 98308
  8.5 20.2 %collective-permute-start = (bf16[168,2048]{1,0:T(8,128)(2,1)}, bf16[168,2048]{1,0:T(8,128)(2,1)S(1)}, u32[]{:S(2)}, u32[]{:S(2)}) collective-permute-start(bf16[168,2048]{1,0:T(8,128)(2,1)} %get-tuple-element.43), channel_id=1, source_target_pairs={{0,16},{16,32},{32,48},{48,64},{64,80},{80,96},{96,112},{112,128},... | collective-permute-start | bytes 2064392 | tf_op jit(solution)/shard_map/ppermute | solution.py:440
  11.2 17.5 %collective-permute-start.1 = (bf16[168,2048]{1,0:T(8,128)(2,1)}, bf16[168,2048]{1,0:T(8,128)(2,1)}, u32[]{:S(2)}, u32[]{:S(2)}) collective-permute-start(bf16[168,2048]{1,0:T(8,128)(2,1)} %get-tuple-element.44), channel_id=1, source_target_pairs={{16,0},{32,16},{48,32},{64,48},{80,64},{96,80},{112,96},{128,112},... | collective-permute-start | bytes 2064392 | tf_op jit(solution)/shard_map/ppermute | solution.py:441
  12.7 16.0 %all-to-all-start = ((bf16[16,16,128]{2,1,0:T(8,128)(2,1)}), bf16[16,16,128]{2,1,0:T(8,128)(2,1)S(1)}, u32[]{:S(2)}, u32[]{:S(2)}) async-start(bf16[16,16,128]{2,1,0:T(8,128)(2,1)} %get-tuple-element.45), calls=%async_computation | async-start | bytes 131072 | tf_op jit(solution)/shard_map/all_to_all | solution.py:451
  42.1 11.1 %collective-permute-start.2 = (bf16[144,2048]{1,0:T(8,128)(2,1)}, bf16[144,2048]{1,0:T(8,128)(2,1)}, u32[]{:S(2)}, u32[]{:S(2)}) collective-permute-start(bf16[144,2048]{1,0:T(8,128)(2,1)} %get-tuple-element.54), channel_id=1, source_target_pairs={{16,0},{32,16},{48,32},{64,48},{80,64},{96,80},{112,96},{128,112},... | collective-permute-start | bytes 1769480 | tf_op jit(solution)/shard_map/ppermute | solution.py:530
  47.7 23.9 %collective-permute-start.3 = (bf16[144,2048]{1,0:T(8,128)(2,1)}, bf16[144,2048]{1,0:T(8,128)(2,1)S(1)}, u32[]{:S(2)}, u32[]{:S(2)}) collective-permute-start(bf16[144,2048]{1,0:T(8,128)(2,1)} %get-tuple-element.65), channel_id=1, source_target_pairs={{0,16},{16,32},{32,48},{48,64},{64,80},{80,96},{96,112},{112,128},... | collective-permute-start | bytes 1769480 | tf_op jit(solution)/shard_map/ppermute | solution.py:529
  47.7 14.1 %all-to-all-start.1 = ((f32[16,8,128]{2,1,0:T(8,128)}), f32[16,8,128]{2,1,0:T(8,128)S(1)}, u32[]{:S(2)}, u32[]{:S(2)}) async-start(f32[16,8,128]{2,1,0:T(8,128)} %get-tuple-element.51), calls=%async_computation.1 | async-start | bytes 131072 | tf_op jit(solution)/shard_map/all_to_all | solution.py:534
  62.4 17.4 %all-to-all-start.2 = ((f32[16,8,128]{2,1,0:T(8,128)}), f32[16,8,128]{2,1,0:T(8,128)S(1)}, u32[]{:S(2)}, u32[]{:S(2)}) async-start(f32[16,8,128]{2,1,0:T(8,128)} %broadcast_in_dim.12), calls=%async_computation.2 | async-start | bytes 131072 | tf_op jit(solution)/shard_map/all_to_all | solution.py:578
